TPU v7x, 32 devices: a whole 2x2x4 slice. The times are simulated.
32 devices in a mesh: dp: 4 (over z), expert: 2 (over x), wshard: 4 (over y, core).
Axes of the slice: x: 2, y: 2, z: 4, core: 2. Of those that a mesh axis runs over, the one named last changes fastest.
Arguments:
- tokens: bfloat16 [8, 512, 768], P(('dp', 'expert'), 'wshard'), may hold values from -6 to 6
- lengths: int32 [8], P(('dp', 'expert')), may hold values from 256 to 512, as said below
- routes: int32 [8, 512, 2], P(('dp', 'expert'), 'wshard'), may hold values from 0 to 3, all different within a row
- drop_order: int32 [8, 512], P(('dp', 'expert'), 'wshard'), may hold values from 0 to 511, each once within a row
- cotangent: bfloat16 [8, 512, 768], P(('dp', 'expert'), 'wshard'), may hold values from -6 to 6
- qkv_weight: bfloat16 [2, 3, 768, 768], P(None, None, 'wshard'), may hold values from -0.21875 to 0.21875
- out_weight: bfloat16 [2, 768, 768], P(None, 'wshard'), may hold values from -0.875 to 0.875
- shared_up: bfloat16 [2, 2, 768, 2048], P(None, None, 'wshard'), may hold values from -0.21875 to 0.21875
- shared_down: bfloat16 [2, 2048, 768], P(None, 'wshard'), may hold values from -0.25 to 0.25
- router_weight: bfloat16 [2, 768, 4], P(None, 'wshard'), may hold values from -0.15625 to 0.15625
- norm_gains: bfloat16 [2, 2, 768], P(None, None, 'wshard'), may hold values from 0.5 to 1.5
- expert_up: bfloat16 [2, 4, 2, 768, 2048], P(None, 'expert', None, None, 'wshard'), may hold values from -0.21875 to 0.21875
- expert_down: bfloat16 [2, 4, 2048, 768], P(None, 'expert', 'wshard'), may hold values from -0.25 to 0.25
Outputs:
- block_out: bfloat16 [8, 512, 768], P(('dp', 'expert'), 'wshard')
- tokens_grad: bfloat16 [8, 512, 768], P(('dp', 'expert'), 'wshard')
- qkv_grad: float32 [2, 3, 768, 768], P(None, None, 'wshard', ('dp', 'expert'))
- out_grad: float32 [2, 768, 768], P(None, 'wshard', ('dp', 'expert'))
- shared_up_grad: float32 [2, 2, 768, 2048], P(None, None, 'wshard', ('dp', 'expert'))
- shared_down_grad: float32 [2, 2048, 768], P(None, 'wshard', ('dp', 'expert'))
- router_grad: float32 [2, 768, 4], P(None, 'wshard')
- gains_grad: float32 [2, 2, 768], P(None, None, 'wshard')
- expert_up_grad: float32 [2, 4, 2, 768, 2048], P(None, 'expert', None, 'dp', 'wshard')
- expert_down_grad: float32 [2, 4, 2048, 768], P(None, 'expert', 'wshard', 'dp')
Inputs may be any that keep to these rules, and one draw needn't show every extreme that they name: lengths[s] counts the real tokens at the start of slot s; some slot is full. `routes`: each token names two different experts. `drop_order`: in every slot each rank occurs once.
All inputs are finite; a program needn't handle non-finite values.
Results may differ from a plain program's by a relative error of at most 0.029.
Values may be sent and summed in bfloat16 or wider, within the bound.
A program may use at most 448 MiB of HBM per device.

v0:
```python
import jax
import jax.numpy as jnp
from jax import lax
from jax.sharding import PartitionSpec as P

HEADS = 12
HEAD_DIM = 64
LAYERS = 2


epsilon = 1e-06
rotary_base = 10000.0
floor_score = -1e30


def rotary_tables(positions, head_size):
    half = head_size // 2
    angles = (
        positions.astype(jnp.float32)[:, None]
        * (rotary_base ** (-jnp.arange(half, dtype=jnp.float32) / half))[None, :]
    )
    return (jnp.cos(angles)[:, None, :], jnp.sin(angles)[:, None, :])


def rotary_apply(values, cosine, sine):
    half = values.shape[-1] // 2
    first = values[..., :half]
    second = values[..., half:]
    return jnp.concatenate(
        [first * cosine - second * sine, second * cosine + first * sine], axis=-1
    )


def rotary_back(grads, cosine, sine):
    half = grads.shape[-1] // 2
    first = grads[..., :half]
    second = grads[..., half:]
    return jnp.concatenate(
        [first * cosine + second * sine, second * cosine - first * sine], axis=-1
    )


def norm_parts(values):
    inverse = lax.rsqrt(jnp.mean(values * values, axis=-1, keepdims=True) + epsilon)
    return (values * inverse, inverse)


def norm_back(grads, normed, inverse):
    return inverse * (grads - normed * jnp.mean(grads * normed, axis=-1, keepdims=True))


def pick_rows(table_rows, index, present):
    safe = jnp.where(present, index, 0)
    return jnp.where(present[:, None], table_rows[safe], 0)


def slot_table(route, order, valid, sequence_len, capacity, experts):
    count = route.shape[0]
    flat_expert = route.reshape(-1)
    priority = (jnp.arange(2, dtype=jnp.int32)[None, :] * sequence_len + order[:, None]).reshape(-1)
    live = jnp.repeat(valid, 2)
    earlier = (
        (priority[None, :] < priority[:, None])
        & (flat_expert[None, :] == flat_expert[:, None])
        & live[None, :]
    )
    place = jnp.sum(earlier.astype(jnp.int32), axis=1)
    kept = live & (place < capacity)
    target = jnp.where(kept, flat_expert * capacity + place, experts * capacity)
    filler = jnp.full((experts * capacity + 1,), 2 * count, jnp.int32)
    slot_pair = filler.at[target].set(jnp.arange(2 * count, dtype=jnp.int32))[: experts * capacity]
    return (target.reshape(count, 2), kept.reshape(count, 2), slot_pair)


def score_block(queries, keys_heads, visible, scale):
    raw = (
        jnp.einsum("qhd,khd->hqk", queries, keys_heads, preferred_element_type=jnp.float32) * scale
    )
    return jnp.where(visible[None], raw, floor_score)


def dispatch(rows, owners, shards, per_owner, capacity, width):
    blocks = rows.reshape(owners, per_owner, capacity, width)
    copies = jnp.broadcast_to(
        blocks[:, None], (owners, shards, per_owner, capacity, width)
    ).reshape(owners * shards, per_owner, capacity, width)
    arrived = lax.all_to_all(copies, ("expert", "wshard"), split_axis=0, concat_axis=2, tiled=True)
    return arrived[0]


def collect(partial_value, owners, shards, per_owner, capacity, width):
    terms = partial_value[None]
    back = lax.all_to_all(
        terms.astype(jnp.bfloat16), ("expert", "wshard"), split_axis=2, concat_axis=0, tiled=True
    ).astype(terms.dtype)
    result = jnp.sum(back.reshape(owners, shards, per_owner, capacity, width), axis=1).astype(
        jnp.bfloat16
    )
    return result.reshape(owners * per_owner * capacity, width)


def silu_grads(act_grad, gate_value, up_value):
    sigmoid_gate = jax.nn.sigmoid(gate_value)
    gate_grad = act_grad * up_value * sigmoid_gate * (1.0 + gate_value * (1.0 - sigmoid_gate))
    up_grad = act_grad * gate_value * sigmoid_gate
    return (gate_grad, up_grad)


def per_device(
    tokens,
    lengths,
    routes,
    drop_order,
    cotangent,
    qkv_weight,
    out_weight,
    shared_up,
    shared_down,
    router_weight,
    norm_gains,
    expert_up,
    expert_down,
):
    local_rows = tokens.shape[1]
    width = tokens.shape[2]
    shards = lax.axis_size("wshard")
    shard = lax.axis_index("wshard")
    owners = lax.axis_size("expert")
    sequence_len = local_rows * shards
    experts = router_weight.shape[2]
    per_owner = expert_up.shape[1]
    capacity = (10 * local_rows + 4 * experts - 1) // (4 * experts)
    scale = HEAD_DIM ** (-0.5)
    positions = shard * local_rows + jnp.arange(local_rows, dtype=jnp.int32)
    key_positions = jnp.arange(sequence_len, dtype=jnp.int32)
    valid = positions < lengths[0]
    visible = (key_positions[None, :] <= positions[:, None]) & (key_positions[None, :] < lengths[0])
    cosine, sine = rotary_tables(positions, HEAD_DIM)
    route = routes[0]
    target, kept, slot_pair = slot_table(
        route, drop_order[0], valid, sequence_len, capacity, experts
    )
    slot_present = slot_pair < 2 * local_rows
    slot_token = slot_pair // 2
    pair_flat = target.reshape(-1)
    pair_kept = kept.reshape(-1)
    route_hot = (route[:, :, None] == jnp.arange(experts, dtype=jnp.int32)[None, None, :]).astype(
        jnp.float32
    )
    project_full, out_full, up_full, down_full, router_full, gains_full = (
        lax.all_gather(qkv_weight, "wshard", axis=2, tiled=True),
        lax.all_gather(out_weight, "wshard", axis=1, tiled=True),
        lax.all_gather(shared_up, "wshard", axis=2, tiled=True),
        lax.all_gather(shared_down, "wshard", axis=1, tiled=True),
        lax.all_gather(router_weight, "wshard", axis=1, tiled=True),
        lax.all_gather(norm_gains, "wshard", axis=2, tiled=True),
    )
    stream = tokens[0].astype(jnp.float32)
    saved = []
    for layer in range(LAYERS):
        gains = gains_full[layer].astype(jnp.float32)
        normed_a, inverse_a = norm_parts(stream)
        hidden = (normed_a * gains[0]).astype(jnp.bfloat16)
        projected = jnp.einsum(
            "td,sde->ste", hidden, project_full[layer], preferred_element_type=jnp.float32
        )
        heads = projected.reshape(3, local_rows, HEADS, HEAD_DIM)
        queries = rotary_apply(heads[0], cosine, sine).astype(jnp.bfloat16)
        keys_local = (
            rotary_apply(heads[1], cosine, sine).astype(jnp.bfloat16).reshape(local_rows, width)
        )
        values_local = projected[2].astype(jnp.bfloat16)
        keys_all, values_all = (
            lax.all_gather(keys_local, "wshard", axis=0, tiled=True),
            lax.all_gather(values_local, "wshard", axis=0, tiled=True),
        )
        keys_heads = keys_all.reshape(sequence_len, HEADS, HEAD_DIM)
        values_heads = values_all.reshape(sequence_len, HEADS, HEAD_DIM)
        masked = score_block(queries, keys_heads, visible, scale)
        top = jnp.max(masked, axis=-1, keepdims=True)
        log_total = top + jnp.log(jnp.sum(jnp.exp(masked - top), axis=-1, keepdims=True))
        probs = jnp.exp(masked - log_total)
        attended = jnp.einsum(
            "hqk,khd->qhd",
            probs.astype(jnp.bfloat16),
            values_heads,
            preferred_element_type=jnp.float32,
        )
        attended = attended.reshape(local_rows, width).astype(jnp.bfloat16)
        middle = stream + jnp.dot(attended, out_full[layer], preferred_element_type=jnp.float32)
        normed_b, inverse_b = norm_parts(middle)
        mixed_in = (normed_b * gains[1]).astype(jnp.bfloat16)
        logits = jnp.dot(mixed_in, router_full[layer], preferred_element_type=jnp.float32)
        gates = jax.nn.softmax(jnp.take_along_axis(logits, route, axis=1), axis=-1)
        shared_inner = jnp.einsum(
            "td,sdf->stf", mixed_in, up_full[layer], preferred_element_type=jnp.float32
        )
        shared_act = (jax.nn.silu(shared_inner[0]) * shared_inner[1]).astype(jnp.bfloat16)
        shared_out = jnp.dot(shared_act, down_full[layer], preferred_element_type=jnp.float32)
        arrived = dispatch(
            pick_rows(mixed_in, slot_token, slot_present),
            owners,
            shards,
            per_owner,
            capacity,
            width,
        )
        expert_inner = jnp.einsum(
            "jrd,jsdf->jsrf", arrived, expert_up[layer], preferred_element_type=jnp.float32
        )
        expert_act = (jax.nn.silu(expert_inner[:, 0]) * expert_inner[:, 1]).astype(jnp.bfloat16)
        partial_value = jnp.einsum(
            "jrf,jfd->jrd", expert_act, expert_down[layer], preferred_element_type=jnp.float32
        )
        returned = collect(partial_value, owners, shards, per_owner, capacity, width)
        pair_rows = pick_rows(returned, pair_flat, pair_kept).reshape(local_rows, 2, width)
        mixture = jnp.sum(gates[:, :, None] * pair_rows.astype(jnp.float32), axis=1)
        stream = middle + shared_out + mixture
        saved.append(
            {
                "normed_a": normed_a,
                "inverse_a": inverse_a,
                "hidden": hidden,
                "queries": queries,
                "keys_heads": keys_heads,
                "values_heads": values_heads,
                "log_total": log_total,
                "attended": attended,
                "normed_b": normed_b,
                "inverse_b": inverse_b,
                "mixed_in": mixed_in,
                "gates": gates,
                "shared_inner": shared_inner,
                "shared_act": shared_act,
                "arrived": arrived,
                "expert_inner": expert_inner,
                "expert_act": expert_act,
                "pair_rows": pair_rows,
            }
        )
    block_out = stream.astype(jnp.bfloat16)[None]
    grad = cotangent[0].astype(jnp.float32) * valid[:, None].astype(jnp.float32)
    dense_parts = []
    expert_parts = []
    for layer in reversed(range(LAYERS)):
        kept_state = saved[layer]
        gains = gains_full[layer].astype(jnp.float32)
        gates = kept_state["gates"]
        mixed_in = kept_state["mixed_in"]
        gate_grad = jnp.sum(grad[:, None, :] * kept_state["pair_rows"].astype(jnp.float32), axis=-1)
        chosen_grad = gates * (gate_grad - jnp.sum(gates * gate_grad, axis=1, keepdims=True))
        logit_grad = jnp.sum(route_hot * chosen_grad[:, :, None], axis=1)
        gate_flat = gates.reshape(-1)
        slot_gate = jnp.where(slot_present, gate_flat[jnp.where(slot_present, slot_pair, 0)], 0.0)
        send_grad = (slot_gate[:, None] * pick_rows(grad, slot_token, slot_present)).astype(
            jnp.bfloat16
        )
        arrived_grad = dispatch(send_grad, owners, shards, per_owner, capacity, width)
        inner = kept_state["expert_inner"]
        act_grad = jnp.einsum(
            "jrd,jfd->jrf", arrived_grad, expert_down[layer], preferred_element_type=jnp.float32
        )
        down_grad = jnp.einsum(
            "jrf,jrd->jfd",
            kept_state["expert_act"],
            arrived_grad,
            preferred_element_type=jnp.float32,
        )
        gate_part, up_part = silu_grads(act_grad, inner[:, 0], inner[:, 1])
        inner_grad = jnp.stack([gate_part, up_part], axis=1).astype(jnp.bfloat16)
        up_grad = jnp.einsum(
            "jrd,jsrf->jsdf", kept_state["arrived"], inner_grad, preferred_element_type=jnp.float32
        )
        input_part = jnp.einsum(
            "jsrf,jsdf->jrd", inner_grad, expert_up[layer], preferred_element_type=jnp.float32
        )
        input_rows = collect(input_part, owners, shards, per_owner, capacity, width)
        mixed_grad = jnp.sum(
            pick_rows(input_rows, pair_flat, pair_kept)
            .reshape(local_rows, 2, width)
            .astype(jnp.float32),
            axis=1,
        )
        router_float = router_full[layer].astype(jnp.float32)
        mixed_grad = mixed_grad + jnp.dot(
            logit_grad, router_float.T, precision=lax.Precision.HIGHEST
        )
        router_grad = jnp.dot(
            mixed_in.astype(jnp.float32).T, logit_grad, precision=lax.Precision.HIGHEST
        )
        branch_out = grad.astype(jnp.bfloat16)
        shared_act_grad = jnp.dot(
            branch_out, down_full[layer].T, preferred_element_type=jnp.float32
        )
        shared_down_grad = jnp.dot(
            kept_state["shared_act"].T, branch_out, preferred_element_type=jnp.float32
        )
        shared_gate_part, shared_up_part = silu_grads(
            shared_act_grad, kept_state["shared_inner"][0], kept_state["shared_inner"][1]
        )
        shared_inner_grad = jnp.stack([shared_gate_part, shared_up_part], axis=0).astype(
            jnp.bfloat16
        )
        shared_up_grad = jnp.einsum(
            "td,stf->sdf", mixed_in, shared_inner_grad, preferred_element_type=jnp.float32
        )
        mixed_grad = mixed_grad + jnp.einsum(
            "stf,sdf->td", shared_inner_grad, up_full[layer], preferred_element_type=jnp.float32
        )
        gain_b_grad = jnp.sum(mixed_grad * kept_state["normed_b"], axis=0)
        middle_grad = grad + norm_back(
            mixed_grad * gains[1], kept_state["normed_b"], kept_state["inverse_b"]
        )
        branch_grad = middle_grad.astype(jnp.bfloat16)
        out_w_grad = jnp.dot(
            kept_state["attended"].T, branch_grad, preferred_element_type=jnp.float32
        )
        attended_grad = jnp.dot(
            branch_grad, out_full[layer].T, preferred_element_type=jnp.float32
        ).astype(jnp.bfloat16)
        attended_grad = attended_grad.reshape(local_rows, HEADS, HEAD_DIM)
        queries = kept_state["queries"]
        keys_heads = kept_state["keys_heads"]
        values_heads = kept_state["values_heads"]
        probs = jnp.exp(score_block(queries, keys_heads, visible, scale) - kept_state["log_total"])
        prob_grad = jnp.einsum(
            "qhd,khd->hqk", attended_grad, values_heads, preferred_element_type=jnp.float32
        )
        score_grad = (
            probs * (prob_grad - jnp.sum(probs * prob_grad, axis=-1, keepdims=True))
        ).astype(jnp.bfloat16)
        query_grad = (
            jnp.einsum("hqk,khd->qhd", score_grad, keys_heads, preferred_element_type=jnp.float32)
            * scale
        )
        key_part = (
            jnp.einsum("hqk,qhd->khd", score_grad, queries, preferred_element_type=jnp.float32)
            * scale
        ).reshape(sequence_len, width)
        value_part = jnp.einsum(
            "hqk,qhd->khd",
            probs.astype(jnp.bfloat16),
            attended_grad,
            preferred_element_type=jnp.float32,
        ).reshape(sequence_len, width)
        key_grad, value_grad = (
            lax.psum_scatter(
                key_part.astype(jnp.bfloat16), "wshard", scatter_dimension=0, tiled=True
            ).astype(jnp.float32),
            lax.psum_scatter(
                value_part.astype(jnp.bfloat16), "wshard", scatter_dimension=0, tiled=True
            ).astype(jnp.float32),
        )
        query_back = rotary_back(query_grad, cosine, sine).reshape(local_rows, width)
        key_back = rotary_back(key_grad.reshape(local_rows, HEADS, HEAD_DIM), cosine, sine).reshape(
            local_rows, width
        )
        project_grad = jnp.stack([query_back, key_back, value_grad], axis=0).astype(jnp.bfloat16)
        qkv_grad = jnp.einsum(
            "td,ste->sde", kept_state["hidden"], project_grad, preferred_element_type=jnp.float32
        )
        hidden_grad = jnp.einsum(
            "ste,sde->td", project_grad, project_full[layer], preferred_element_type=jnp.float32
        )
        gain_a_grad = jnp.sum(hidden_grad * kept_state["normed_a"], axis=0)
        grad = middle_grad + norm_back(
            hidden_grad * gains[0], kept_state["normed_a"], kept_state["inverse_a"]
        )
        dense_parts.append(
            (
                qkv_grad,
                out_w_grad,
                shared_up_grad,
                shared_down_grad,
                router_grad,
                jnp.stack([gain_a_grad, gain_b_grad], axis=0),
            )
        )
        expert_parts.append((up_grad, down_grad))
    dense_parts = dense_parts[::-1]
    expert_parts = expert_parts[::-1]
    stacked = tuple(
        (jnp.stack([part[index] for part in dense_parts], axis=0) for index in range(6))
    )
    shard_grads = (
        lax.psum_scatter(
            stacked[0].astype(jnp.bfloat16), "wshard", scatter_dimension=2, tiled=True
        ).astype(jnp.float32),
        lax.psum_scatter(
            stacked[1].astype(jnp.bfloat16), "wshard", scatter_dimension=1, tiled=True
        ).astype(jnp.float32),
        lax.psum_scatter(
            stacked[2].astype(jnp.bfloat16), "wshard", scatter_dimension=2, tiled=True
        ).astype(jnp.float32),
        lax.psum_scatter(
            stacked[3].astype(jnp.bfloat16), "wshard", scatter_dimension=1, tiled=True
        ).astype(jnp.float32),
        lax.psum_scatter(
            stacked[4].astype(jnp.bfloat16), "wshard", scatter_dimension=1, tiled=True
        ).astype(jnp.float32),
        lax.psum_scatter(
            stacked[5].astype(jnp.bfloat16), "wshard", scatter_dimension=2, tiled=True
        ).astype(jnp.float32),
    )
    large_grads = (
        lax.psum_scatter(
            shard_grads[0].astype(jnp.bfloat16), ("dp", "expert"), scatter_dimension=3, tiled=True
        ).astype(jnp.float32),
        lax.psum_scatter(
            shard_grads[1].astype(jnp.bfloat16), ("dp", "expert"), scatter_dimension=2, tiled=True
        ).astype(jnp.float32),
        lax.psum_scatter(
            shard_grads[2].astype(jnp.bfloat16), ("dp", "expert"), scatter_dimension=3, tiled=True
        ).astype(jnp.float32),
        lax.psum_scatter(
            shard_grads[3].astype(jnp.bfloat16), ("dp", "expert"), scatter_dimension=2, tiled=True
        ).astype(jnp.float32),
    )
    small_grads = lax.psum((shard_grads[4], shard_grads[5]), ("dp", "expert"))
    expert_stacked = (
        jnp.stack([part[0] for part in expert_parts], axis=0),
        jnp.stack([part[1] for part in expert_parts], axis=0),
    )
    expert_total = (
        lax.psum_scatter(
            expert_stacked[0].astype(jnp.bfloat16), "dp", scatter_dimension=3, tiled=True
        ).astype(jnp.float32),
        lax.psum_scatter(
            expert_stacked[1].astype(jnp.bfloat16), "dp", scatter_dimension=3, tiled=True
        ).astype(jnp.float32),
    )
    tokens_grad = grad.astype(jnp.bfloat16)[None]
    return (
        block_out,
        tokens_grad,
        large_grads[0],
        large_grads[1],
        large_grads[2],
        large_grads[3],
        small_grads[0],
        small_grads[1],
        expert_total[0],
        expert_total[1],
    )


def solution(mesh):
    in_specs = (
        P(("dp", "expert"), "wshard", None),
        P(("dp", "expert")),
        P(("dp", "expert"), "wshard", None),
        P(("dp", "expert"), "wshard"),
        P(("dp", "expert"), "wshard", None),
        P(None, None, "wshard", None),
        P(None, "wshard", None),
        P(None, None, "wshard", None),
        P(None, "wshard", None),
        P(None, "wshard", None),
        P(None, None, "wshard"),
        P(None, "expert", None, None, "wshard"),
        P(None, "expert", "wshard", None),
    )
    out_specs = (
        P(("dp", "expert"), "wshard", None),
        P(("dp", "expert"), "wshard", None),
        P(None, None, "wshard", ("dp", "expert")),
        P(None, "wshard", ("dp", "expert")),
        P(None, None, "wshard", ("dp", "expert")),
        P(None, "wshard", ("dp", "expert")),
        P(None, "wshard", None),
        P(None, None, "wshard"),
        P(None, "expert", None, "dp", "wshard"),
        P(None, "expert", "wshard", "dp"),
    )
    return jax.shard_map(
        per_device, mesh=mesh, in_specs=in_specs, out_specs=out_specs, check_vma=False
    )
```

profile of v0, /device:TPU:4, one launch (start us, length us, event | category | flops | bytes accessed | tf_op | source)
XLA Modules:
  0.0 2242.0 jit_solution(15067761584487557871)
XLA Ops:
  26.7 33.8 %all-gather.7.cloned.1.call-done = bf16[2,3,768,768]{3,2,1,0:T(8,128)(2,1)} async-done(((bf16[2,3,192,768]{3,2,1,0:T(8,128)(2,1)}), bf16[2,3,768,768]{3,2,1,0:T(8,128)(2,1)}) %all-gather.7.cloned.1.call-update) | async-done | bytes 7077904 | tf_op jit(solution)/shard_map/all_gather | solution.py:151
  72.9 13.6 all_gather.33
  101.7 31.6 %all-to-all-done = bf16[8,2,80,768]{3,2,1,0:T(8,128)(2,1)S(1)} async-done(((bf16[8,2,80,768]{3,2,1,0:T(8,128)(2,1)}), bf16[8,2,80,768]{3,2,1,0:T(8,128)(2,1)S(1)}, u32[]{:S(2)}, u32[]{:S(2)}) %all-to-all-start) | async-done | bytes 1966112 | tf_op jit(solution)/shard_map/all_to_all | solution.py:87
  152.9 38.1 %all_gather.37 = bf16[2,768,4]{2,0,1:T(2,128)(2,1)S(1)} all-gather(bf16[2,192,4]{2,0,1:T(2,128)(2,1)S(1)} %copy.287), channel_id=1, replica_groups=mesh['dp'=4,'expert'=2,'wshard'=4] {'wshard'}, dimensions={1}, use_global_device_ids=true | all-gather | bytes 15360 | tf_op jit(solution)/shard_map/all_gather | solution.py:155
  220.5 44.0 %all-gather.13.cloned.1.call-done = bf16[2,2048,768]{2,1,0:T(8,128)(2,1)} async-done(((bf16[2,512,768]{2,1,0:T(8,128)(2,1)}), bf16[2,2048,768]{2,1,0:T(8,128)(2,1)}) %all-gather.13.cloned.1.call-update) | async-done | bytes 6291472 | tf_op jit(solution)/shard_map/all_gather | solution.py:154
  308.2 17.9 all-to-all-done.2
  358.8 9.0 all-to-all-done.3
  383.8 23.7 %all-to-all-done.4 = bf16[8,2,80,768]{3,2,1,0:T(8,128)(2,1)S(1)} async-done(((bf16[8,2,80,768]{3,2,1,0:T(8,128)(2,1)}), bf16[8,2,80,768]{3,2,1,0:T(8,128)(2,1)S(1)}, u32[]{:S(2)}, u32[]{:S(2)}) %all-to-all-start.4) | async-done | bytes 1966112 | tf_op jit(solution)/shard_map/all_to_all | solution.py:87
  479.4 14.5 reduce-scatter.34.cloned.1.call-done
  495.6 24.6 %reduce-scatter.26.cloned.1.call-done = bf16[128,768]{1,0:T(8,128)(2,1)} async-done(((bf16[512,768]{1,0:T(8,128)(2,1)}), bf16[128,768]{1,0:T(8,128)(2,1)}) %reduce-scatter.26.cloned.1.call-update) | async-done | bytes 196624 | tf_op jit(solution)/shard_map/reduce_scatter | solution.py:350
  526.8 28.5 %all_to_all.96 = bf16[8,2,80,768]{3,2,1,0:T(8,128)(2,1)S(1)} all-to-all(bf16[8,2,80,768]{3,2,1,0:T(8,128)(2,1)S(1)} %bitcast.617), channel_id=1, replica_groups=mesh['dp'=4,'expert'=2,'wshard'=4] {'expert','wshard'}, dimensions={0} | all-to-all | bytes 3932160 | tf_op jit(solution)/shard_map/all_to_all | solution.py:87
  642.0 31.6 %copy.331 = bf16[2,2,768,2048]{3,1,0,2:T(2,128)(2,1)} copy(bf16[2,2,768,2048]{2,3,1,0:T(8,128)(2,1)} %pad_maximum_fusion) | data formatting | bytes 25165824 | tf_op jit(solution)/shard_map/stack | solution.py:383
  684.8 18.3 copy.328
  740.7 16.4 copy.335
  771.2 329.3 %all-reduce.14.cloned.1.call-done = (bf16[2,3,768,768]{3,0,1,2:T(2,128)(2,1)}, bf16[2,2,768,2048]{3,1,0,2:T(2,128)(2,1)}) async-done(((bf16[2,3,768,768]{3,0,1,2:T(2,128)(2,1)}, bf16[2,2,768,2048]{3,1,0,2:T(2,128)(2,1)}), (bf16[2,3,768,768]{3,0,1,2:T(2,128)(2,1)}, bf16[2,2,768,2048]{3,1,0,2:T(2,128)(2,1)})) %all-reduce.14.cloned.1.call-update) | async-done | bytes 19660816
  1103.2 146.5 %copy.369 = bf16[2,3,192,768]{0,1,2,3:T(4,128)(2,1)} copy(bf16[2,3,192,768]{3,0,1,2:T(2,128)(2,1)S(1)} %constant_dynamic-slice_fusion.1) | data formatting | bytes 3538944
  1249.7 132.8 %reshape.814 = bf16[768,1152]{1,0:T(8,128)(2,1)} reshape(bf16[768,192,3,2]{3,2,1,0:T(4,128)(2,1)} %bitcast.185) | data formatting | bytes 3538944
  1387.8 313.9 %copy.373 = bf16[2,2,192,2048]{1,0,2,3:T(2,128)(2,1)} copy(bf16[2,2,192,2048]{3,1,0,2:T(2,128)(2,1)S(1)} %constant_dynamic-slice_fusion) | data formatting | bytes 6291456
  1701.7 323.3 %reshape.818 = bf16[2048,768]{1,0:T(8,128)(2,1)} reshape(bf16[2048,192,2,2]{3,2,1,0:T(2,128)(2,1)} %bitcast.190) | data formatting | bytes 6291456
  2034.3 38.4 %all-reduce.5 = (f32[2,192,4]{1,2,0:T(4,128)}, f32[2,2,192]{2,1,0:T(2,128)}) all-reduce(bf16[2,192,4]{1,2,0:T(4,128)(2,1)S(1)} %copy.376, bf16[2,2,192]{2,1,0:T(2,128)(2,1)S(1)} %copy.378), channel_id=1, replica_groups=mesh['dp'=4,'expert'=2,'wshard'=4] {'dp','expert'}, use_global_device_ids=true, to_apply=%region_47.49 | all-reduce | flops 2304 | bytes 13824 | tf_op jit(solution)/shard_map/psum | solution.py:419
  2086.4 18.4 reshape.815
  2104.9 22.3 copy.370
  2128.0 56.0 %reshape.819 = bf16[256,192,2,2]{3,2,1,0:T(2,128)(2,1)} reshape(bf16[256,768]{1,0:T(8,128)(2,1)} %reduce-scatter.42.cloned.1.call-done) | data formatting | bytes 786432
  2184.0 49.9 %copy.374 = bf16[2,2,192,256]{3,1,0,2:T(2,128)(2,1)S(1)} copy(bf16[2,2,192,256]{1,0,2,3:T(2,128)(2,1)} %bitcast.602) | data formatting | bytes 786432
  (689 shorter events, 445.3 us)
Async XLA Ops:
  7.2 53.3 %all-gather.7.cloned.1.call-start = ((), (), s32[]{:S(2)}) async-start(), calls=%async_computation.19 | async-start | bytes 8847360 | tf_op jit(solution)/shard_map/all_gather | solution.py:151
  8.0 82.9 %all-gather.9.cloned.1.call-start = ((), (), s32[]{:S(2)}) async-start(), calls=%async_computation.20 | async-start | bytes 2949120 | tf_op jit(solution)/shard_map/all_gather | solution.py:152
  8.7 208.0 %all-gather.11.cloned.1.call-start = ((), (), s32[]{:S(2)}) async-start(), calls=%async_computation.21 | async-start | bytes 15728640 | tf_op jit(solution)/shard_map/all_gather | solution.py:153
  9.4 255.0 %all-gather.13.cloned.1.call-start = ((), (), s32[]{:S(2)}) async-start(), calls=%async_computation.22 | async-start | bytes 7864320 | tf_op jit(solution)/shard_map/all_gather | solution.py:154
  96.5 36.8 %all-to-all-start = ((bf16[8,2,80,768]{3,2,1,0:T(8,128)(2,1)}), bf16[8,2,80,768]{3,2,1,0:T(8,128)(2,1)S(1)}, u32[]{:S(2)}, u32[]{:S(2)}) async-start(bf16[8,2,80,768]{3,2,1,0:T(8,128)(2,1)} %bitcast.614), calls=%async_computation | async-start | bytes 3932160 | tf_op jit(solution)/shard_map/all_to_all | solution.py:87
  147.0 54.9 %all-to-all-start.1 = ((bf16[1,2,640,768]{3,1,0,2:T(2,128)(2,1)}), bf16[1,2,640,768]{3,1,0,2:T(2,128)(2,1)S(1)}, u32[]{:S(2)}, u32[]{:S(2)}) async-start(bf16[1,2,640,768]{3,1,0,2:T(2,128)(2,1)} %copy.293), calls=%async_computation.1 | async-start | bytes 3932160 | tf_op jit(solution)/shard_map/all_to_all | solution.py:93
  297.3 28.8 %all-to-all-start.2 = ((bf16[8,2,80,768]{3,2,1,0:T(8,128)(2,1)}), bf16[8,2,80,768]{3,2,1,0:T(8,128)(2,1)S(1)}, u32[]{:S(2)}, u32[]{:S(2)}) async-start(bf16[8,2,80,768]{3,2,1,0:T(8,128)(2,1)} %bitcast.615), calls=%async_computation.2 | async-start | bytes 3932160 | tf_op jit(solution)/shard_map/all_to_all | solution.py:87
  339.6 28.2 %all-to-all-start.3 = ((bf16[1,2,640,768]{3,1,0,2:T(2,128)(2,1)}), bf16[1,2,640,768]{3,1,0,2:T(2,128)(2,1)S(1)}, u32[]{:S(2)}, u32[]{:S(2)}) async-start(bf16[1,2,640,768]{3,1,0,2:T(2,128)(2,1)} %copy.302), calls=%async_computation.3 | async-start | bytes 3932160 | tf_op jit(solution)/shard_map/all_to_all | solution.py:93
  419.8 27.8 %all-to-all-start.5 = ((bf16[1,2,640,768]{3,1,0,2:T(2,128)(2,1)}), bf16[1,2,640,768]{3,1,0,2:T(2,128)(2,1)S(1)}, u32[]{:S(2)}, u32[]{:S(2)}) async-start(bf16[1,2,640,768]{3,1,0,2:T(2,128)(2,1)} %copy.307), calls=%async_computation.5 | async-start | bytes 3932160 | tf_op jit(solution)/shard_map/all_to_all | solution.py:93
  423.8 70.1 %reduce-scatter.34.cloned.1.call-start = ((), (), s32[]{:S(2)}) async-start(), calls=%async_computation.27 | async-start | bytes 983040
  471.7 48.5 %reduce-scatter.26.cloned.1.call-start = ((), (), s32[]{:S(2)}) async-start(), calls=%async_computation.23 | async-start | bytes 983040 | tf_op jit(solution)/shard_map/reduce_scatter | solution.py:350
  563.6 29.4 %all-to-all-start.7 = ((bf16[1,2,640,768]{3,1,0,2:T(2,128)(2,1)}), bf16[1,2,640,768]{3,1,0,2:T(2,128)(2,1)}, u32[]{:S(2)}, u32[]{:S(2)}) async-start(bf16[1,2,640,768]{3,1,0,2:T(2,128)(2,1)} %copy.318), calls=%async_computation.8 | async-start | bytes 3932160 | tf_op jit(solution)/shard_map/all_to_all | solution.py:93
  569.1 108.3 %reduce-scatter.36.cloned.1.call-start = ((), (), s32[]{:S(2)}) async-start(), calls=%async_computation.28 | async-start | bytes 983040
  617.3 61.7 %reduce-scatter.28.cloned.1.call-start = ((), (), s32[]{:S(2)}) async-start(), calls=%async_computation.24 | async-start | bytes 983040 | tf_op jit(solution)/shard_map/reduce_scatter | solution.py:350
  621.6 104.6 %reduce-scatter.30.cloned.1.call-start = ((), (), s32[]{:S(2)}) async-start(), calls=%async_computation.25 | async-start | bytes 2949120 | tf_op jit(solution)/shard_map/reduce_scatter | solution.py:389
  624.3 140.5 %reduce-scatter.32.cloned.1.call-start = ((), (), s32[]{:S(2)}) async-start(), calls=%async_computation.26 | async-start | bytes 7864320 | tf_op jit(solution)/shard_map/reduce_scatter | solution.py:395
  631.7 468.8 %all-reduce.14.cloned.1.call-start = ((), (), s32[]{:S(2)}) async-start(), calls=%async_computation.35 | async-start | bytes 39321600
  703.2 1325.0 %reduce-scatter.44.cloned.1.call-start = ((), (), s32[]{:S(2)}) async-start(), calls=%async_computation.32 | async-start | bytes 245760
  712.5 1320.8 %reduce-scatter.46.cloned.1.call-start = ((), (), s32[]{:S(2)}) async-start(), calls=%async_computation.33 | async-start | bytes 245760
  721.6 1351.1 %reduce-scatter.40.cloned.1.call-start = ((), (), s32[]{:S(2)}) async-start(), calls=%async_computation.30 | async-start | bytes 663552
  732.4 1342.1 %all-reduce.16.cloned.1.call-start = ((), (), s32[]{:S(2)}) async-start(), calls=%async_computation.36 | async-start | bytes 18874368
  764.7 1319.8 %all-reduce.12.cloned.1.call-start = ((), (), s32[]{:S(2)}) async-start(), calls=%async_computation.34 | async-start | bytes 3145728
  769.8 1316.7 %reduce-scatter.38.cloned.1.call-start = ((), (), s32[]{:S(2)}) async-start(), calls=%async_computation.29 | async-start | bytes 1990656
  1382.5 745.5 %reduce-scatter.42.cloned.1.call-start = ((), (), s32[]{:S(2)}) async-start(), calls=%async_computation.31 | async-start | bytes 3538944
  (179 other events, 3098.4 us)
Sparse Core Ops, SparseCore 0:
  9.6 50.8 all-gather.6
  62.0 28.2 all-gather.8
  91.9 124.7 all-gather.10
  218.1 46.3 all-gather.12
  471.8 22.1 reduce-scatter.33
  496.9 23.1 reduce-scatter.25
  617.4 22.0 reduce-scatter.35
  642.7 23.1 reduce-scatter.27
  669.0 32.8 reduce-scatter.29
  704.2 58.8 reduce-scatter.31
  765.8 334.7 all-reduce.13
  1103.4 19.6 reduce-scatter.43
  1126.1 19.7 reduce-scatter.45
  1149.7 63.9 reduce-scatter.39
  1216.7 323.7 all-reduce.15
  1543.8 88.2 all-reduce.11
  1635.4 65.7 reduce-scatter.37
  2025.1 75.7 reduce-scatter.41
where the time goes:
time: 2260 us; the launch traced here: 2240 us
  local copies, waits for them, and re-layouts  1290 us (57%)
  waiting for transfers between devices  552 us (24%)
  blocking collectives  151 us (7%)
  matrix products  126 us (6%)
  other arithmetic  64.5 us (3%)
  starting transfers between devices  36 us (2%)
    unnamed x393, local copies, waits for them, and re-layouts  1130 us
    unnamed x28, waiting for transfers between devices  347 us
    all_to_all x3, waiting for transfers between devices, dispatch(): lax.all_to_all(copies, ('expert', 'wshard'), split_axis=0, concat_axis=2,...  73.2 us
    another operation x2, local copies, waits for them, and re-layouts, per_device(): jnp.stack([part[index] for part in dense_parts], axis=0)  50 us
  transfers between devices with their start and end apart: 25, of which 12 were waited for; matrix products, arithmetic and copies ran while one was open for 56% of the time, Pallas kernels for 0%

commit v1 on v0

v1 whole, which is shorter than its diff:
```python
import functools

import jax
import jax.numpy as jnp
from jax import lax
from jax.experimental import pallas as pl
from jax.experimental.pallas import tpu as pltpu
from jax.sharding import PartitionSpec as P

HEADS = 12
LAYERS = 2
epsilon = 1e-06
rotary_base = 10000.0
HEAD_DIM = 64
floor_score = -1e30
bf16 = jnp.bfloat16
f32 = jnp.float32
VMEM_LIMIT = 60 << 20


def mul(a, b):
    return lax.dot_general(a, b, (((1,), (0,)), ((), ())), preferred_element_type=f32)


def mul_nt(a, b):
    return lax.dot_general(a, b, (((1,), (1,)), ((), ())), preferred_element_type=f32)


def mul_tn(a, b):
    return lax.dot_general(a, b, (((0,), (0,)), ((), ())), preferred_element_type=f32)


def mul_pair(a, b):
    high = b.astype(bf16)
    low = (b - high.astype(f32)).astype(bf16)
    return mul(a, high) + mul(a, low)


def rows_at(index, size):
    return pl.ds(pl.multiple_of(index * size, size), size)


def call(kernel, outs, scratch, *operands, cost=None):
    vmem = pl.BlockSpec(memory_space=pltpu.VMEM)
    return pl.pallas_call(
        kernel,
        out_shape=tuple(jax.ShapeDtypeStruct(s, d) for s, d in outs),
        in_specs=[vmem] * len(operands),
        out_specs=tuple([vmem] * len(outs)),
        scratch_shapes=[pltpu.VMEM(s, d) for s, d in scratch],
        compiler_params=pltpu.CompilerParams(vmem_limit_bytes=VMEM_LIMIT),
        cost_estimate=cost,
    )(*operands)


def swapped(values):
    lane = lax.broadcasted_iota(jnp.int32, values.shape, 1)
    half = HEAD_DIM // 2
    size = values.shape[1]
    return jnp.where(
        lax.rem(lane, HEAD_DIM) < half,
        pltpu.roll(values, size - half, 1),
        pltpu.roll(values, half, 1),
    )


def attend_kernel(
    hidden, weight, cosine, sine, length, out_weight, partial, queries, keys, values, probs, attended
):
    count = hidden.shape[0]
    window = cosine.shape[1]
    tile = count // 2
    for part, ref in enumerate((queries, keys, values)):
        made = mul(hidden[...], weight[part])
        if part < 2:
            made = made * cosine[...] + swapped(made) * sine[...]
        if part == 0:
            made = made * (HEAD_DIM ** (-0.5))
        ref[...] = made.astype(bf16)
    limit = length[0:1, 0:1]
    for head in range(window // HEAD_DIM):
        lanes = slice(head * HEAD_DIM, (head + 1) * HEAD_DIM)
        for block in range(2):
            seen = (block + 1) * tile
            own = slice(block * tile, seen)
            raw = mul_nt(queries[own, lanes], keys[0:seen, lanes])
            row = lax.broadcasted_iota(jnp.int32, raw.shape, 0) + block * tile
            column = lax.broadcasted_iota(jnp.int32, raw.shape, 1)
            raw = jnp.where((column <= row) & (column < limit), raw, floor_score)
            raised = jnp.exp(raw - jnp.max(raw, axis=-1, keepdims=True))
            prob = (raised / jnp.sum(raised, axis=-1, keepdims=True)).astype(bf16)
            probs[head, own, 0:seen] = prob
            attended[own, lanes] = mul(prob, values[0:seen, lanes]).astype(bf16)
    partial[...] = mul(attended[...], out_weight[...]).astype(bf16)


def attend(hidden, weight, cosine, sine, length, out_weight):
    count, width = hidden.shape
    window = cosine.shape[1]
    heads = window // HEAD_DIM
    piece = ((count, window), bf16)
    return call(
        attend_kernel,
        [((count, width), bf16), piece, piece, piece, ((heads, count, count), bf16), piece],
        [],
        hidden, weight, cosine, sine, length, out_weight,
    )


def attend_back_kernel(
    grad, hidden, weight, cosine, sine, queries, keys, values, probs, attended, out_weight, spread,
    partial, dense, attended_grad, dq, dk, dv, made, lift,
):
    count, width = grad.shape
    window = cosine.shape[1]
    tile = count // 2
    columns = dense.shape[0]
    owners = spread.shape[1] // 128
    planes = columns // owners
    chunk = width // planes
    side = width // columns
    attended_grad[...] = mul_nt(grad[...], out_weight[...]).astype(bf16)
    for head in range(window // HEAD_DIM):
        lanes = slice(head * HEAD_DIM, (head + 1) * HEAD_DIM)
        for block in (1, 0):
            seen = (block + 1) * tile
            own = slice(block * tile, seen)
            prob_b = probs[head, own, 0:seen]
            prob = prob_b.astype(f32)
            mine = attended_grad[own, lanes]
            prob_grad = mul_nt(mine, values[0:seen, lanes])
            score = prob * (prob_grad - jnp.sum(prob * prob_grad, axis=-1, keepdims=True))
            score = score.astype(bf16)
            dq[own, lanes] = mul(score, keys[0:seen, lanes])
            key_part = mul_tn(score, queries[own, lanes])
            value_part = mul_tn(prob_b, mine)
            if block == 1:
                dk[0:seen, lanes] = key_part
                dv[0:seen, lanes] = value_part
            else:
                dk[0:seen, lanes] = dk[0:seen, lanes] + key_part
                dv[0:seen, lanes] = dv[0:seen, lanes] + value_part
    back = dq[...] * (HEAD_DIM ** (-0.5))
    made[0] = (back * cosine[...] - swapped(back) * sine[...]).astype(bf16)
    back = dk[...]
    made[1] = (back * cosine[...] - swapped(back) * sine[...]).astype(bf16)
    made[2] = dv[...].astype(bf16)
    total = mul_nt(made[0], weight[0])
    total = total + mul_nt(made[1], weight[1])
    total = total + mul_nt(made[2], weight[2])
    partial[...] = total.astype(bf16)
    for part in range(3):
        spaced = mul(made[part], spread[...]).astype(bf16)
        found = mul_tn(hidden[...], spaced)
        for a in range(planes):
            for b in range(owners):
                dense[a * owners + b, part * chunk : (part + 1) * chunk, :] = found[
                    a * chunk : (a + 1) * chunk, b * 128 : (b + 1) * 128
                ].astype(bf16)
    start = pl.multiple_of(lax.rem(lax.axis_index("wshard") * chunk, 128), 64)
    for j in range(columns):
        lift[:, 0:side] = mul_tn(attended[...], grad[:, j * side : (j + 1) * side])
        dense[j, 3 * chunk : 4 * chunk, 0:side] = lift[pl.ds(start, chunk), 0:side].astype(bf16)


def attend_back(
    grad, hidden, weight, cosine, sine, queries, keys, values, probs, attended, out_weight, spread
):
    count, width = hidden.shape
    window = cosine.shape[1]
    owners = spread.shape[1] // 128
    planes = lax.axis_size("dp")
    return call(
        attend_back_kernel,
        [((count, width), bf16), ((planes * owners, 4 * (width // planes), 128), bf16)],
        [
            ((count, window), bf16),
            ((count, window), f32),
            ((count, window), f32),
            ((count, window), f32),
            ((3, count, window), bf16),
            ((window, 128), f32),
        ],
        grad, hidden, weight, cosine, sine, queries, keys, values, probs, attended, out_weight, spread,
    )


def first_lane(shape):
    return lax.broadcasted_iota(jnp.int32, shape, len(shape) - 1)


def expert_kernel(
    mixed, select, back, chosen, router, up, down, wide, narrow,
    partial, arrived, inner, scale, gates, shared_inner, sent, shared_out,
):
    group, _, rows = select.shape
    per_owner, slots, width = arrived.shape
    capacity = slots // group
    units = down.shape[1]
    shards = lax.axis_size("wshard")
    owner = lax.axis_index("expert")
    count = shared_out.shape[0]

    @pl.loop(0, group)
    def _(g):
        block = mixed[rows_at(g, rows), :]
        found = mul(select[g], block).astype(bf16)
        logits = mul_nt(block, router[...]) + chosen[rows_at(g, rows), :]
        raised = jnp.exp(logits - jnp.max(logits, axis=-1, keepdims=True))
        gate = raised / jnp.sum(raised, axis=-1, keepdims=True)
        gates[rows_at(g, rows), :] = gate
        spots = mul_pair(select[g], gate)
        for j in range(per_owner):
            arrived[j, rows_at(g, capacity), :] = found[j * capacity : (j + 1) * capacity]
            scale[j, rows_at(g, capacity), :] = spots[j * capacity : (j + 1) * capacity, j : j + 1]

    parts = 2
    tile = slots // parts

    for j in range(per_owner):

        @pl.loop(0, parts)
        def _(i):
            own = rows_at(i, tile)
            block = arrived[j, own, :]
            gate = mul(block, up[j, 0])
            lift = mul(block, up[j, 1])
            inner[j, own, 0:units] = gate.astype(bf16)
            inner[j, own, units : 2 * units] = lift.astype(bf16)
            act = (gate / (1.0 + jnp.exp(-gate)) * lift).astype(bf16)
            made = (mul(act, down[j]) * scale[j, own, :]).astype(bf16)
            for q in range(group // parts):
                sent[i * (group // parts) + q, j * capacity : (j + 1) * capacity, :] = made[
                    q * capacity : (q + 1) * capacity
                ]

    piece = count // 2

    @pl.loop(0, 2)
    def _(i):
        own = rows_at(i, piece)
        block = mixed[rows_at(owner * 2 + i, piece), :]
        gate = mul(block, wide[0])
        lift = mul(block, wide[1])
        shared_inner[own, 0:units] = gate.astype(bf16)
        shared_inner[own, units : 2 * units] = lift.astype(bf16)
        act = (gate / (1.0 + jnp.exp(-gate)) * lift).astype(bf16)
        shared_out[own, :] = mul(act, narrow[...])

    @pl.loop(0, group)
    def _(g):
        near = jnp.clip(g - owner * shards, 0, shards - 1)
        here = (lax.div(g, shards) == owner).astype(f32)
        made = mul(back[g], sent[g]) + here * shared_out[rows_at(near, rows), :]
        partial[rows_at(g, rows), :] = made.astype(bf16)


def expert(mixed, select, back, chosen, router, up, down, wide, narrow):
    group, spots, rows = select.shape
    per_owner, _, width, units = up.shape
    slots = group * spots // per_owner
    count = rows * lax.axis_size("wshard")
    return call(
        expert_kernel,
        [
            (mixed.shape, bf16),
            ((per_owner, slots, width), bf16),
            ((per_owner, slots, 2 * units), bf16),
            ((per_owner, slots, 1), f32),
            ((group * rows, 128), f32),
            ((count, 2 * units), bf16),
        ],
        [((group, spots, width), bf16), ((count, width), f32)],
        mixed, select, back, chosen, router, up, down, wide, narrow,
    )


def silu_back(grad, gate, lift):
    sig = 1.0 / (1.0 + jnp.exp(-gate))
    silu = gate * sig
    act = (silu * lift).astype(bf16)
    gate_grad = (grad * lift * sig * (1.0 + gate * (1.0 - sig))).astype(bf16)
    lift_grad = (grad * silu).astype(bf16)
    return act, gate_grad, lift_grad


def routed_back_kernel(
    grad, select, up, down, arrived, inner, scale,
    totals, sent, spot,
    picked, deep,
):
    group, spots, rows = select.shape
    per_owner, slots, width = arrived.shape
    capacity = slots // group
    units = down.shape[1]
    planes = totals.shape[0]
    chunk = width // planes

    @pl.loop(0, group)
    def _(g):
        found = mul(select[g], grad[rows_at(g, rows), :]).astype(bf16)
        for j in range(per_owner):
            picked[j, rows_at(g, capacity), :] = found[j * capacity : (j + 1) * capacity]

    parts = 2
    tile = slots // parts

    for j in range(per_owner):

        @pl.loop(0, parts)
        def _(i):
            own = rows_at(i, tile)
            block = picked[j, own, :]
            weigh = scale[j, own, :]
            raw = mul_nt(block, down[j])
            picked[j, own, :] = (block.astype(f32) * weigh).astype(bf16)
            gate = inner[j, own, 0:units].astype(f32)
            lift = inner[j, own, units : 2 * units].astype(f32)
            act, gate_grad, lift_grad = silu_back(raw * weigh, gate, lift)
            heat = jnp.sum(raw * act.astype(f32), axis=-1, keepdims=True)
            heat = jnp.where(first_lane((tile, 128)) == j, heat, 0.0)
            deep[j, 0, own, :] = gate_grad
            deep[j, 1, own, :] = lift_grad
            deep[j, 2, own, :] = act
            made = (mul_nt(gate_grad, up[j, 0]) + mul_nt(lift_grad, up[j, 1])).astype(bf16)
            for q in range(group // parts):
                here = slice(q * capacity, (q + 1) * capacity)
                there = slice(j * capacity, (j + 1) * capacity)
                sent[i * (group // parts) + q, there, :] = made[here]
                spot[i * (group // parts) + q, there, :] = heat[here]

    for j in range(per_owner):
        for s in range(3):
            lead = picked if s == 2 else arrived
            found = mul_tn(lead[j], deep[j, s])
            for a in range(planes):
                totals[a, j, s] = found[a * chunk : (a + 1) * chunk].astype(bf16)


def routed_back(grad, select, up, down, arrived, inner, scale):
    group, spots, rows = select.shape
    per_owner, slots, width = arrived.shape
    units = down.shape[1]
    planes = lax.axis_size("dp")
    return call(
        routed_back_kernel,
        [
            ((planes, per_owner, 3, width // planes, units), bf16),
            ((group, spots, width), bf16),
            ((group, spots, 128), f32),
        ],
        [((per_owner, slots, width), bf16), ((per_owner, 3, slots, units), bf16)],
        grad, select, up, down, arrived, inner, scale,
    )


def shared_back_kernel(
    grad, mixed, back, router, wide, narrow, gates, shared_inner, sent, spot,
    partial, dense, router_grad,
    shared_out, shared_deep,
):
    group, rows, spots = back.shape
    width = grad.shape[1]
    units = narrow.shape[0]
    planes = lax.axis_size("dp")
    chunk = width // planes
    columns = dense.shape[0]
    owners = columns // planes
    side = width // columns
    part = units // owners
    shards = lax.axis_size("wshard")
    owner = lax.axis_index("expert")
    count = shared_out.shape[0]
    piece = count // 2

    @pl.loop(0, 2)
    def _(i):
        own = rows_at(i, piece)
        block = grad[rows_at(owner * 2 + i, piece), :]
        raw = mul_nt(block, narrow[...])
        gate = shared_inner[own, 0:units].astype(f32)
        lift = shared_inner[own, units : 2 * units].astype(f32)
        act, gate_grad, lift_grad = silu_back(raw, gate, lift)
        shared_deep[0, own, :] = gate_grad
        shared_deep[1, own, :] = lift_grad
        shared_deep[2, own, :] = act
        shared_out[own, :] = mul_nt(gate_grad, wide[0]) + mul_nt(lift_grad, wide[1])

    router_grad[...] = jnp.zeros_like(router_grad)

    @pl.loop(0, group)
    def _(g):
        near = jnp.clip(g - owner * shards, 0, shards - 1)
        here = (lax.div(g, shards) == owner).astype(f32)
        gate = gates[rows_at(g, rows), :]
        heat = mul_pair(back[g], spot[g])
        logit = (gate * (heat - jnp.sum(gate * heat, axis=-1, keepdims=True))).astype(bf16)
        router_grad[...] += mul_tn(logit, mixed[rows_at(g, rows), :])
        made = mul(back[g], sent[g]) + mul(logit, router[...])
        made = made + here * shared_out[rows_at(near, rows), :]
        partial[rows_at(g, rows), :] = made.astype(bf16)

    base = 0
    for s in range(2):
        found = mul_tn(mixed[rows_at(owner, count), :], shared_deep[s])
        size = min(part, 128)
        for h in range(part // size):
            for a in range(planes):
                for b in range(owners):
                    lanes = slice(b * part + h * size, b * part + (h + 1) * size)
                    dense[a * owners + b, base : base + chunk, 0:size] = found[
                        a * chunk : (a + 1) * chunk, lanes
                    ].astype(bf16)
            base += chunk
    own_grad = grad[rows_at(owner, count), :]
    for b in range(columns):
        dense[b, base : base + units, 0:side] = mul_tn(
            shared_deep[2], own_grad[:, b * side : (b + 1) * side]
        ).astype(bf16)


def dense_rows(width, units, planes, owners):
    part = units // owners
    return 2 * (part // min(part, 128)) * (width // planes) + units


def shared_back(grad, mixed, back, router, wide, narrow, gates, shared_inner, sent, spot):
    rows = back.shape[1]
    _, width, units = wide.shape
    count = rows * lax.axis_size("wshard")
    planes = lax.axis_size("dp")
    owners = lax.axis_size("expert")
    return call(
        shared_back_kernel,
        [
            (mixed.shape, bf16),
            ((planes * owners, dense_rows(width, units, planes, owners), 128), bf16),
            ((128, width), f32),
        ],
        [((count, width), f32), ((3, count, units), bf16)],
        grad, mixed, back, router, wide, narrow, gates, shared_inner, sent, spot,
    )


MESH = pl.DeviceIdType.MESH

def layout(axes):
    wide = lax.axis_size("wshard")
    tall = lax.axis_size("expert") if "expert" in axes else 1
    shard = lax.axis_index("wshard")
    owner = lax.axis_index("expert") if "expert" in axes else 0
    return tall, wide, owner, shard

def steps_of(tall, wide):
    return [(a, b) for a in range(tall) for b in range(wide // 2)]

def place(tall, wide, owner, shard, step, sign, flip):
    half = wide // 2
    own = lax.rem(owner + sign * step[0] + tall, tall) if tall > 1 else 0
    low = lax.rem(shard, 2)
    if flip:
        low = 1 - low
    pair = lax.rem(lax.div(shard, 2) + sign * step[1] + half, half)
    return own, pair * 2 + low

def target(axes, where):
    named = {"wshard": where[1]}
    if "expert" in axes:
        named["expert"] = where[0]
    return named

def greet(axes, tall, wide, owner, shard):
    barrier = pltpu.get_barrier_semaphore()
    steps = steps_of(tall, wide)
    for step in steps[1:]:
        pl.semaphore_signal(barrier, inc=1, device_id=target(axes, place(tall, wide, owner, shard, step, 1, False)), device_id_type=MESH)
    pl.semaphore_signal(barrier, inc=1, device_id=target(axes, place(tall, wide, owner, shard, steps[0], 1, True)), device_id_type=MESH)
    pl.semaphore_wait(barrier, len(steps))

def gather_kernel(axes, x_ref, o_ref, send, recv, fsend, frecv):
    tall, wide, owner, shard = layout(axes)
    steps = steps_of(tall, wide)
    rows = x_ref.shape[0]
    def block(where):
        return o_ref.at[pl.ds(pl.multiple_of((where[0] * wide + where[1]) * rows, rows), rows)]
    me = (owner, shard)
    partner = place(tall, wide, owner, shard, steps[0], 1, True)
    greet(axes, tall, wide, owner, shard)
    copies = []
    for i, step in reversed(list(enumerate(steps))):
        there = partner if i == 0 else place(tall, wide, owner, shard, step, 1, False)
        copy = pltpu.make_async_remote_copy(src_ref=x_ref, dst_ref=block(me), send_sem=send.at[i], recv_sem=recv.at[i], device_id=target(axes, there), device_id_type=MESH)
        copy.start()
        copies.append(copy)
    mine = block(me)
    mine[...] = x_ref[...]
    passed = []
    for i, step in list(enumerate(steps))[1:]:
        source = place(tall, wide, owner, shard, step, -1, False)
        arrived = pltpu.make_async_remote_copy(src_ref=x_ref, dst_ref=block(source), send_sem=send.at[i], recv_sem=recv.at[i], device_id=target(axes, partner), device_id_type=MESH)
        arrived.wait_recv()
        onward = pltpu.make_async_remote_copy(src_ref=block(source), dst_ref=block(source), send_sem=fsend.at[i - 1], recv_sem=frecv.at[i - 1], device_id=target(axes, partner), device_id_type=MESH)
        onward.start()
        passed.append(onward)
    last = pltpu.make_async_remote_copy(src_ref=x_ref, dst_ref=block(partner), send_sem=send.at[0], recv_sem=recv.at[0], device_id=target(axes, partner), device_id_type=MESH)
    last.wait_recv()
    for i, step in list(enumerate(steps))[1:]:
        source = place(tall, wide, owner, shard, step, -1, True)
        arrived = pltpu.make_async_remote_copy(src_ref=x_ref, dst_ref=block(source), send_sem=fsend.at[i - 1], recv_sem=frecv.at[i - 1], device_id=target(axes, partner), device_id_type=MESH)
        arrived.wait_recv()
    for copy in copies + passed:
        copy.wait_send()

def gather(x, axes, cid):
    n = lax.axis_size("wshard") * (lax.axis_size("expert") if "expert" in axes else 1)
    h = n // 2
    dma = pltpu.SemaphoreType.DMA
    return pl.pallas_call(functools.partial(gather_kernel, axes),
        out_shape=jax.ShapeDtypeStruct((n * x.shape[0],) + x.shape[1:], x.dtype),
        in_specs=[pl.BlockSpec(memory_space=pltpu.VMEM)], out_specs=pl.BlockSpec(memory_space=pltpu.VMEM),
        scratch_shapes=[dma((h,)), dma((h,)), dma((max(h - 1, 1),)), dma((max(h - 1, 1),))],
        compiler_params=pltpu.CompilerParams(collective_id=cid, has_side_effects=True, vmem_limit_bytes=32 << 20))(x)

def reduce_kernel(axes, p_ref, o_ref, inbox, total, second, send, recv, fsend, frecv):
    tall, wide, owner, shard = layout(axes)
    steps = steps_of(tall, wide)
    rows = o_ref.shape[0]
    def block(where):
        return pl.ds(pl.multiple_of((where[0] * wide + where[1]) * rows, rows), rows)
    partner = place(tall, wide, owner, shard, steps[0], 1, True)
    greet(axes, tall, wide, owner, shard)
    order = list(reversed(list(enumerate(steps))))
    copies = []
    for i, step in order:
        there = place(tall, wide, owner, shard, step, 1, True)
        copy = pltpu.make_async_remote_copy(src_ref=p_ref.at[block(there)], dst_ref=inbox.at[i], send_sem=send.at[i], recv_sem=recv.at[i], device_id=target(axes, partner), device_id_type=MESH)
        copy.start()
        copies.append(copy)
    onward = []
    for n, (i, step) in enumerate(order):
        copies[n].wait_recv()
        there = place(tall, wide, owner, shard, step, 1, False)
        both = p_ref[block(there)].astype(jnp.float32) + inbox[i].astype(jnp.float32)
        if i == 0:
            o_ref[...] = both
        else:
            total[i - 1] = both.astype(total.dtype)
            copy = pltpu.make_async_remote_copy(src_ref=total.at[i - 1], dst_ref=second.at[i - 1], send_sem=fsend.at[i - 1], recv_sem=frecv.at[i - 1], device_id=target(axes, there), device_id_type=MESH)
            copy.start()
            onward.append((i, copy))
    for i, copy in onward:
        copy.wait_recv()
        o_ref[...] += second[i - 1].astype(jnp.float32)
    for copy in copies:
        copy.wait_send()
    for i, copy in onward:
        copy.wait_send()

def reduce(p, axes, cid):
    n = lax.axis_size("wshard") * (lax.axis_size("expert") if "expert" in axes else 1)
    h = n // 2
    rows = p.shape[0] // n
    dma = pltpu.SemaphoreType.DMA
    blk = (rows,) + p.shape[1:]
    return pl.pallas_call(functools.partial(reduce_kernel, axes),
        out_shape=jax.ShapeDtypeStruct(blk, jnp.float32),
        in_specs=[pl.BlockSpec(memory_space=pltpu.VMEM)], out_specs=pl.BlockSpec(memory_space=pltpu.VMEM),
        scratch_shapes=[pltpu.VMEM((h,) + blk, p.dtype), pltpu.VMEM((h - 1,) + blk, p.dtype), pltpu.VMEM((h - 1,) + blk, p.dtype), dma((h,)), dma((h,)), dma((h - 1,)), dma((h - 1,))],
        compiler_params=pltpu.CompilerParams(collective_id=cid, has_side_effects=True, vmem_limit_bytes=32 << 20))(p)


def norm_parts(values):
    inverse = lax.rsqrt(jnp.mean(values * values, axis=-1, keepdims=True) + epsilon)
    return (values * inverse, inverse)


def norm_back(grads, normed, inverse):
    return inverse * (grads - normed * jnp.mean(grads * normed, axis=-1, keepdims=True))


SLOT = ("wshard",)
PLANE = ("expert", "wshard")


def per_device(
    tokens,
    lengths,
    routes,
    drop_order,
    cotangent,
    qkv_weight,
    out_weight,
    shared_up,
    shared_down,
    router_weight,
    norm_gains,
    expert_up,
    expert_down,
):
    rows = tokens.shape[1]
    width = tokens.shape[2]
    shards = lax.axis_size("wshard")
    shard = lax.axis_index("wshard")
    owners = lax.axis_size("expert")
    owner = lax.axis_index("expert")
    planes = lax.axis_size("dp")
    assert planes == shards
    group = owners * shards
    columns = planes * owners
    count = rows * shards
    experts = router_weight.shape[2]
    per_owner = expert_up.shape[1]
    units = expert_up.shape[4]
    capacity = (10 * rows + 4 * experts - 1) // (4 * experts)
    room = (capacity + 15) // 16 * 16
    chunk = width // shards
    side = width // columns
    window = (chunk + 127) // 128 * 128
    offset = lax.rem(shard * chunk, 128)
    starts = [a * chunk // 128 * 128 for a in range(shards)]
    transposed = [(a * shards + b, b * shards + a) for a in range(planes) for b in range(shards)]

    positions = shard * rows + jnp.arange(rows, dtype=jnp.int32)
    valid = positions < lengths[0]
    facts = jnp.stack(
        [routes[0, :, 0], routes[0, :, 1], drop_order[0], valid.astype(jnp.int32)], axis=0
    )
    facts = jnp.concatenate([facts, jnp.zeros_like(facts)], axis=0)
    facts = gather(facts, PLANE, 5).reshape(group, 8, rows)
    mine = owner * per_owner + jnp.arange(per_owner, dtype=jnp.int32)
    first = facts[:, None, 0, :] == mine[None, :, None]
    second = facts[:, None, 1, :] == mine[None, :, None]
    live = (first | second) & (facts[:, None, 3, :] > 0)
    priority = facts[:, None, 2, :] + jnp.where(second, count, 0)
    earlier = (priority[:, :, None, :] < priority[:, :, :, None]) & live[:, :, None, :]
    place = jnp.sum(earlier.astype(jnp.int32), axis=-1)
    place = jnp.where(live & (place < capacity), place, room)
    spot = jnp.arange(room, dtype=jnp.int32)
    select = (place[:, :, None, :] == spot[None, None, :, None]).astype(bf16)
    select = select.reshape(group, per_owner * room, rows)
    back = (place.transpose(0, 2, 1)[:, :, :, None] == spot[None, None, None, :]).astype(bf16)
    back = back.reshape(group, rows, per_owner * room)
    lane = jnp.arange(128, dtype=jnp.int32)
    named = jnp.where(lane < experts, lax.rem(lane + owner * per_owner, experts), -1)
    both = (facts[:, 0, :, None] == named) | (facts[:, 1, :, None] == named)
    chosen = jnp.where(both, 0.0, floor_score).astype(f32).reshape(group * rows, 128)

    project = jnp.stack([qkv_weight[..., s : s + window] for s in starts], axis=0)
    project = lax.all_to_all(project, "wshard", split_axis=0, concat_axis=0, tiled=True)
    project = project.transpose(1, 2, 0, 3, 4).reshape(LAYERS, 3, width, window)
    wide = shared_up.reshape(LAYERS, 2, chunk, shards, units)
    wide = lax.all_to_all(
        wide.transpose(3, 0, 1, 2, 4), "wshard", split_axis=0, concat_axis=0, tiled=True
    )
    wide = wide.transpose(1, 2, 0, 3, 4).reshape(LAYERS, 2, width, units)
    small = jnp.concatenate([router_weight.transpose(0, 2, 1), norm_gains], axis=1)
    small = lax.all_gather(small, "wshard", axis=2, tiled=True)
    router_full = jnp.zeros((LAYERS, 128, width), bf16)
    router_full = router_full.at[:, :experts].set(
        jnp.roll(small[:, :experts], -owner * per_owner, axis=1)
    )
    gains_full = small[:, experts:].astype(f32)
    out_padded = lax.dynamic_update_slice(
        jnp.zeros((LAYERS, window, width), bf16), out_weight, (0, offset, 0)
    )
    half = HEAD_DIM // 2
    lanes = jnp.arange(window, dtype=jnp.int32)
    angles = jnp.arange(count, dtype=jnp.int32).astype(f32)[:, None] * (
        rotary_base ** (-(lanes % half).astype(f32) / half)
    )[None, :]
    cosine = jnp.cos(angles)
    sine = jnp.where((lanes % HEAD_DIM < half)[None, :], -jnp.sin(angles), jnp.sin(angles))
    length = jnp.broadcast_to(lengths[:, None], (8, 128))
    sub = chunk // owners
    slot_lane = jnp.arange(owners * 128, dtype=jnp.int32)
    origin = jnp.where(slot_lane % 128 < sub, offset + slot_lane // 128 * sub + slot_lane % 128, -1)
    spread = (lanes[:, None] == origin[None, :]).astype(bf16)

    grad_block = (cotangent[0].astype(f32) * valid[:, None].astype(f32)).astype(bf16)
    grad_plane = gather(grad_block, PLANE, 2)

    stream = tokens[0].astype(f32)
    saved = []
    for layer in range(LAYERS):
        gains = gains_full[layer]
        normed_a, inverse_a = norm_parts(stream)
        hidden = gather((normed_a * gains[0]).astype(bf16), SLOT, 1)
        partial, queries, keys, values, probs, attended = attend(
            hidden, project[layer], cosine, sine, length, out_padded[layer]
        )
        middle = stream + reduce(partial, SLOT, 3)
        normed_b, inverse_b = norm_parts(middle)
        mixed = gather((normed_b * gains[1]).astype(bf16), PLANE, 2)
        partial, arrived, inner, scale, gates, shared_inner = expert(
            mixed, select, back, chosen, router_full[layer], expert_up[layer], expert_down[layer],
            wide[layer], shared_down[layer],
        )
        stream = middle + reduce(partial, PLANE, 4)
        saved.append(
            (normed_a, inverse_a, hidden, queries, keys, values, probs, attended, normed_b,
             inverse_b, mixed, arrived, inner, scale, gates, shared_inner)
        )
    block_out = stream.astype(bf16)[None]
    grad = grad_block.astype(f32)
    gathered = []
    small_grads = [None] * LAYERS
    for layer in reversed(range(LAYERS)):
        (normed_a, inverse_a, hidden, queries, keys, values, probs, attended, normed_b,
         inverse_b, mixed, arrived, inner, scale, gates, shared_inner) = saved[layer]
        gains = gains_full[layer]
        if layer < LAYERS - 1:
            grad_plane = gather(grad.astype(bf16), PLANE, 2)
        totals, sent, heat = routed_back(
            grad_plane, select, expert_up[layer], expert_down[layer], arrived, inner, scale
        )
        partial, dense_b, router_grad = shared_back(
            grad_plane, mixed, back, router_full[layer], wide[layer], shared_down[layer], gates,
            shared_inner, sent, heat,
        )
        mixed_grad = reduce(partial, PLANE, 4)
        gain_b_grad = jnp.sum(mixed_grad * normed_b, axis=0)
        middle_grad = grad + norm_back(mixed_grad * gains[1], normed_b, inverse_b)
        branch_grad = gather(middle_grad.astype(bf16), SLOT, 1)
        partial, dense_a = attend_back(
            branch_grad, hidden, project[layer], cosine, sine, queries, keys, values, probs,
            attended, out_padded[layer], spread,
        )
        hidden_grad = reduce(partial, SLOT, 3)
        gain_a_grad = jnp.sum(hidden_grad * normed_a, axis=0)
        grad = middle_grad + norm_back(hidden_grad * gains[0], normed_a, inverse_a)
        gathered.append((totals, dense_b, dense_a))
        small_grads[layer] = jnp.concatenate(
            [
                jnp.roll(router_grad[:experts], owner * per_owner, axis=0),
                gain_a_grad[None],
                gain_b_grad[None],
            ],
            axis=0,
        )
    reduced = []
    last = None
    for totals, _, _ in gathered:
        if last is not None:
            totals, last = lax.optimization_barrier((totals, last))
        last = lax.psum_scatter(totals, "dp", scatter_dimension=0, tiled=True)
        reduced.append(last[0])
    dense = jnp.concatenate([piece for item in gathered for piece in item[1:]], axis=1)
    dense, last = lax.optimization_barrier((dense, last))
    dense = lax.psum_scatter(dense, ("dp", "expert"), scatter_dimension=0, tiled=True)[0]
    first_rows = gathered[0][1].shape[1]
    layer_rows = first_rows + gathered[0][2].shape[1]
    reduced = [
        (reduced[i], dense[i * layer_rows :][:first_rows], dense[i * layer_rows + first_rows :][: layer_rows - first_rows])
        for i in reversed(range(LAYERS))
    ]
    small_all = lax.psum(jnp.stack(small_grads, axis=0), ("dp", "expert", "wshard"))
    small_own = lax.dynamic_slice_in_dim(small_all, shard * chunk, chunk, axis=2)
    turned = jnp.stack(
        [
            jnp.concatenate([dense_a[: 3 * chunk], dense_b[: dense_b.shape[0] - units]], axis=0)
            for _, dense_b, dense_a in reduced
        ],
        axis=0,
    )
    turned = lax.ppermute(turned, ("dp", "wshard"), transposed).astype(f32)
    totals = jnp.stack([item[0] for item in reduced], axis=0)
    qkv_grad = turned[:, : 3 * chunk, :sub].reshape(LAYERS, 3, chunk, sub)
    part = units // owners
    size = min(part, 128)
    up_grad = turned[:, 3 * chunk :, :size].reshape(LAYERS, 2, part // size, chunk, size)
    up_grad = up_grad.transpose(0, 1, 3, 2, 4).reshape(LAYERS, 2, chunk, part)
    out_grad = jnp.stack([item[2][3 * chunk :, :side] for item in reduced], axis=0)
    down_grad = jnp.stack([item[1][item[1].shape[0] - units :, :side] for item in reduced], axis=0)
    return (
        block_out,
        grad.astype(bf16)[None],
        qkv_grad,
        out_grad.astype(f32),
        up_grad,
        down_grad.astype(f32),
        small_own[:, :experts].transpose(0, 2, 1),
        small_own[:, experts:],
        totals[:, :, :2].astype(f32),
        totals[:, :, 2].transpose(0, 1, 3, 2).astype(f32),
    )


def solution(mesh):
    in_specs = (
        P(("dp", "expert"), "wshard", None),
        P(("dp", "expert")),
        P(("dp", "expert"), "wshard", None),
        P(("dp", "expert"), "wshard"),
        P(("dp", "expert"), "wshard", None),
        P(None, None, "wshard", None),
        P(None, "wshard", None),
        P(None, None, "wshard", None),
        P(None, "wshard", None),
        P(None, "wshard", None),
        P(None, None, "wshard"),
        P(None, "expert", None, None, "wshard"),
        P(None, "expert", "wshard", None),
    )
    out_specs = (
        P(("dp", "expert"), "wshard", None),
        P(("dp", "expert"), "wshard", None),
        P(None, None, "wshard", ("dp", "expert")),
        P(None, "wshard", ("dp", "expert")),
        P(None, None, "wshard", ("dp", "expert")),
        P(None, "wshard", ("dp", "expert")),
        P(None, "wshard", None),
        P(None, None, "wshard"),
        P(None, "expert", None, "dp", "wshard"),
        P(None, "expert", "wshard", "dp"),
    )
    return jax.shard_map(
        per_device, mesh=mesh, in_specs=in_specs, out_specs=out_specs, check_vma=False
    )
```

time: 2260 us -> 708 us (0.31)
  local copies, waits for them, and re-layouts: 1290 us -> 68.6 us
  waiting for transfers between devices: 552 us -> 146 us
  Pallas kernels: 0 us -> 377 us
  matrix products: 126 us -> 0 us
  blocking collectives: 151 us -> 53.3 us
  other arithmetic: 64.5 us -> 30.6 us
    unnamed x393 -> x83, local copies, waits for them, and re-layouts: 1130 us -> 20.2 us
    pallas_call x0 -> x27, Pallas kernels: none -> 377 us  [the longest x10 146 us: call(): pl.pallas_call(kernel, out_shape=tuple((jax.ShapeDtypeStruct(s, d) for s,...]
    unnamed x28 -> x3, waiting for transfers between devices: 347 us -> 0.05 us
    dot_general x54 -> x0, matrix products: 126 us -> none  [the longest x2 11.9 us: per_device(): jnp.einsum('stf,sdf->td', shared_inner_grad, up_full[layer], preferred_el...]
    all_to_all x7 -> x2, waiting for transfers between devices: 96.2 us -> 0.01 us  [the longest x1 0.01 us: per_device(): lax.all_to_all(project, 'wshard', split_axis=0, concat_axis=0, tiled=True)]
    reduce_scatter x4 -> x3, waiting for transfers between devices: 24.6 us -> 116 us  [the longest x1 88.6 us: per_device(): lax.psum_scatter(dense, ('dp', 'expert'), scatter_dimension=0, tiled=True)]
    all_gather x4 -> x0, waiting for transfers between devices: 84.5 us -> none  [the longest x1 44 us: per_device(): lax.all_gather(shared_down, 'wshard', axis=1, tiled=True)]
    all_gather x6 -> x1, blocking collectives: 84.2 us -> 7.5 us  [per_device(): small = lax.all_gather(small, 'wshard', axis=2, tiled=True)]
  transfers between devices with their start and end apart: 25 -> 6, of which waited for: 12 -> 3; matrix products, arithmetic and copies ran while one was open for 56% -> 10% of each run, Pallas kernels for 0% -> 36%
where the time goes in v1:
time: 708 us; the launch traced here: 705 us
  Pallas kernels  377 us (53%)
  waiting for transfers between devices  146 us (21%)
  local copies, waits for them, and re-layouts  68.6 us (10%)
  blocking collectives  53.3 us (8%)
  other arithmetic  30.6 us (4%)
  between operations  15.5 us (2%)
  starting transfers between devices  13.9 us (2%)
    pallas_call x10, Pallas kernels, call(): pl.pallas_call(kernel, out_shape=tuple((jax.ShapeDtypeStruct(s, d) for s,...  146 us
    pallas_call x9, Pallas kernels, gather(): pl.pallas_call(functools.partial(gather_kernel, axes), out_shape=jax.Shap...  141 us
    pallas_call x8, Pallas kernels, reduce(): pl.pallas_call(functools.partial(reduce_kernel, axes), out_shape=jax.Shap...  89.5 us
    reduce_scatter x1, waiting for transfers between devices, per_device(): lax.psum_scatter(dense, ('dp', 'expert'), scatter_dimension=0, tiled=True)  88.6 us
    psum x1, blocking collectives, per_device(): lax.psum(jnp.stack(small_grads, axis=0), ('dp', 'expert', 'wshard'))  45.8 us
    ppermute x1, waiting for transfers between devices, per_device(): turned = lax.ppermute(turned, ('dp', 'wshard'), transposed).astype(f32)  29.9 us
    reduce_scatter x2, waiting for transfers between devices, per_device(): last = lax.psum_scatter(totals, 'dp', scatter_dimension=0, tiled=True)  27.8 us
    unnamed x83, local copies, waits for them, and re-layouts  20.2 us
  transfers between devices with their start and end apart: 6, of which 3 were waited for; matrix products, arithmetic and copies ran while one was open for 10% of the time, Pallas kernels for 36%

profile of v1, /device:TPU:4, one launch (start us, length us, event | category | flops | bytes accessed | tf_op | source)
XLA Modules:
  0.0 704.8 jit_solution(1904290081205050650)
XLA Ops:
  18.3 24.2 %shard_map.208 = s32[64,128]{1,0:T(8,128)S(1)} custom-call(s32[8,128]{1,0:T(8,128)S(1)} %concatenate.31.x_ref), custom_call_target="tpu_custom_call" | custom-call | tf_op jit(solution)/shard_map/pallas_call | solution.py:518
  65.4 9.7 %slice_reduce_fusion = (f32[768]{0:T(1024)S(1)}, f32[768]{0:T(1024)}, f32[768]{0:T(1024)}, f32[768]{0:T(1024)S(1)}) fusion(f32[2,2,768]{1,0,2:T(2,128)S(1)} %slice_convert_fusion.1), kind=kLoop, calls=%fused_computation.42 | loop fusion | bytes 24576 | tf_op jit(solution)/shard_map/slice | solution.py:693
  88.1 38.0 %shard_map.204.hidden = bf16[512,768]{1,0:T(8,128)(2,1)S(1)} custom-call(bf16[128,768]{1,0:T(8,128)(2,1)S(1)} %fusion.5.x_ref), custom_call_target="tpu_custom_call" | custom-call | tf_op jit(solution)/shard_map/pallas_call | solution.py:518
  160.9 14.6 %shard_map.207.mixed = bf16[1024,768]{1,0:T(8,128)(2,1)S(1)} custom-call(bf16[128,768]{1,0:T(8,128)(2,1)S(1)} %multiply_convert_fusion.2.x_ref), custom_call_target="tpu_custom_call" | custom-call | tf_op jit(solution)/shard_map/pallas_call | solution.py:518
  179.5 20.4 %shard_map.209 = (bf16[1024,768]{1,0:T(8,128)(2,1)}, bf16[2,640,768]{2,1,0:T(8,128)(2,1)}, bf16[2,640,1024]{2,1,0:T(8,128)(2,1)}, f32[2,640,1]{2,1,0:T(8,128)}, ...) custom-call(bf16[1024,768]{1,0:T(8,128)(2,1)} %copy-done, bf16[8,160,128]{2,1,0:T(8,128)(2,1)} %fusion.select, ...), custom_call_target="tpu_custom_call" | custom-call | tf_op jit(solution)/shard_map/pallas_call | solution.py:45
  201.3 13.9 %shard_map.210 = f32[128,768]{1,0:T(8,128)S(1)} custom-call(bf16[1024,768]{1,0:T(8,128)(2,1)S(1)} %copy-done.11), custom_call_target="tpu_custom_call" | custom-call | tf_op jit(solution)/shard_map/pallas_call | solution.py:565
  233.3 8.7 %shard_map.213 = f32[128,768]{1,0:T(8,128)S(1)} custom-call(bf16[512,768]{1,0:T(8,128)(2,1)S(1)} %copy-done.14), custom_call_target="tpu_custom_call" | custom-call | tf_op jit(solution)/shard_map/pallas_call | solution.py:565
  242.2 13.1 %shard_map.214.mixed = bf16[1024,768]{1,0:T(8,128)(2,1)S(1)} custom-call(bf16[128,768]{1,0:T(8,128)(2,1)S(1)} %multiply_convert_fusion.x_ref), custom_call_target="tpu_custom_call" | custom-call | tf_op jit(solution)/shard_map/pallas_call | solution.py:518
  256.5 13.7 %shard_map.217.grad = bf16[1024,768]{1,0:T(8,128)(2,1)S(1)} custom-call(bf16[128,768]{1,0:T(8,128)(2,1)S(1)} %get-tuple-element.224.x_ref), custom_call_target="tpu_custom_call" | custom-call | tf_op jit(solution)/shard_map/pallas_call | solution.py:518
  271.3 20.3 %shard_map.215 = (bf16[1024,768]{1,0:T(8,128)(2,1)}, bf16[2,640,768]{2,1,0:T(8,128)(2,1)}, bf16[2,640,1024]{2,1,0:T(8,128)(2,1)}, f32[2,640,1]{2,1,0:T(8,128)}, ...) custom-call(bf16[1024,768]{1,0:T(8,128)(2,1)} %copy-done.1, bf16[8,160,128]{2,1,0:T(8,128)(2,1)} %fusion.select, ...), custom_call_target="tpu_custom_call" | custom-call | tf_op jit(solution)/shard_map/pallas_call | solution.py:45
  291.6 17.7 %shard_map.218 = (bf16[4,2,3,192,512]{4,3,2,1,0:T(8,128)(2,1)}, bf16[8,160,768]{2,1,0:T(8,128)(2,1)}, f32[8,160,128]{2,1,0:T(8,128)}) custom-call(bf16[1024,768]{1,0:T(8,128)(2,1)} %copy-done.2, bf16[8,160,128]{2,1,0:T(8,128)(2,1)} %fusion.select, bf16[2,2,768,512]{3,2,1,0:T(8,128)(2,1)} %get-tuple-element.189.up, ...), custom_call_target="tpu_custom_call" | custom-call | tf_op jit(solution)/shard_map/pallas_call | solution.py:45
  310.7 13.9 %shard_map.216 = f32[128,768]{1,0:T(8,128)S(1)} custom-call(bf16[1024,768]{1,0:T(8,128)(2,1)S(1)} %copy-done.8), custom_call_target="tpu_custom_call" | custom-call | tf_op jit(solution)/shard_map/pallas_call | solution.py:565
  324.6 14.9 %shard_map.219 = (bf16[1024,768]{1,0:T(8,128)(2,1)}, bf16[8,1280,128]{2,1,0:T(8,128)(2,1)}, f32[128,768]{1,0:T(8,128)}) custom-call(bf16[1024,768]{1,0:T(8,128)(2,1)} %copy-done.2, bf16[1024,768]{1,0:T(8,128)(2,1)} %copy-done.1, bf16[8,128,160]{2,1,0:T(8,128)(2,1)} %compare_convert_fusion.back, bf16[128,768]{1,0:T(8,128)(2,1)} %get-tuple-element.218.router, ...), custom_call_target="tpu_custom_call" | custom-call | tf_op jit(solution)/shard_map/pallas_call | solution.py:45
  340.9 13.9 %shard_map.220 = f32[128,768]{1,0:T(8,128)S(1)} custom-call(bf16[1024,768]{1,0:T(8,128)(2,1)S(1)} %copy-done.10), custom_call_target="tpu_custom_call" | custom-call | tf_op jit(solution)/shard_map/pallas_call | solution.py:565
  364.3 12.2 %shard_map.222 = (bf16[512,768]{1,0:T(8,128)(2,1)}, bf16[8,768,128]{2,1,0:T(8,128)(2,1)}) custom-call(bf16[512,768]{1,0:T(8,128)(2,1)} %copy-done.7, bf16[512,768]{1,0:T(8,128)(2,1)} %copy-done.5, bf16[3,768,256]{2,1,0:T(8,128)(2,1)} %bitcast.138, f32[512,256]{1,0:T(8,128)} %get-tuple-element.221.cosine, f32[512,256]{1,0:T(8,128)} %get-tuple-element.220.sine, ...), custom_call_target="tpu_custom_call" | custom-call | tf_op jit(solution)/shard_map/pallas_call | solution.py:45
  387.4 13.2 %shard_map.224.grad = bf16[1024,768]{1,0:T(8,128)(2,1)S(1)} custom-call(bf16[128,768]{1,0:T(8,128)(2,1)S(1)} %get-tuple-element.181.x_ref), custom_call_target="tpu_custom_call" | custom-call | tf_op jit(solution)/shard_map/pallas_call | solution.py:518
  401.8 18.0 %shard_map.225 = (bf16[4,2,3,192,512]{4,3,2,1,0:T(8,128)(2,1)}, bf16[8,160,768]{2,1,0:T(8,128)(2,1)}, f32[8,160,128]{2,1,0:T(8,128)}) custom-call(bf16[1024,768]{1,0:T(8,128)(2,1)} %copy-done.3, bf16[8,160,128]{2,1,0:T(8,128)(2,1)} %fusion.select, bf16[2,2,768,512]{3,2,1,0:T(8,128)(2,1)} %get-tuple-element.190.up, ...), custom_call_target="tpu_custom_call" | custom-call | tf_op jit(solution)/shard_map/pallas_call | solution.py:45
  419.9 15.0 %shard_map.226 = (bf16[1024,768]{1,0:T(8,128)(2,1)}, bf16[8,1280,128]{2,1,0:T(8,128)(2,1)}, f32[128,768]{1,0:T(8,128)}) custom-call(bf16[1024,768]{1,0:T(8,128)(2,1)} %copy-done.3, bf16[1024,768]{1,0:T(8,128)(2,1)} %copy-done, bf16[8,128,160]{2,1,0:T(8,128)(2,1)} %compare_convert_fusion.back, bf16[128,768]{1,0:T(8,128)(2,1)} %get-tuple-element.219.router, ...), custom_call_target="tpu_custom_call" | custom-call | tf_op jit(solution)/shard_map/pallas_call | solution.py:45
  436.3 13.9 %shard_map.227 = f32[128,768]{1,0:T(8,128)S(1)} custom-call(bf16[1024,768]{1,0:T(8,128)(2,1)S(1)} %copy-done.9), custom_call_target="tpu_custom_call" | custom-call | tf_op jit(solution)/shard_map/pallas_call | solution.py:565
  459.6 12.2 %shard_map.229 = (bf16[512,768]{1,0:T(8,128)(2,1)}, bf16[8,768,128]{2,1,0:T(8,128)(2,1)}) custom-call(bf16[512,768]{1,0:T(8,128)(2,1)} %copy-done.6, bf16[512,768]{1,0:T(8,128)(2,1)} %copy-done.4, bf16[3,768,256]{2,1,0:T(8,128)(2,1)} %bitcast.136, f32[512,256]{1,0:T(8,128)} %get-tuple-element.221.cosine, f32[512,256]{1,0:T(8,128)} %get-tuple-element.220.sine, ...), custom_call_target="tpu_custom_call" | custom-call | tf_op jit(solution)/shard_map/pallas_call | solution.py:45
  478.2 27.8 %reduce-scatter.6.cloned.1.call-done = bf16[1,2,3,192,512]{4,3,2,1,0:T(8,128)(2,1)} async-done(((bf16[4,2,3,192,512]{4,3,2,1,0:T(8,128)(2,1)}), bf16[1,2,3,192,512]{4,3,2,1,0:T(8,128)(2,1)}) %reduce-scatter.6.cloned.1.call-update) | async-done | bytes 1179664 | tf_op jit(solution)/shard_map/reduce_scatter | solution.py:745
  515.9 45.8 %psum.7 = f32[2,6,768]{2,1,0:T(8,128)S(1)} all-reduce(f32[2,6,768]{2,1,0:T(8,128)S(1)} %pad_maximum_fusion.4), channel_id=1, replica_groups=mesh['dp'=4,'expert'=2,'wshard'=4] {'dp','expert','wshard'}, use_global_device_ids=true, to_apply=%region_16.18 | all-reduce | flops 9216 | bytes 73728 | tf_op jit(solution)/shard_map/psum | solution.py:756
  570.1 88.6 %reduce-scatter.8.cloned.1.call-done = bf16[1,4096,128]{2,1,0:T(8,128)(2,1)} async-done(((bf16[8,4096,128]{2,1,0:T(8,128)(2,1)}), bf16[1,4096,128]{2,1,0:T(8,128)(2,1)}) %reduce-scatter.8.cloned.1.call-update) | async-done | bytes 1048592 | tf_op jit(solution)/shard_map/reduce_scatter | solution.py:749
  666.3 29.9 %collective-permute-done = bf16[2,1344,128]{2,1,0:T(8,128)(2,1)S(1)} collective-permute-done((bf16[2,1344,128]{2,1,0:T(8,128)(2,1)S(1)}, bf16[2,1344,128]{2,1,0:T(8,128)(2,1)S(1)}, u32[]{:S(2)}, u32[]{:S(2)}) %collective-permute-start) | collective-permute-done | bytes 688160 | tf_op jit(solution)/shard_map/ppermute | solution.py:765
  (208 shorter events, 176.1 us)
Async XLA Ops:
  10.7 33.4 %copy-start.18 = (bf16[1,128,768]{2,1,0:T(8,128)(2,1)S(1)}, bf16[1,128,768]{2,1,0:T(8,128)(2,1)}, u32[]{:S(2)}) copy-start(bf16[1,128,768]{2,1,0:T(8,128)(2,1)} %param.17) | copy-start | bytes 589828
  10.7 34.2 %copy-start.32 = (bf16[2,192,4]{1,2,0:T(4,128)(2,1)S(1)}, bf16[2,192,4]{1,2,0:T(4,128)(2,1)}, u32[]{:S(2)}) copy-start(bf16[2,192,4]{1,2,0:T(4,128)(2,1)} %param.26) | copy-start | bytes 9220
  10.7 34.4 %copy-start.33 = (bf16[2,2,192]{2,1,0:T(2,128)(2,1)S(1)}, bf16[2,2,192]{2,1,0:T(2,128)(2,1)}, u32[]{:S(2)}) copy-start(bf16[2,2,192]{2,1,0:T(2,128)(2,1)} %param.27) | copy-start | bytes 4612
  10.7 69.5 %all-to-all-start = ((bf16[4,2,3,192,256]{4,3,2,1,0:T(8,128)(2,1)}), bf16[4,2,3,192,256]{4,3,2,1,0:T(8,128)(2,1)}, u32[]{:S(2)}, u32[]{:S(2)}) async-start(bf16[4,2,3,192,256]{4,3,2,1,0:T(8,128)(2,1)} %pad_maximum_fusion.1), calls=%async_computation | async-start | bytes 4718592 | tf_op jit(solution)/shard_map/all_to_all | solution.py:649
  62.8 12.5 %copy-start.29 = (f32[512]{0:T(512)S(1)}, f32[512]{0:T(512)}, u32[]{:S(2)}) copy-start(f32[512]{0:T(512)} %iota_convert_fusion) | copy-start | bytes 6148
  62.8 12.5 %copy-start.34 = (f32[256]{0:T(256)S(1)}, f32[256]{0:T(256)}, u32[]{:S(2)}) copy-start(f32[256]{0:T(256)} %fusion.30) | copy-start | bytes 3076
  62.8 12.5 %copy-start.36 = (pred[256]{0:T(512)(128)(4,1)S(1)}, pred[256]{0:T(512)(128)(4,1)}, u32[]{:S(2)}) copy-start(pred[256]{0:T(512)(128)(4,1)} %fusion.31) | copy-start | bytes 772
  63.9 15.4 %copy-start.30 = (f32[128]{0:T(128)}, f32[128]{0:T(128)S(1)}, u32[]{:S(2)}) copy-start(f32[128]{0:T(128)S(1)} %add_rsqrt_fusion.3) | copy-start | bytes 1540
  65.4 13.9 %copy-start.19 = (s32[8,128,160]{2,1,0:T(8,128)S(1)}, s32[8,128,160]{2,1,0:T(8,128)}, u32[]{:S(2)}) copy-start(s32[8,128,160]{2,1,0:T(8,128)} %copy.79) | copy-start | bytes 1966084
  65.4 13.9 %copy-start.28 = (s32[160]{0:T(256)S(1)}, s32[160]{0:T(256)}, u32[]{:S(2)}) copy-start(s32[160]{0:T(256)} %eq.163) | copy-start | bytes 1924
  80.2 96.5 %all-to-all-start.1 = ((bf16[4,2,2,192,512]{4,3,2,1,0:T(8,128)(2,1)}), bf16[4,2,2,192,512]{4,3,2,1,0:T(8,128)(2,1)S(1)}, u32[]{:S(2)}, u32[]{:S(2)}) async-start(bf16[4,2,2,192,512]{4,3,2,1,0:T(8,128)(2,1)} %copy.81), calls=%async_computation.1 | async-start | bytes 6291456 | tf_op jit(solution)/shard_map/all_to_all | solution.py:652
  85.5 334.3 %reduce-scatter.4.cloned.1.call-start = ((), (), s32[]{:S(2)}) async-start(), calls=%async_computation.5 | async-start | bytes 5898240 | tf_op jit(solution)/shard_map/reduce_scatter | solution.py:745
  86.0 42.8 %copy-start.24 = (bf16[2,512,768]{2,1,0:T(8,128)(2,1)S(1)}, bf16[2,512,768]{2,1,0:T(8,128)(2,1)}, u32[]{:S(2)}) copy-start(bf16[2,512,768]{2,1,0:T(8,128)(2,1)} %param.25) | copy-start | bytes 4718596
  88.1 41.9 %copy-start.21 = (bf16[2,2,512,768]{3,2,1,0:T(8,128)(2,1)S(1)}, bf16[2,2,512,768]{3,2,1,0:T(8,128)(2,1)}, u32[]{:S(2)}) copy-start(bf16[2,2,512,768]{3,2,1,0:T(8,128)(2,1)} %param.29) | copy-start | bytes 9437188
  142.5 18.4 %copy-start.26 = (f32[768]{0:T(1024)S(1)}, f32[768]{0:T(1024)}, u32[]{:S(2)}) copy-start(f32[768]{0:T(1024)} %get-tuple-element.175) | copy-start | bytes 9220
  179.5 35.7 %copy-start.17 = (f32[128,768]{1,0:T(8,128)S(1)}, f32[128,768]{1,0:T(8,128)}, u32[]{:S(2)}) copy-start(f32[128,768]{1,0:T(8,128)} %copy-done.16) | copy-start | bytes 1179652
  201.3 14.1 %copy-start.27 = (f32[768]{0:T(1024)S(1)}, f32[768]{0:T(1024)}, u32[]{:S(2)}) copy-start(f32[768]{0:T(1024)} %get-tuple-element.174) | copy-start | bytes 9220
  224.4 17.5 %copy-start.25 = (bf16[1,128,768]{2,1,0:T(8,128)(2,1)S(1)}, bf16[1,128,768]{2,1,0:T(8,128)(2,1)}, u32[]{:S(2)}) copy-start(bf16[1,128,768]{2,1,0:T(8,128)(2,1)} %param.21) | copy-start | bytes 589828
  224.4 17.5 %copy-start.37 = (f32[128]{0:T(128)S(1)}, f32[128]{0:T(128)}, u32[]{:S(2)}) copy-start(f32[128]{0:T(128)} %compare_convert_fusion.1) | copy-start | bytes 1540
  309.3 196.6 %reduce-scatter.6.cloned.1.call-start = ((), (), s32[]{:S(2)}) async-start(), calls=%async_computation.6 | async-start | bytes 5898240 | tf_op jit(solution)/shard_map/reduce_scatter | solution.py:745
  419.8 238.8 %reduce-scatter.8.cloned.1.call-start = ((), (), s32[]{:S(2)}) async-start(), calls=%async_computation.7 | async-start | bytes 9437184 | tf_op jit(solution)/shard_map/reduce_scatter | solution.py:749
  478.2 29.3 %copy-start.12 = (bf16[512,768]{1,0:T(8,128)(2,1)S(1)}, bf16[512,768]{1,0:T(8,128)(2,1)}, u32[]{:S(2)}) copy-start(bf16[512,768]{1,0:T(8,128)(2,1)} %get-tuple-element.96.p_ref) | copy-start | bytes 2359300
  478.2 37.3 %copy-start.31 = (f32[128]{0:T(128)S(1)}, f32[128]{0:T(128)}, u32[]{:S(2)}) copy-start(f32[128]{0:T(128)} %copy-done.30) | copy-start | bytes 1540
  661.1 35.1 %collective-permute-start = (bf16[2,1344,128]{2,1,0:T(8,128)(2,1)S(1)}, bf16[2,1344,128]{2,1,0:T(8,128)(2,1)S(1)}, u32[]{:S(2)}, u32[]{:S(2)}) collective-permute-start(bf16[2,1344,128]{2,1,0:T(8,128)(2,1)S(1)} %pad_maximum_fusion.2), channel_id=1, source_target_pairs={{0,0},{1,8},{2,16},{3,24},{8,1},{9,9},{10,17},{11,25},{16,2},{17,1... | collective-permute-start | bytes 2064392 | tf_op jit(solution)/shard_map/ppermute | solution.py:765
  (21 other events, 48.9 us)
Sparse Core Ops, SparseCore 0:
  309.4 85.9 reduce-scatter.3
  419.9 85.9 reduce-scatter.5
  509.6 149.0 reduce-scatter.7

commit v2 on v1

--- a/solution.py
+++ b/solution.py
@@ -40,17 +40,61 @@
     return pl.ds(pl.multiple_of(index * size, size), size)
 
 
-def call(kernel, outs, scratch, *operands, cost=None):
+class Far:
+    def __init__(self, value):
+        self.value = value
+
+
+def call(kernel, outs, scratch, *operands):
     vmem = pl.BlockSpec(memory_space=pltpu.VMEM)
+    far = pl.BlockSpec(memory_space=pl.ANY)
     return pl.pallas_call(
         kernel,
         out_shape=tuple(jax.ShapeDtypeStruct(s, d) for s, d in outs),
-        in_specs=[vmem] * len(operands),
+        in_specs=[far if isinstance(o, Far) else vmem for o in operands],
         out_specs=tuple([vmem] * len(outs)),
-        scratch_shapes=[pltpu.VMEM(s, d) for s, d in scratch],
+        scratch_shapes=[pltpu.VMEM(*s) if isinstance(s, tuple) else s for s in scratch],
         compiler_params=pltpu.CompilerParams(vmem_limit_bytes=VMEM_LIMIT),
-        cost_estimate=cost,
-    )(*operands)
+    )(*[o.value if isinstance(o, Far) else o for o in operands])
+
+
+def fetch(pairs, sems):
+    copies = [pltpu.make_async_copy(a, b, sems.at[n]) for n, (a, b) in enumerate(pairs)]
+    for copy in copies:
+        copy.start()
+    return copies
+
+
+def settle_all(copies):
+    for copy in copies:
+        copy.wait()
+
+
+DMA = pltpu.SemaphoreType.DMA
+
+
+def project_pairs(source, held):
+    if len(source.shape) == 3:
+        return [(source, held)]
+    shards, kinds, chunk, _ = source.shape
+    window = held.shape[2]
+    return [
+        (
+            source.at[a, kinds - 2 + part // 2, :, pl.ds(part % 2 * window, window)],
+            held.at[part, pl.ds(a * chunk, chunk), :],
+        )
+        for a in range(shards)
+        for part in range(3)
+    ]
+
+
+def wide_pairs(source, held):
+    shards, _, chunk, _ = source.shape
+    return [
+        (source.at[a, s], held.at[s, pl.ds(a * chunk, chunk), :])
+        for a in range(shards)
+        for s in range(2)
+    ]
 
 
 def swapped(values):
@@ -65,15 +109,20 @@
 
 
 def attend_kernel(
-    hidden, weight, cosine, sine, length, out_weight, partial, queries, keys, values, probs, attended
+    hidden, source, cosine, sine, length, out_weight, partial, queries, keys, values, probs, attended,
+    weight, sems,
 ):
     count = hidden.shape[0]
-    window = cosine.shape[1]
+    window = weight.shape[2]
     tile = count // 2
+    copies = fetch(project_pairs(source, weight), sems)
+    cosines = jnp.concatenate([cosine[...]] * (window // 128), axis=1)
+    sines = jnp.concatenate([sine[...]] * (window // 128), axis=1)
+    settle_all(copies)
     for part, ref in enumerate((queries, keys, values)):
         made = mul(hidden[...], weight[part])
         if part < 2:
-            made = made * cosine[...] + swapped(made) * sine[...]
+            made = made * cosines + swapped(made) * sines
         if part == 0:
             made = made * (HEAD_DIM ** (-0.5))
         ref[...] = made.astype(bf16)
@@ -94,31 +143,33 @@
     partial[...] = mul(attended[...], out_weight[...]).astype(bf16)
 
 
-def attend(hidden, weight, cosine, sine, length, out_weight):
+def attend(hidden, source, cosine, sine, length, out_weight):
     count, width = hidden.shape
-    window = cosine.shape[1]
+    window = out_weight.shape[0]
     heads = window // HEAD_DIM
     piece = ((count, window), bf16)
     return call(
         attend_kernel,
         [((count, width), bf16), piece, piece, piece, ((heads, count, count), bf16), piece],
-        [],
-        hidden, weight, cosine, sine, length, out_weight,
+        [((3, width, window), bf16), DMA((16,))],
+        hidden, Far(source), cosine, sine, length, out_weight,
     )
 
 
 def attend_back_kernel(
-    grad, hidden, weight, cosine, sine, queries, keys, values, probs, attended, out_weight, spread,
-    partial, dense, attended_grad, dq, dk, dv, made, lift,
+    grad, hidden, source, cosine, sine, queries, keys, values, probs, attended, out_weight, spread,
+    partial, dense, attended_grad, dq, dk, dv, made, lift, weight, sems,
 ):
     count, width = grad.shape
-    window = cosine.shape[1]
+    window = weight.shape[2]
     tile = count // 2
-    columns = dense.shape[0]
-    owners = spread.shape[1] // 128
-    planes = columns // owners
+    owners, planes = dense.shape[:2]
+    columns = owners * planes
     chunk = width // planes
     side = width // columns
+    copies = fetch(project_pairs(source, weight), sems)
+    cosines = jnp.concatenate([cosine[...]] * (window // 128), axis=1)
+    sines = jnp.concatenate([sine[...]] * (window // 128), axis=1)
     attended_grad[...] = mul_nt(grad[...], out_weight[...]).astype(bf16)
     for head in range(window // HEAD_DIM):
         lanes = slice(head * HEAD_DIM, (head + 1) * HEAD_DIM)
@@ -141,10 +192,11 @@
                 dk[0:seen, lanes] = dk[0:seen, lanes] + key_part
                 dv[0:seen, lanes] = dv[0:seen, lanes] + value_part
     back = dq[...] * (HEAD_DIM ** (-0.5))
-    made[0] = (back * cosine[...] - swapped(back) * sine[...]).astype(bf16)
+    made[0] = (back * cosines - swapped(back) * sines).astype(bf16)
     back = dk[...]
-    made[1] = (back * cosine[...] - swapped(back) * sine[...]).astype(bf16)
+    made[1] = (back * cosines - swapped(back) * sines).astype(bf16)
     made[2] = dv[...].astype(bf16)
+    settle_all(copies)
     total = mul_nt(made[0], weight[0])
     total = total + mul_nt(made[1], weight[1])
     total = total + mul_nt(made[2], weight[2])
@@ -154,25 +206,27 @@
         found = mul_tn(hidden[...], spaced)
         for a in range(planes):
             for b in range(owners):
-                dense[a * owners + b, part * chunk : (part + 1) * chunk, :] = found[
+                dense[b, a, part * chunk : (part + 1) * chunk, :] = found[
                     a * chunk : (a + 1) * chunk, b * 128 : (b + 1) * 128
                 ].astype(bf16)
     start = pl.multiple_of(lax.rem(lax.axis_index("wshard") * chunk, 128), 64)
     for j in range(columns):
         lift[:, 0:side] = mul_tn(attended[...], grad[:, j * side : (j + 1) * side])
-        dense[j, 3 * chunk : 4 * chunk, 0:side] = lift[pl.ds(start, chunk), 0:side].astype(bf16)
+        dense[j % owners, j // owners, 3 * chunk : 4 * chunk, 0:side] = lift[
+            pl.ds(start, chunk), 0:side
+        ].astype(bf16)
 
 
 def attend_back(
-    grad, hidden, weight, cosine, sine, queries, keys, values, probs, attended, out_weight, spread
+    grad, hidden, source, cosine, sine, queries, keys, values, probs, attended, out_weight, spread
 ):
     count, width = hidden.shape
-    window = cosine.shape[1]
+    window = out_weight.shape[0]
     owners = spread.shape[1] // 128
     planes = lax.axis_size("dp")
     return call(
         attend_back_kernel,
-        [((count, width), bf16), ((planes * owners, 4 * (width // planes), 128), bf16)],
+        [((count, width), bf16), ((owners, planes, 4 * (width // planes), 128), bf16)],
         [
             ((count, window), bf16),
             ((count, window), f32),
@@ -180,8 +234,11 @@
             ((count, window), f32),
             ((3, count, window), bf16),
             ((window, 128), f32),
+            ((3, width, window), bf16),
+            DMA((16,)),
         ],
-        grad, hidden, weight, cosine, sine, queries, keys, values, probs, attended, out_weight, spread,
+        grad, hidden, Far(source), cosine, sine, queries, keys, values, probs, attended, out_weight,
+        spread,
     )
 
 
@@ -189,17 +246,11 @@
     return lax.broadcasted_iota(jnp.int32, shape, len(shape) - 1)
 
 
-def expert_kernel(
-    mixed, select, back, chosen, router, up, down, wide, narrow,
-    partial, arrived, inner, scale, gates, shared_inner, sent, shared_out,
-):
+def route_part(mixed, select, chosen, router, arrived, scale, gates):
     group, _, rows = select.shape
-    per_owner, slots, width = arrived.shape
+    per_owner, slots, _ = arrived.shape
     capacity = slots // group
-    units = down.shape[1]
-    shards = lax.axis_size("wshard")
     owner = lax.axis_index("expert")
-    count = shared_out.shape[0]
 
     @pl.loop(0, group)
     def _(g):
@@ -211,15 +262,69 @@
         gates[rows_at(g, rows), :] = gate
         spots = mul_pair(select[g], gate)
         for j in range(per_owner):
-            arrived[j, rows_at(g, capacity), :] = found[j * capacity : (j + 1) * capacity]
-            scale[j, rows_at(g, capacity), :] = spots[j * capacity : (j + 1) * capacity, j : j + 1]
-
-    parts = 2
-    tile = slots // parts
+            here = slice(j * capacity, (j + 1) * capacity)
+            mine = first_lane((capacity, 128)) == owner * per_owner + j
+            arrived[j, rows_at(g, capacity), :] = found[here]
+            scale[j, rows_at(g, capacity), :] = jnp.sum(
+                jnp.where(mine, spots[here], 0.0), axis=-1, keepdims=True
+            )
+
+
+def glu(gate, lift):
+    return (gate / (1.0 + jnp.exp(-gate)) * lift).astype(bf16)
+
+
+def finish_part(mixed, back, wide, narrow, partial, sent, shared_out):
+    group, rows, _ = back.shape
+    shards = lax.axis_size("wshard")
+    owner = lax.axis_index("expert")
+    count = shared_out.shape[0]
+    piece = count // 2
+
+    @pl.loop(0, 2)
+    def _(i):
+        block = mixed[rows_at(owner * 2 + i, piece), :]
+        act = glu(mul(block, wide[0]), mul(block, wide[1]))
+        shared_out[rows_at(i, piece), :] = mul(act, narrow[...])
+
+    @pl.loop(0, group)
+    def _(g):
+        near = jnp.clip(g - owner * shards, 0, shards - 1)
+        here = (lax.div(g, shards) == owner).astype(f32)
+        made = mul(back[g], sent[g]) + here * shared_out[rows_at(near, rows), :]
+        partial[rows_at(g, rows), :] = made.astype(bf16)
+
+
+def send_rows(sent, made, i, j, group, parts, capacity):
+    for q in range(group // parts):
+        sent[i * (group // parts) + q, j * capacity : (j + 1) * capacity, :] = made[
+            q * capacity : (q + 1) * capacity
+        ]
+
+
+PARTS = 2
+
+
+def expert_kernel(
+    layer, mixed, select, back, chosen, router, far_up, far_down, far_wide, far_narrow,
+    partial, arrived, inner, scale, gates,
+    sent, shared_out, up, down, wide, narrow, sems, wide_sems,
+):
+    group = select.shape[0]
+    per_owner, slots, width = arrived.shape
+    capacity = slots // group
+    units = down.shape[1]
+    copies = fetch(
+        [(far_up.at[layer], up), (far_down.at[layer], down), (far_narrow.at[layer], narrow)], sems
+    )
+    more = fetch(wide_pairs(far_wide, wide), wide_sems)
+    route_part(mixed, select, chosen, router, arrived, scale, gates)
+    settle_all(copies)
+    tile = slots // PARTS
 
     for j in range(per_owner):
 
-        @pl.loop(0, parts)
+        @pl.loop(0, PARTS)
         def _(i):
             own = rows_at(i, tile)
             block = arrived[j, own, :]
@@ -227,52 +332,127 @@
             lift = mul(block, up[j, 1])
             inner[j, own, 0:units] = gate.astype(bf16)
             inner[j, own, units : 2 * units] = lift.astype(bf16)
-            act = (gate / (1.0 + jnp.exp(-gate)) * lift).astype(bf16)
-            made = (mul(act, down[j]) * scale[j, own, :]).astype(bf16)
-            for q in range(group // parts):
-                sent[i * (group // parts) + q, j * capacity : (j + 1) * capacity, :] = made[
-                    q * capacity : (q + 1) * capacity
-                ]
-
-    piece = count // 2
-
-    @pl.loop(0, 2)
-    def _(i):
-        own = rows_at(i, piece)
-        block = mixed[rows_at(owner * 2 + i, piece), :]
-        gate = mul(block, wide[0])
-        lift = mul(block, wide[1])
-        shared_inner[own, 0:units] = gate.astype(bf16)
-        shared_inner[own, units : 2 * units] = lift.astype(bf16)
-        act = (gate / (1.0 + jnp.exp(-gate)) * lift).astype(bf16)
-        shared_out[own, :] = mul(act, narrow[...])
-
-    @pl.loop(0, group)
-    def _(g):
-        near = jnp.clip(g - owner * shards, 0, shards - 1)
-        here = (lax.div(g, shards) == owner).astype(f32)
-        made = mul(back[g], sent[g]) + here * shared_out[rows_at(near, rows), :]
-        partial[rows_at(g, rows), :] = made.astype(bf16)
-
-
-def expert(mixed, select, back, chosen, router, up, down, wide, narrow):
+            made = (mul(glu(gate, lift), down[j]) * scale[j, own, :]).astype(bf16)
+            send_rows(sent, made, i, j, group, PARTS, capacity)
+
+    settle_all(more)
+    finish_part(mixed, back, wide, narrow, partial, sent, shared_out)
+
+
+def expert(layer, mixed, select, back, chosen, router, up, down, wide, narrow):
     group, spots, rows = select.shape
-    per_owner, _, width, units = up.shape
+    _, per_owner, _, width, units = up.shape
     slots = group * spots // per_owner
     count = rows * lax.axis_size("wshard")
     return call(
-        expert_kernel,
+        functools.partial(expert_kernel, layer),
         [
             (mixed.shape, bf16),
             ((per_owner, slots, width), bf16),
             ((per_owner, slots, 2 * units), bf16),
             ((per_owner, slots, 1), f32),
             ((group * rows, 128), f32),
-            ((count, 2 * units), bf16),
         ],
-        [((group, spots, width), bf16), ((count, width), f32)],
-        mixed, select, back, chosen, router, up, down, wide, narrow,
-    )
+        [
+            ((group, spots, width), bf16),
+            ((count, width), f32),
+            (up.shape[1:], bf16),
+            (down.shape[1:], bf16),
+            ((2, width, units), bf16),
+            (narrow.shape[1:], bf16),
+            DMA((3,)),
+            DMA((8,)),
+        ],
+        mixed, select, back, chosen, router, Far(up), Far(down), Far(wide), Far(narrow),
+    )
+
+
+def route_kernel(
+    layer, mixed, select, chosen, router, far_up,
+    arrived, inner, scale, gates,
+    up, sems,
+):
+    per_owner, slots, _ = arrived.shape
+    units = up.shape[3]
+    copies = fetch([(far_up.at[layer], up)], sems)
+    route_part(mixed, select, chosen, router, arrived, scale, gates)
+    settle_all(copies)
+    tile = slots // PARTS
+
+    for j in range(per_owner):
+
+        @pl.loop(0, PARTS)
+        def _(i):
+            own = rows_at(i, tile)
+            block = arrived[j, own, :]
+            inner[j, own, 0:units] = mul(block, up[j, 0]).astype(bf16)
+            inner[j, own, units : 2 * units] = mul(block, up[j, 1]).astype(bf16)
+
+
+def route(layer, mixed, select, chosen, router, up):
+    group, spots, rows = select.shape
+    _, per_owner, _, width, units = up.shape
+    slots = group * spots // per_owner
+    return call(
+        functools.partial(route_kernel, layer),
+        [
+            ((per_owner, slots, width), bf16),
+            ((per_owner, slots, 2 * units), bf16),
+            ((per_owner, slots, 1), f32),
+            ((group * rows, 128), f32),
+        ],
+        [(up.shape[1:], bf16), DMA((1,))],
+        mixed, select, chosen, router, Far(up),
+    )
+
+
+def finish_kernel(
+    layer, mixed, back, inner, scale, far_down, far_wide, far_narrow, after,
+    partial,
+    sent, shared_out, down, wide, narrow, sems, wide_sems,
+):
+    group = back.shape[0]
+    per_owner, slots, _ = inner.shape
+    capacity = slots // group
+    units = down.shape[1]
+    copies = fetch([(far_down.at[layer], down), (far_narrow.at[layer], narrow)], sems)
+    more = fetch(wide_pairs(far_wide, wide), wide_sems)
+    settle_all(copies)
+    tile = slots // PARTS
+
+    for j in range(per_owner):
+
+        @pl.loop(0, PARTS)
+        def _(i):
+            own = rows_at(i, tile)
+            gate = inner[j, own, 0:units].astype(f32)
+            lift = inner[j, own, units : 2 * units].astype(f32)
+            made = (mul(glu(gate, lift), down[j]) * scale[j, own, :]).astype(bf16)
+            send_rows(sent, made, i, j, group, PARTS, capacity)
+
+    settle_all(more)
+    finish_part(mixed, back, wide, narrow, partial, sent, shared_out)
+
+
+def finish(layer, mixed, back, inner, scale, down, wide, narrow, after):
+    group, rows, spots = back.shape
+    width = mixed.shape[1]
+    units = down.shape[2]
+    count = rows * lax.axis_size("wshard")
+    return call(
+        functools.partial(finish_kernel, layer),
+        [(mixed.shape, bf16)],
+        [
+            ((group, spots, width), bf16),
+            ((count, width), f32),
+            (down.shape[1:], bf16),
+            ((2, width, units), bf16),
+            (narrow.shape[1:], bf16),
+            DMA((2,)),
+            DMA((8,)),
+        ],
+        mixed, back, inner, scale, Far(down), Far(wide), Far(narrow), Far(after),
+    )[0]
 
 
 def silu_back(grad, gate, lift):
@@ -285,9 +465,9 @@
 
 
 def routed_back_kernel(
-    grad, select, up, down, arrived, inner, scale,
+    layer, grad, select, far_up, far_down, arrived, inner, scale,
     totals, sent, spot,
-    picked, deep,
+    picked, deep, up, down, sems,
 ):
     group, spots, rows = select.shape
     per_owner, slots, width = arrived.shape
@@ -295,6 +475,8 @@
     units = down.shape[1]
     planes = totals.shape[0]
     chunk = width // planes
+    owner = lax.axis_index("expert")
+    copies = fetch([(far_down.at[layer], down), (far_up.at[layer], up)], sems)
 
     @pl.loop(0, group)
     def _(g):
@@ -302,12 +484,12 @@
         for j in range(per_owner):
             picked[j, rows_at(g, capacity), :] = found[j * capacity : (j + 1) * capacity]
 
-    parts = 2
-    tile = slots // parts
+    settle_all(copies)
+    tile = slots // PARTS
 
     for j in range(per_owner):
 
-        @pl.loop(0, parts)
+        @pl.loop(0, PARTS)
         def _(i):
             own = rows_at(i, tile)
             block = picked[j, own, :]
@@ -318,16 +500,13 @@
             lift = inner[j, own, units : 2 * units].astype(f32)
             act, gate_grad, lift_grad = silu_back(raw * weigh, gate, lift)
             heat = jnp.sum(raw * act.astype(f32), axis=-1, keepdims=True)
-            heat = jnp.where(first_lane((tile, 128)) == j, heat, 0.0)
+            heat = jnp.where(first_lane((tile, 128)) == owner * per_owner + j, heat, 0.0)
             deep[j, 0, own, :] = gate_grad
             deep[j, 1, own, :] = lift_grad
             deep[j, 2, own, :] = act
             made = (mul_nt(gate_grad, up[j, 0]) + mul_nt(lift_grad, up[j, 1])).astype(bf16)
-            for q in range(group // parts):
-                here = slice(q * capacity, (q + 1) * capacity)
-                there = slice(j * capacity, (j + 1) * capacity)
-                sent[i * (group // parts) + q, there, :] = made[here]
-                spot[i * (group // parts) + q, there, :] = heat[here]
+            send_rows(sent, made, i, j, group, PARTS, capacity)
+            send_rows(spot, heat, i, j, group, PARTS, capacity)
 
     for j in range(per_owner):
         for s in range(3):
@@ -337,49 +516,59 @@
                 totals[a, j, s] = found[a * chunk : (a + 1) * chunk].astype(bf16)
 
 
-def routed_back(grad, select, up, down, arrived, inner, scale):
+def routed_back(layer, grad, select, up, down, arrived, inner, scale):
     group, spots, rows = select.shape
     per_owner, slots, width = arrived.shape
-    units = down.shape[1]
+    units = down.shape[2]
     planes = lax.axis_size("dp")
     return call(
-        routed_back_kernel,
+        functools.partial(routed_back_kernel, layer),
         [
             ((planes, per_owner, 3, width // planes, units), bf16),
             ((group, spots, width), bf16),
             ((group, spots, 128), f32),
         ],
-        [((per_owner, slots, width), bf16), ((per_owner, 3, slots, units), bf16)],
-        grad, select, up, down, arrived, inner, scale,
+        [
+            ((per_owner, slots, width), bf16),
+            ((per_owner, 3, slots, units), bf16),
+            (up.shape[1:], bf16),
+            (down.shape[1:], bf16),
+            DMA((2,)),
+        ],
+        grad, select, Far(up), Far(down), arrived, inner, scale,
     )
 
 
 def shared_back_kernel(
-    grad, mixed, back, router, wide, narrow, gates, shared_inner, sent, spot,
+    layer, grad, mixed, back, router, far_wide, far_narrow, gates, sent, spot, after,
     partial, dense, router_grad,
-    shared_out, shared_deep,
+    shared_out, shared_deep, wide, narrow, sems, wide_sems,
 ):
     group, rows, spots = back.shape
     width = grad.shape[1]
     units = narrow.shape[0]
     planes = lax.axis_size("dp")
     chunk = width // planes
-    columns = dense.shape[0]
-    owners = columns // planes
+    owners = dense.shape[0]
+    columns = owners * planes
     side = width // columns
     part = units // owners
     shards = lax.axis_size("wshard")
     owner = lax.axis_index("expert")
     count = shared_out.shape[0]
     piece = count // 2
+    copies = fetch([(far_narrow.at[layer], narrow)], sems)
+    more = fetch(wide_pairs(far_wide, wide), wide_sems)
+    settle_all(copies)
+    settle_all(more)
 
     @pl.loop(0, 2)
     def _(i):
         own = rows_at(i, piece)
-        block = grad[rows_at(owner * 2 + i, piece), :]
-        raw = mul_nt(block, narrow[...])
-        gate = shared_inner[own, 0:units].astype(f32)
-        lift = shared_inner[own, units : 2 * units].astype(f32)
+        raw = mul_nt(grad[rows_at(owner * 2 + i, piece), :], narrow[...])
+        block = mixed[rows_at(owner * 2 + i, piece), :]
+        gate = mul(block, wide[0])
+        lift = mul(block, wide[1])
         act, gate_grad, lift_grad = silu_back(raw, gate, lift)
         shared_deep[0, own, :] = gate_grad
         shared_deep[1, own, :] = lift_grad
@@ -408,13 +597,13 @@
             for a in range(planes):
                 for b in range(owners):
                     lanes = slice(b * part + h * size, b * part + (h + 1) * size)
-                    dense[a * owners + b, base : base + chunk, 0:size] = found[
+                    dense[b, a, base : base + chunk, 0:size] = found[
                         a * chunk : (a + 1) * chunk, lanes
                     ].astype(bf16)
             base += chunk
     own_grad = grad[rows_at(owner, count), :]
     for b in range(columns):
-        dense[b, base : base + units, 0:side] = mul_tn(
+        dense[b % owners, b // owners, base : base + units, 0:side] = mul_tn(
             shared_deep[2], own_grad[:, b * side : (b + 1) * side]
         ).astype(bf16)
 
@@ -424,21 +613,30 @@
     return 2 * (part // min(part, 128)) * (width // planes) + units
 
 
-def shared_back(grad, mixed, back, router, wide, narrow, gates, shared_inner, sent, spot):
+def shared_back(layer, grad, mixed, back, router, wide, narrow, gates, sent, spot, after):
     rows = back.shape[1]
-    _, width, units = wide.shape
+    width = mixed.shape[1]
+    units = narrow.shape[1]
     count = rows * lax.axis_size("wshard")
     planes = lax.axis_size("dp")
     owners = lax.axis_size("expert")
     return call(
-        shared_back_kernel,
+        functools.partial(shared_back_kernel, layer),
         [
             (mixed.shape, bf16),
-            ((planes * owners, dense_rows(width, units, planes, owners), 128), bf16),
+            ((owners, planes, dense_rows(width, units, planes, owners), 128), bf16),
             ((128, width), f32),
         ],
-        [((count, width), f32), ((3, count, units), bf16)],
-        grad, mixed, back, router, wide, narrow, gates, shared_inner, sent, spot,
+        [
+            ((count, width), f32),
+            ((3, count, units), bf16),
+            ((2, width, units), bf16),
+            (narrow.shape[1:], bf16),
+            DMA((1,)),
+            DMA((8,)),
+        ],
+        grad, mixed, back, router, Far(wide), Far(narrow), gates, sent, spot,
+        Far(narrow if after is None else after),
     )
 
 
@@ -477,49 +675,161 @@
     pl.semaphore_signal(barrier, inc=1, device_id=target(axes, place(tall, wide, owner, shard, steps[0], 1, True)), device_id_type=MESH)
     pl.semaphore_wait(barrier, len(steps))
 
-def gather_kernel(axes, x_ref, o_ref, send, recv, fsend, frecv):
+def gather_start(axes, x_ref, o_ref, sems):
     tall, wide, owner, shard = layout(axes)
     steps = steps_of(tall, wide)
     rows = x_ref.shape[0]
-    def block(where):
-        return o_ref.at[pl.ds(pl.multiple_of((where[0] * wide + where[1]) * rows, rows), rows)]
-    me = (owner, shard)
-    partner = place(tall, wide, owner, shard, steps[0], 1, True)
-    greet(axes, tall, wide, owner, shard)
+    send, recv = sems[:2]
+    mine = o_ref.at[rows_at(owner * wide + shard, rows)]
     copies = []
     for i, step in reversed(list(enumerate(steps))):
-        there = partner if i == 0 else place(tall, wide, owner, shard, step, 1, False)
-        copy = pltpu.make_async_remote_copy(src_ref=x_ref, dst_ref=block(me), send_sem=send.at[i], recv_sem=recv.at[i], device_id=target(axes, there), device_id_type=MESH)
+        there = place(tall, wide, owner, shard, step, 1, i == 0)
+        copy = pltpu.make_async_remote_copy(
+            src_ref=x_ref, dst_ref=mine, send_sem=send.at[i], recv_sem=recv.at[i],
+            device_id=target(axes, there), device_id_type=MESH,
+        )
         copy.start()
         copies.append(copy)
-    mine = block(me)
     mine[...] = x_ref[...]
+    return copies
+
+
+def gather_pass(axes, x_ref, o_ref, sems):
+    tall, wide, owner, shard = layout(axes)
+    steps = steps_of(tall, wide)
+    rows = x_ref.shape[0]
+    send, recv, fsend, frecv = sems
+    partner = target(axes, place(tall, wide, owner, shard, steps[0], 1, True))
     passed = []
     for i, step in list(enumerate(steps))[1:]:
         source = place(tall, wide, owner, shard, step, -1, False)
-        arrived = pltpu.make_async_remote_copy(src_ref=x_ref, dst_ref=block(source), send_sem=send.at[i], recv_sem=recv.at[i], device_id=target(axes, partner), device_id_type=MESH)
-        arrived.wait_recv()
-        onward = pltpu.make_async_remote_copy(src_ref=block(source), dst_ref=block(source), send_sem=fsend.at[i - 1], recv_sem=frecv.at[i - 1], device_id=target(axes, partner), device_id_type=MESH)
+        block = o_ref.at[rows_at(source[0] * wide + source[1], rows)]
+        pltpu.make_async_remote_copy(
+            src_ref=x_ref, dst_ref=block, send_sem=send.at[i], recv_sem=recv.at[i],
+            device_id=partner, device_id_type=MESH,
+        ).wait_recv()
+        onward = pltpu.make_async_remote_copy(
+            src_ref=block, dst_ref=block, send_sem=fsend.at[i - 1], recv_sem=frecv.at[i - 1],
+            device_id=partner, device_id_type=MESH,
+        )
         onward.start()
         passed.append(onward)
-    last = pltpu.make_async_remote_copy(src_ref=x_ref, dst_ref=block(partner), send_sem=send.at[0], recv_sem=recv.at[0], device_id=target(axes, partner), device_id_type=MESH)
-    last.wait_recv()
-    for i, step in list(enumerate(steps))[1:]:
+    return passed
+
+
+def gather_end(axes, x_ref, o_ref, sems, copies):
+    tall, wide, owner, shard = layout(axes)
+    steps = steps_of(tall, wide)
+    rows = x_ref.shape[0]
+    send, recv, fsend, frecv = sems
+    partner = target(axes, place(tall, wide, owner, shard, steps[0], 1, True))
+    for i, step in enumerate(steps):
         source = place(tall, wide, owner, shard, step, -1, True)
-        arrived = pltpu.make_async_remote_copy(src_ref=x_ref, dst_ref=block(source), send_sem=fsend.at[i - 1], recv_sem=frecv.at[i - 1], device_id=target(axes, partner), device_id_type=MESH)
-        arrived.wait_recv()
-    for copy in copies + passed:
+        block = o_ref.at[rows_at(source[0] * wide + source[1], rows)]
+        pltpu.make_async_remote_copy(
+            src_ref=x_ref, dst_ref=block, send_sem=send.at[0] if i == 0 else fsend.at[i - 1],
+            recv_sem=recv.at[0] if i == 0 else frecv.at[i - 1],
+            device_id=partner, device_id_type=MESH,
+        ).wait_recv()
+    for copy in copies:
         copy.wait_send()
 
+
+def gather_kernel(axes, x_ref, o_ref, *sems):
+    greet(axes, *layout(axes))
+    copies = gather_start(axes, x_ref, o_ref, sems)
+    copies = copies + gather_pass(axes, x_ref, o_ref, sems)
+    gather_end(axes, x_ref, o_ref, sems, copies)
+
+
+def gather_sems(axes):
+    h = group_size(axes) // 2
+    return [DMA((h,)), DMA((h,)), DMA((max(h - 1, 1),)), DMA((max(h - 1, 1),))]
+
+
+def group_size(axes):
+    return lax.axis_size("wshard") * (lax.axis_size("expert") if "expert" in axes else 1)
+
+
 def gather(x, axes, cid):
-    n = lax.axis_size("wshard") * (lax.axis_size("expert") if "expert" in axes else 1)
-    h = n // 2
-    dma = pltpu.SemaphoreType.DMA
-    return pl.pallas_call(functools.partial(gather_kernel, axes),
-        out_shape=jax.ShapeDtypeStruct((n * x.shape[0],) + x.shape[1:], x.dtype),
-        in_specs=[pl.BlockSpec(memory_space=pltpu.VMEM)], out_specs=pl.BlockSpec(memory_space=pltpu.VMEM),
-        scratch_shapes=[dma((h,)), dma((h,)), dma((max(h - 1, 1),)), dma((max(h - 1, 1),))],
-        compiler_params=pltpu.CompilerParams(collective_id=cid, has_side_effects=True, vmem_limit_bytes=32 << 20))(x)
+    vmem = pl.BlockSpec(memory_space=pltpu.VMEM)
+    return pl.pallas_call(
+        functools.partial(gather_kernel, axes),
+        out_shape=jax.ShapeDtypeStruct((group_size(axes) * x.shape[0],) + x.shape[1:], x.dtype),
+        in_specs=[vmem],
+        out_specs=vmem,
+        scratch_shapes=gather_sems(axes),
+        compiler_params=pltpu.CompilerParams(
+            collective_id=cid, has_side_effects=True, vmem_limit_bytes=32 << 20
+        ),
+    )(x)
+
+
+def begin_kernel(groups, *refs):
+    n = len(groups)
+    blocks, weight = refs[:n], refs[n]
+    outs, columns = refs[n + 1 : 2 * n + 1], refs[2 * n + 1]
+    sems = [refs[2 * n + 2 + 4 * i : 2 * n + 6 + 4 * i] for i in range(n)]
+    send, recv, local = refs[6 * n + 2 :]
+    tall, wide, owner, shard = layout(PLANE)
+    chunk = weight.shape[2]
+    window = columns.shape[2]
+    barrier = pltpu.get_barrier_semaphore()
+    steps = steps_of(tall, wide)
+    greeted = [(step, False) for step in steps[1:]] + [(step, True) for step in steps_of(1, wide)]
+    for step, flip in greeted:
+        pl.semaphore_signal(
+            barrier, inc=1, device_id=target(PLANE, place(tall, wide, owner, shard, step, 1, flip)),
+            device_id_type=MESH,
+        )
+    pl.semaphore_wait(barrier, len(greeted))
+    lines = columns.at[:, rows_at(shard, chunk), :]
+
+    def piece(a):
+        return weight.at[0, :, :, pl.ds(pl.multiple_of(a * chunk // 128 * 128, 128), window)]
+
+    copies = []
+    for k in range(1, wide):
+        there = lax.rem(shard + k, wide)
+        copy = pltpu.make_async_remote_copy(
+            src_ref=piece(there), dst_ref=lines, send_sem=send.at[k - 1], recv_sem=recv.at[k - 1],
+            device_id=target(SLOT, (0, there)), device_id_type=MESH,
+        )
+        copy.start()
+        copies.append(copy)
+    own = pltpu.make_async_copy(piece(shard), lines, local)
+    own.start()
+    sent = [gather_start(g, blocks[i], outs[i], sems[i]) for i, g in enumerate(groups)]
+    for i, g in enumerate(groups):
+        sent[i] = sent[i] + gather_pass(g, blocks[i], outs[i], sems[i])
+    for i, g in enumerate(groups):
+        gather_end(g, blocks[i], outs[i], sems[i], sent[i])
+    own.wait()
+    for copy in copies:
+        copy.wait_recv()
+        copy.wait_send()
+
+
+def begin(blocks, groups, weight, window, cid):
+    vmem = pl.BlockSpec(memory_space=pltpu.VMEM)
+    width = weight.shape[3]
+    others = lax.axis_size("wshard") - 1
+    outs = [
+        jax.ShapeDtypeStruct((group_size(g) * x.shape[0],) + x.shape[1:], x.dtype)
+        for x, g in zip(blocks, groups)
+    ] + [jax.ShapeDtypeStruct((3, width, window), weight.dtype)]
+    return pl.pallas_call(
+        functools.partial(begin_kernel, groups),
+        out_shape=tuple(outs),
+        in_specs=[vmem] * len(blocks) + [pl.BlockSpec(memory_space=pl.ANY)],
+        out_specs=tuple([vmem] * len(outs)),
+        scratch_shapes=[s for g in groups for s in gather_sems(g)]
+        + [DMA((others,)), DMA((others,)), DMA],
+        compiler_params=pltpu.CompilerParams(
+            collective_id=cid, has_side_effects=True, vmem_limit_bytes=32 << 20
+        ),
+    )(*blocks, weight)
+
 
 def reduce_kernel(axes, p_ref, o_ref, inbox, total, second, send, recv, fsend, frecv):
     tall, wide, owner, shard = layout(axes)
@@ -626,7 +936,17 @@
         [routes[0, :, 0], routes[0, :, 1], drop_order[0], valid.astype(jnp.int32)], axis=0
     )
     facts = jnp.concatenate([facts, jnp.zeros_like(facts)], axis=0)
-    facts = gather(facts, PLANE, 5).reshape(group, 8, rows)
+    small = jnp.concatenate([router_weight.transpose(0, 2, 1), norm_gains], axis=1)
+    lines = LAYERS * (experts + 2)
+    small = small.reshape(lines, chunk)
+    small = jnp.pad(small, ((0, -lines % 16), (0, window - chunk)))
+    grad_block = (cotangent[0].astype(f32) * valid[:, None].astype(f32)).astype(bf16)
+    slot_tokens, facts, small, grad_plane, project = begin(
+        (tokens[0], facts, small, grad_block), (SLOT, PLANE, SLOT, PLANE), qkv_weight, window, 5
+    )
+    facts = facts.reshape(group, 8, rows)
+    small = small.reshape(shards, -1, window)[:, :lines, :chunk]
+    small = small.transpose(1, 0, 2).reshape(LAYERS, experts + 2, width)
     mine = owner * per_owner + jnp.arange(per_owner, dtype=jnp.int32)
     first = facts[:, None, 0, :] == mine[None, :, None]
     second = facts[:, None, 1, :] == mine[None, :, None]
@@ -641,118 +961,139 @@
     back = (place.transpose(0, 2, 1)[:, :, :, None] == spot[None, None, None, :]).astype(bf16)
     back = back.reshape(group, rows, per_owner * room)
     lane = jnp.arange(128, dtype=jnp.int32)
-    named = jnp.where(lane < experts, lax.rem(lane + owner * per_owner, experts), -1)
+    named = jnp.where(lane < experts, lane, -1)
     both = (facts[:, 0, :, None] == named) | (facts[:, 1, :, None] == named)
     chosen = jnp.where(both, 0.0, floor_score).astype(f32).reshape(group * rows, 128)
 
-    project = jnp.stack([qkv_weight[..., s : s + window] for s in starts], axis=0)
-    project = lax.all_to_all(project, "wshard", split_axis=0, concat_axis=0, tiled=True)
-    project = project.transpose(1, 2, 0, 3, 4).reshape(LAYERS, 3, width, window)
-    wide = shared_up.reshape(LAYERS, 2, chunk, shards, units)
-    wide = lax.all_to_all(
-        wide.transpose(3, 0, 1, 2, 4), "wshard", split_axis=0, concat_axis=0, tiled=True
-    )
-    wide = wide.transpose(1, 2, 0, 3, 4).reshape(LAYERS, 2, width, units)
-    small = jnp.concatenate([router_weight.transpose(0, 2, 1), norm_gains], axis=1)
-    small = lax.all_gather(small, "wshard", axis=2, tiled=True)
+    def columns_of(weight, size, places):
+        return jnp.stack([weight[..., s : s + size] for s in places], axis=0)
+
+    def exchanged(packed, after):
+        packed, after = lax.optimization_barrier((packed, after))
+        return lax.all_to_all(packed, "wshard", split_axis=0, concat_axis=0, tiled=True), after
+
+    assert 2 * window == units
+    own_units = [a * units for a in range(shards)]
+    early = columns_of(shared_up[0], units, own_units)
+    early, slot_tokens = exchanged(early, slot_tokens)
+    late = columns_of(qkv_weight[1], window, starts)
+    late = jnp.concatenate(
+        [
+            columns_of(shared_up[1], units, own_units),
+            jnp.concatenate([late[:, 0:1], late[:, 1:2]], axis=3),
+            jnp.concatenate([late[:, 2:3], late[:, 2:3]], axis=3),
+        ],
+        axis=1,
+    )
     router_full = jnp.zeros((LAYERS, 128, width), bf16)
-    router_full = router_full.at[:, :experts].set(
-        jnp.roll(small[:, :experts], -owner * per_owner, axis=1)
-    )
+    router_full = router_full.at[:, :experts].set(small[:, :experts])
     gains_full = small[:, experts:].astype(f32)
     out_padded = lax.dynamic_update_slice(
         jnp.zeros((LAYERS, window, width), bf16), out_weight, (0, offset, 0)
     )
     half = HEAD_DIM // 2
-    lanes = jnp.arange(window, dtype=jnp.int32)
+    wave = jnp.arange(128, dtype=jnp.int32)
     angles = jnp.arange(count, dtype=jnp.int32).astype(f32)[:, None] * (
-        rotary_base ** (-(lanes % half).astype(f32) / half)
+        rotary_base ** (-(wave % half).astype(f32) / half)
     )[None, :]
     cosine = jnp.cos(angles)
-    sine = jnp.where((lanes % HEAD_DIM < half)[None, :], -jnp.sin(angles), jnp.sin(angles))
+    sine = jnp.where((wave % HEAD_DIM < half)[None, :], -jnp.sin(angles), jnp.sin(angles))
     length = jnp.broadcast_to(lengths[:, None], (8, 128))
+    lanes = jnp.arange(window, dtype=jnp.int32)
     sub = chunk // owners
     slot_lane = jnp.arange(owners * 128, dtype=jnp.int32)
     origin = jnp.where(slot_lane % 128 < sub, offset + slot_lane // 128 * sub + slot_lane % 128, -1)
     spread = (lanes[:, None] == origin[None, :]).astype(bf16)
 
-    grad_block = (cotangent[0].astype(f32) * valid[:, None].astype(f32)).astype(bf16)
-    grad_plane = gather(grad_block, PLANE, 2)
-
     stream = tokens[0].astype(f32)
     saved = []
     for layer in range(LAYERS):
+        last = layer == LAYERS - 1
         gains = gains_full[layer]
         normed_a, inverse_a = norm_parts(stream)
-        hidden = gather((normed_a * gains[0]).astype(bf16), SLOT, 1)
+        if layer == 0:
+            hidden = (norm_parts(slot_tokens.astype(f32))[0] * gains[0]).astype(bf16)
+        else:
+            hidden = gather((normed_a * gains[0]).astype(bf16), SLOT, 1)
         partial, queries, keys, values, probs, attended = attend(
-            hidden, project[layer], cosine, sine, length, out_padded[layer]
+            hidden, project, cosine, sine, length, out_padded[layer]
         )
         middle = stream + reduce(partial, SLOT, 3)
         normed_b, inverse_b = norm_parts(middle)
         mixed = gather((normed_b * gains[1]).astype(bf16), PLANE, 2)
-        partial, arrived, inner, scale, gates, shared_inner = expert(
-            mixed, select, back, chosen, router_full[layer], expert_up[layer], expert_down[layer],
-            wide[layer], shared_down[layer],
+        wide = late if last else early
+        if last:
+            arrived, inner, scale, gates = route(
+                layer, mixed, select, chosen, router_full[layer], expert_up
+            )
+        else:
+            late, mixed = exchanged(late, mixed)
+            partial, arrived, inner, scale, gates = expert(
+                layer, mixed, select, back, chosen, router_full[layer], expert_up, expert_down,
+                wide, shared_down,
+            )
+            stream = middle + reduce(partial, PLANE, 4)
+        saved.append(
+            (normed_a, inverse_a, hidden, project, queries, keys, values, probs, attended, normed_b,
+             inverse_b, mixed, wide, arrived, inner, scale, gates)
         )
-        stream = middle + reduce(partial, PLANE, 4)
-        saved.append(
-            (normed_a, inverse_a, hidden, queries, keys, values, probs, attended, normed_b,
-             inverse_b, mixed, arrived, inner, scale, gates, shared_inner)
-        )
-    block_out = stream.astype(bf16)[None]
+        project = late
     grad = grad_block.astype(f32)
-    gathered = []
+
+    def near_sum(piece):
+        def part(k):
+            return lax.dynamic_index_in_dim(piece, lax.rem(owner + k, owners), 0, keepdims=False)
+
+        total = part(0).astype(f32)
+        for k in range(1, owners):
+            hop = [(b, (b + k) % owners) for b in range(owners)]
+            total = total + lax.ppermute(part(k), "expert", hop).astype(f32)
+        return total.astype(bf16)
+
+    def far_sum(piece):
+        return lax.psum_scatter(piece, "dp", scatter_dimension=0, tiled=True)[0]
+
+    reduced = [None] * LAYERS
+    pieces = []
+    after = None
     small_grads = [None] * LAYERS
     for layer in reversed(range(LAYERS)):
-        (normed_a, inverse_a, hidden, queries, keys, values, probs, attended, normed_b,
-         inverse_b, mixed, arrived, inner, scale, gates, shared_inner) = saved[layer]
+        (normed_a, inverse_a, hidden, project, queries, keys, values, probs, attended, normed_b,
+         inverse_b, mixed, wide, arrived, inner, scale, gates) = saved[layer]
         gains = gains_full[layer]
         if layer < LAYERS - 1:
             grad_plane = gather(grad.astype(bf16), PLANE, 2)
         totals, sent, heat = routed_back(
-            grad_plane, select, expert_up[layer], expert_down[layer], arrived, inner, scale
+            layer, grad_plane, select, expert_up, expert_down, arrived, inner, scale
         )
         partial, dense_b, router_grad = shared_back(
-            grad_plane, mixed, back, router_full[layer], wide[layer], shared_down[layer], gates,
-            shared_inner, sent, heat,
+            layer, grad_plane, mixed, back, router_full[layer], wide, shared_down, gates, sent, heat,
+            after,
         )
+        after = far_sum(totals)
+        reduced[layer] = after
         mixed_grad = reduce(partial, PLANE, 4)
         gain_b_grad = jnp.sum(mixed_grad * normed_b, axis=0)
         middle_grad = grad + norm_back(mixed_grad * gains[1], normed_b, inverse_b)
         branch_grad = gather(middle_grad.astype(bf16), SLOT, 1)
         partial, dense_a = attend_back(
-            branch_grad, hidden, project[layer], cosine, sine, queries, keys, values, probs,
+            branch_grad, hidden, project, cosine, sine, queries, keys, values, probs,
             attended, out_padded[layer], spread,
         )
         hidden_grad = reduce(partial, SLOT, 3)
         gain_a_grad = jnp.sum(hidden_grad * normed_a, axis=0)
         grad = middle_grad + norm_back(hidden_grad * gains[0], normed_a, inverse_a)
-        gathered.append((totals, dense_b, dense_a))
+        pieces += [near_sum(dense_b), near_sum(dense_a)]
+        first_rows = dense_b.shape[2]
         small_grads[layer] = jnp.concatenate(
-            [
-                jnp.roll(router_grad[:experts], owner * per_owner, axis=0),
-                gain_a_grad[None],
-                gain_b_grad[None],
-            ],
-            axis=0,
+            [router_grad[:experts], gain_a_grad[None], gain_b_grad[None]], axis=0
         )
-    reduced = []
-    last = None
-    for totals, _, _ in gathered:
-        if last is not None:
-            totals, last = lax.optimization_barrier((totals, last))
-        last = lax.psum_scatter(totals, "dp", scatter_dimension=0, tiled=True)
-        reduced.append(last[0])
-    dense = jnp.concatenate([piece for item in gathered for piece in item[1:]], axis=1)
-    dense, last = lax.optimization_barrier((dense, last))
-    dense = lax.psum_scatter(dense, ("dp", "expert"), scatter_dimension=0, tiled=True)[0]
-    first_rows = gathered[0][1].shape[1]
-    layer_rows = first_rows + gathered[0][2].shape[1]
-    reduced = [
-        (reduced[i], dense[i * layer_rows :][:first_rows], dense[i * layer_rows + first_rows :][: layer_rows - first_rows])
-        for i in reversed(range(LAYERS))
-    ]
+    dense = far_sum(jnp.concatenate(pieces, axis=1)).reshape(LAYERS, -1, 128)[::-1]
+    reduced = [(reduced[i], dense[i, :first_rows], dense[i, first_rows:]) for i in range(LAYERS)]
+    grad, mixed = lax.optimization_barrier((grad, saved[-1][11]))
+    wide, arrived, inner, scale, gates = saved[-1][12:]
+    partial = finish(LAYERS - 1, mixed, back, inner, scale, expert_down, wide, shared_down, after)
+    block_out = (middle + reduce(partial, PLANE, 4)).astype(bf16)[None]
     small_all = lax.psum(jnp.stack(small_grads, axis=0), ("dp", "expert", "wshard"))
     small_own = lax.dynamic_slice_in_dim(small_all, shard * chunk, chunk, axis=2)
     turned = jnp.stack(

time: 708 us -> 570 us (0.81)
  waiting for transfers between devices: 146 us -> 48.8 us
  local copies, waits for them, and re-layouts: 68.6 us -> 42.1 us
  Pallas kernels: 377 us -> 360 us
  blocking collectives: 53.3 us -> 45.6 us
    reduce_scatter x3, waiting for transfers between devices: 116 us -> 0.01 us  [far_sum(): return lax.psum_scatter(piece, 'dp', scatter_dimension=0, tiled=True)[0]]
    pallas_call x9 -> x6, Pallas kernels: 141 us -> 63.9 us  [gather(): pl.pallas_call(functools.partial(gather_kernel, axes), out_shape=jax.Shap...]
    pallas_call x0 -> x1, Pallas kernels: none -> 31 us  [begin(): pl.pallas_call(functools.partial(begin_kernel, groups), out_shape=tuple(o...]
    pallas_call x8, Pallas kernels: 89.5 us -> 114 us  [reduce(): pl.pallas_call(functools.partial(reduce_kernel, axes), out_shape=jax.Shap...]
    ppermute x0 -> x4, waiting for transfers between devices: none -> 19.4 us  [near_sum(): total = total + lax.ppermute(part(k), 'expert', hop).astype(f32)]
    slice x1, local copies, waits for them, and re-layouts: 9.71 us -> 0.03 us  [per_device(): mixed = gather((normed_b * gains[1]).astype(bf16), PLANE, 2)]
    all_gather x1 -> x0, blocking collectives: 7.5 us -> none  [per_device(): small = lax.all_gather(small, 'wshard', axis=2, tiled=True)]
    pallas_call x10 -> x11, Pallas kernels: 146 us -> 151 us  [call(): pl.pallas_call(kernel, out_shape=tuple((jax.ShapeDtypeStruct(s, d) for s,...]
  transfers between devices with their start and end apart: 6 -> 10, of which waited for: 3 -> 2; matrix products, arithmetic and copies ran while one was open for 10% -> 8% of each run, Pallas kernels for 36% -> 48%
where the time goes in v2:
time: 570 us; the launch traced here: 561 us
  Pallas kernels  360 us (63%)
  waiting for transfers between devices  48.8 us (9%)
  blocking collectives  45.6 us (8%)
  local copies, waits for them, and re-layouts  42.1 us (7%)
  other arithmetic  29.6 us (5%)
  starting transfers between devices  19 us (3%)
  between operations  15.6 us (3%)
    pallas_call x11, Pallas kernels, call(): pl.pallas_call(kernel, out_shape=tuple((jax.ShapeDtypeStruct(s, d) for s,...  151 us
    pallas_call x8, Pallas kernels, reduce(): pl.pallas_call(functools.partial(reduce_kernel, axes), out_shape=jax.Shap...  114 us
    pallas_call x6, Pallas kernels, gather(): pl.pallas_call(functools.partial(gather_kernel, axes), out_shape=jax.Shap...  63.9 us
    psum x1, blocking collectives, per_device(): lax.psum(jnp.stack(small_grads, axis=0), ('dp', 'expert', 'wshard'))  45.6 us
    pallas_call x1, Pallas kernels, begin(): pl.pallas_call(functools.partial(begin_kernel, groups), out_shape=tuple(o...  31 us
    ppermute x1, waiting for transfers between devices, per_device(): turned = lax.ppermute(turned, ('dp', 'wshard'), transposed).astype(f32)  29.4 us
    ppermute x4, waiting for transfers between devices, near_sum(): total = total + lax.ppermute(part(k), 'expert', hop).astype(f32)  19.4 us
    unnamed x94, local copies, waits for them, and re-layouts  18.1 us
  transfers between devices with their start and end apart: 10, of which 2 were waited for; matrix products, arithmetic and copies ran while one was open for 8% of the time, Pallas kernels for 48%

profile of v2, /device:TPU:4, one launch (start us, length us, event | category | flops | bytes accessed | tf_op | source)
XLA Modules:
  0.0 561.2 jit_solution(1160098552562949955)
XLA Ops:
  14.4 31.0 %shard_map.204 = (bf16[512,768]{1,0:T(8,128)(2,1)S(1)}, s32[64,128]{1,0:T(8,128)S(1)}, bf16[64,256]{1,0:T(8,128)(2,1)S(1)}, bf16[1024,768]{1,0:T(8,128)(2,1)S(1)}, bf16[3,768,256]{2,1,0:T(8,128)(2,1)S(1)}) custom-call(bf16[128,768]{1,0:T(8,128)(2,1)S(1)} %bitcast.154, s32[8,128]{1,0:T(8,128)S(1)} %concatenate.32.refs_1_, bf16[16,256]{1,0:T(8,128)(2,1)S(1)} %pad.7.refs_2_, ...), custom_call_target="tpu_custom_call" | custom-call | tf_op jit(solution)/shard_map/pallas_call | solution.py:821
  69.3 8.7 %shard_map.206 = f32[128,768]{1,0:T(8,128)S(1)} custom-call(bf16[512,768]{1,0:T(8,128)(2,1)S(1)} %copy-done.17), custom_call_target="tpu_custom_call" | custom-call | tf_op jit(solution)/shard_map/pallas_call | solution.py:875
  79.4 13.4 %shard_map.207.mixed = bf16[1024,768]{1,0:T(8,128)(2,1)S(1)} custom-call(bf16[128,768]{1,0:T(8,128)(2,1)S(1)} %multiply_convert_fusion.2.x_ref), custom_call_target="tpu_custom_call" | custom-call | tf_op jit(solution)/shard_map/pallas_call | solution.py:756
  106.4 18.5 %shard_map.208 = (bf16[1024,768]{1,0:T(8,128)(2,1)}, bf16[2,640,768]{2,1,0:T(8,128)(2,1)}, bf16[2,640,1024]{2,1,0:T(8,128)(2,1)}, f32[2,640,1]{2,1,0:T(8,128)}, f32[1024,128]{1,0:T(8,128)}) custom-call(bf16[1024,768]{1,0:T(8,128)(2,1)} %copy-done.1, bf16[8,160,128]{2,1,0:T(8,128)(2,1)} %fusion.7.select, bf16[8,128,160]{2,1,0:T(8,128)(2,1)} %compare_convert_fusion.back, ...), custom_call_target="tpu_custom_call" | custom-call | tf_op jit(solution)/shard_map/pallas_call | solution.py:51
  126.3 18.8 %shard_map.209 = f32[128,768]{1,0:T(8,128)S(1)} custom-call(bf16[1024,768]{1,0:T(8,128)(2,1)S(1)} %copy-done.13), custom_call_target="tpu_custom_call" | custom-call | tf_op jit(solution)/shard_map/pallas_call | solution.py:875
  154.6 8.6 %shard_map.211 = (bf16[512,768]{1,0:T(8,128)(2,1)}, bf16[512,256]{1,0:T(8,128)(2,1)}, bf16[512,256]{1,0:T(8,128)(2,1)}, bf16[512,256]{1,0:T(8,128)(2,1)}, bf16[4...) custom-call(bf16[512,768]{1,0:T(8,128)(2,1)} %copy-done.3, bf16[4,4,192,512]{3,2,1,0:T(8,128)(2,1)} %all-to-all-done.1.source.far_wide, ...), custom_call_target="tpu_custom_call" | custom-call | tf_op jit(solution)/shard_map/pallas_call | solution.py:51
  164.4 8.7 %shard_map.212 = f32[128,768]{1,0:T(8,128)S(1)} custom-call(bf16[512,768]{1,0:T(8,128)(2,1)S(1)} %copy-done.16), custom_call_target="tpu_custom_call" | custom-call | tf_op jit(solution)/shard_map/pallas_call | solution.py:875
  173.3 13.2 %shard_map.213.mixed = bf16[1024,768]{1,0:T(8,128)(2,1)S(1)} custom-call(bf16[128,768]{1,0:T(8,128)(2,1)S(1)} %multiply_convert_fusion.x_ref), custom_call_target="tpu_custom_call" | custom-call | tf_op jit(solution)/shard_map/pallas_call | solution.py:756
  187.7 11.8 %shard_map.214 = (bf16[2,640,768]{2,1,0:T(8,128)(2,1)}, bf16[2,640,1024]{2,1,0:T(8,128)(2,1)}, f32[2,640,1]{2,1,0:T(8,128)}, f32[1024,128]{1,0:T(8,128)}) custom-call(bf16[1024,768]{1,0:T(8,128)(2,1)} %copy-done, bf16[8,160,128]{2,1,0:T(8,128)(2,1)} %fusion.7.select, f32[1024,128]{1,0:T(8,128)} %or_select_fusion.chosen, ...), custom_call_target="tpu_custom_call" | custom-call | tf_op jit(solution)/shard_map/pallas_call | solution.py:51
  199.5 17.1 %shard_map.215 = (bf16[4,2,3,192,512]{4,3,2,1,0:T(8,128)(2,1)}, bf16[8,160,768]{2,1,0:T(8,128)(2,1)}, f32[8,160,128]{2,1,0:T(8,128)}) custom-call(bf16[1024,768]{1,0:T(8,128)(2,1)} %copy-done.4, bf16[8,160,128]{2,1,0:T(8,128)(2,1)} %fusion.7.select, bf16[2,2,2,768,512]{4,3,2,1,0:T(8,128)(2,1)} %far_up.7, bf16[2,2,512,768]{3,2,1,0:T(8,128)(2,1)} %far_down.7, ...), custom_call_target="tpu_custom_call" | custom-call | tf_op jit(solution)/shard_map/pallas_call | solution.py:51
  217.4 16.1 %shard_map.216 = (bf16[1024,768]{1,0:T(8,128)(2,1)}, bf16[2,4,1280,128]{3,2,1,0:T(8,128)(2,1)}, f32[128,768]{1,0:T(8,128)}) custom-call(bf16[1024,768]{1,0:T(8,128)(2,1)} %copy-done.4, bf16[1024,768]{1,0:T(8,128)(2,1)} %copy-done, bf16[8,128,160]{2,1,0:T(8,128)(2,1)} %compare_convert_fusion.back, bf16[128,768]{1,0:T(8,128)(2,1)} %get-tuple-element.172.router, ...), custom_call_target="tpu_custom_call" | custom-call | tf_op jit(solution)/shard_map/pallas_call | solution.py:51
  234.9 13.9 %shard_map.217 = f32[128,768]{1,0:T(8,128)S(1)} custom-call(bf16[1024,768]{1,0:T(8,128)(2,1)S(1)} %copy-done.12), custom_call_target="tpu_custom_call" | custom-call | tf_op jit(solution)/shard_map/pallas_call | solution.py:875
  258.8 12.4 %shard_map.219 = (bf16[512,768]{1,0:T(8,128)(2,1)}, bf16[2,4,768,128]{3,2,1,0:T(8,128)(2,1)}) custom-call(bf16[512,768]{1,0:T(8,128)(2,1)} %copy-done.8, bf16[512,768]{1,0:T(8,128)(2,1)} %copy-done.3, bf16[4,4,192,512]{3,2,1,0:T(8,128)(2,1)} %all-to-all-done.1.source.far_wide, f32[512,128]{1,0:T(8,128)} %get-tuple-element.175.cosine, ...), custom_call_target="tpu_custom_call" | custom-call | tf_op jit(solution)/shard_map/pallas_call | solution.py:51
  272.3 8.7 %shard_map.220 = f32[128,768]{1,0:T(8,128)S(1)} custom-call(bf16[512,768]{1,0:T(8,128)(2,1)S(1)} %copy-done.15), custom_call_target="tpu_custom_call" | custom-call | tf_op jit(solution)/shard_map/pallas_call | solution.py:875
  282.0 13.2 %shard_map.221.grad = bf16[1024,768]{1,0:T(8,128)(2,1)S(1)} custom-call(bf16[128,768]{1,0:T(8,128)(2,1)S(1)} %get-tuple-element.132.x_ref), custom_call_target="tpu_custom_call" | custom-call | tf_op jit(solution)/shard_map/pallas_call | solution.py:756
  296.4 17.1 %shard_map.222 = (bf16[4,2,3,192,512]{4,3,2,1,0:T(8,128)(2,1)}, bf16[8,160,768]{2,1,0:T(8,128)(2,1)}, f32[8,160,128]{2,1,0:T(8,128)}) custom-call(bf16[1024,768]{1,0:T(8,128)(2,1)} %copy-done.2, bf16[8,160,128]{2,1,0:T(8,128)(2,1)} %fusion.7.select, bf16[2,2,2,768,512]{4,3,2,1,0:T(8,128)(2,1)} %far_up.7, bf16[2,2,512,768]{3,2,1,0:T(8,128)(2,1)} %far_down.7, ...), custom_call_target="tpu_custom_call" | custom-call | tf_op jit(solution)/shard_map/pallas_call | solution.py:51
  319.2 17.3 %shard_map.223 = (bf16[1024,768]{1,0:T(8,128)(2,1)}, bf16[2,4,1280,128]{3,2,1,0:T(8,128)(2,1)}, f32[128,768]{1,0:T(8,128)}) custom-call(bf16[1024,768]{1,0:T(8,128)(2,1)} %copy-done.2, bf16[1024,768]{1,0:T(8,128)(2,1)} %copy-done.1, bf16[8,128,160]{2,1,0:T(8,128)(2,1)} %compare_convert_fusion.back, bf16[128,768]{1,0:T(8,128)(2,1)} %get-tuple-element.173.router, ...), custom_call_target="tpu_custom_call" | custom-call | tf_op jit(solution)/shard_map/pallas_call | solution.py:51
  339.2 33.7 %shard_map.224 = f32[128,768]{1,0:T(8,128)S(1)} custom-call(bf16[1024,768]{1,0:T(8,128)(2,1)S(1)} %copy-done.11), custom_call_target="tpu_custom_call" | custom-call | tf_op jit(solution)/shard_map/pallas_call | solution.py:875
  382.9 12.4 %shard_map.226 = (bf16[512,768]{1,0:T(8,128)(2,1)}, bf16[2,4,768,128]{3,2,1,0:T(8,128)(2,1)}) custom-call(bf16[512,768]{1,0:T(8,128)(2,1)} %copy-done.10, bf16[512,768]{1,0:T(8,128)(2,1)} %fusion.4.hidden, bf16[3,768,256]{2,1,0:T(8,128)(2,1)} %copy-done.6, f32[512,128]{1,0:T(8,128)} %get-tuple-element.175.cosine, f32[512,128]{1,0:T(8,128)} %get-tuple-element.174.sine, ...), custom_call_target="tpu_custom_call" | custom-call | tf_op jit(solution)/shard_map/pallas_call | solution.py:51
  401.0 19.4 %collective-permute-done.3 = bf16[4,768,128]{2,1,0:T(8,128)(2,1)S(1)} collective-permute-done((bf16[4,768,128]{2,1,0:T(8,128)(2,1)S(1)}, bf16[4,768,128]{2,1,0:T(8,128)(2,1)S(1)}, u32[]{:S(2)}, u32[]{:S(2)}) %collective-permute-start.3) | collective-permute-done | bytes 786464 | tf_op jit(solution)/shard_map/ppermute | solution.py:1050
  435.7 11.6 %shard_map.228.p_ref = bf16[1024,768]{1,0:T(8,128)(2,1)} custom-call(bf16[1024,768]{1,0:T(8,128)(2,1)} %copy-done, bf16[8,128,160]{2,1,0:T(8,128)(2,1)} %compare_convert_fusion.back, bf16[2,640,1024]{2,1,0:T(8,128)(2,1)} %get-tuple-element.84.inner, f32[2,640,1]{2,1,0:T(8,128)} %get-tuple-element.85.scale, bf16[2,2,512,768]{3,2,1,0:T(8,128)(2,1)} %far_down.7, ...), custom_call_target="tpu_custom_call" | custom-call | tf_op jit(solution)/shard_map/pallas_call | solution.py:51
  448.7 14.0 %shard_map.229 = f32[128,768]{1,0:T(8,128)S(1)} custom-call(bf16[1024,768]{1,0:T(8,128)(2,1)S(1)} %copy-done.5), custom_call_target="tpu_custom_call" | custom-call | tf_op jit(solution)/shard_map/pallas_call | solution.py:875
  462.8 45.6 %psum.7 = f32[2,6,768]{2,1,0:T(8,128)S(1)} all-reduce(f32[2,6,768]{2,1,0:T(8,128)S(1)} %pad_maximum_fusion.4), channel_id=1, replica_groups=mesh['dp'=4,'expert'=2,'wshard'=4] {'dp','expert','wshard'}, use_global_device_ids=true, to_apply=%region_17.18 | all-reduce | flops 9216 | bytes 73728 | tf_op jit(solution)/shard_map/psum | solution.py:1097
  522.1 29.4 %collective-permute-done.4 = bf16[2,1344,128]{2,1,0:T(8,128)(2,1)S(1)} collective-permute-done((bf16[2,1344,128]{2,1,0:T(8,128)(2,1)S(1)}, bf16[2,1344,128]{2,1,0:T(8,128)(2,1)S(1)}, u32[]{:S(2)}, u32[]{:S(2)}) %collective-permute-start.4) | collective-permute-done | bytes 688160 | tf_op jit(solution)/shard_map/ppermute | solution.py:1106
  (234 shorter events, 131.2 us)
Async XLA Ops:
  7.2 3.9 copy-start.38
  7.2 3.8 copy-start.39
  47.7 48.1 %all-to-all-start = ((bf16[4,2,192,512]{3,2,1,0:T(8,128)(2,1)}), bf16[4,2,192,512]{3,2,1,0:T(8,128)(2,1)}, u32[]{:S(2)}, u32[]{:S(2)}) async-start(bf16[4,2,192,512]{3,2,1,0:T(8,128)(2,1)} %pad_maximum_fusion.1), calls=%async_computation | async-start | bytes 3145728 | tf_op jit(solution)/shard_map/all_to_all | solution.py:973
  56.0 45.3 %copy-start.31 = (bf16[2,6,768]{2,1,0:T(8,128)(2,1)}, bf16[2,6,768]{2,1,0:T(8,128)(2,1)S(1)}, u32[]{:S(2)}) copy-start(bf16[2,6,768]{2,1,0:T(8,128)(2,1)S(1)} %reshape.266) | copy-start | bytes 55300
  69.3 9.3 %copy-start.18 = (bf16[3,192,768]{2,1,0:T(8,128)(2,1)S(1)}, bf16[3,192,768]{2,1,0:T(8,128)(2,1)}, u32[]{:S(2)}) copy-start(bf16[3,192,768]{2,1,0:T(8,128)(2,1)} %slice_bitcast_fusion.2) | copy-start | bytes 2654212
  79.0 14.9 %copy-start.25 = (bf16[1,2,192,512]{3,2,1,0:T(8,128)(2,1)S(1)}, bf16[1,2,192,512]{3,2,1,0:T(8,128)(2,1)}, u32[]{:S(2)}) copy-start(bf16[1,2,192,512]{3,2,1,0:T(8,128)(2,1)} %get-tuple-element.142) | copy-start | bytes 1179652
  79.0 14.9 %copy-start.26 = (bf16[1,2,192,512]{3,2,1,0:T(8,128)(2,1)S(1)}, bf16[1,2,192,512]{3,2,1,0:T(8,128)(2,1)}, u32[]{:S(2)}) copy-start(bf16[1,2,192,512]{3,2,1,0:T(8,128)(2,1)} %get-tuple-element.143) | copy-start | bytes 1179652
  79.1 14.9 %copy-start.27 = (bf16[1,2,192,512]{3,2,1,0:T(8,128)(2,1)S(1)}, bf16[1,2,192,512]{3,2,1,0:T(8,128)(2,1)}, u32[]{:S(2)}) copy-start(bf16[1,2,192,512]{3,2,1,0:T(8,128)(2,1)} %get-tuple-element.144) | copy-start | bytes 1179652
  79.1 14.9 %copy-start.28 = (bf16[1,2,192,512]{3,2,1,0:T(8,128)(2,1)S(1)}, bf16[1,2,192,512]{3,2,1,0:T(8,128)(2,1)}, u32[]{:S(2)}) copy-start(bf16[1,2,192,512]{3,2,1,0:T(8,128)(2,1)} %get-tuple-element.145) | copy-start | bytes 1179652
  95.9 58.8 %all-to-all-start.1 = ((bf16[4,4,192,512]{3,2,1,0:T(8,128)(2,1)}), bf16[4,4,192,512]{3,2,1,0:T(8,128)(2,1)}, u32[]{:S(2)}, u32[]{:S(2)}) async-start(bf16[4,4,192,512]{3,2,1,0:T(8,128)(2,1)} %maximum_maximum_fusion), calls=%async_computation.1 | async-start | bytes 6291456 | tf_op jit(solution)/shard_map/all_to_all | solution.py:973
  101.2 218.0 %reduce-scatter.4.cloned.1.call-start = ((), (), s32[]{:S(2)}) async-start(), calls=%async_computation.5 | async-start | bytes 5898240 | tf_op jit(solution)/shard_map/reduce_scatter | solution.py:1054
  216.6 219.1 %reduce-scatter.6.cloned.1.call-start = ((), (), s32[]{:S(2)}) async-start(), calls=%async_computation.6 | async-start | bytes 5898240 | tf_op jit(solution)/shard_map/reduce_scatter | solution.py:1054
  233.5 16.0 %copy-start.35 = (f32[128]{0:T(128)S(1)}, f32[128]{0:T(128)}, u32[]{:S(2)}) copy-start(f32[128]{0:T(128)} %copy-done.34) | copy-start | bytes 1540
  313.5 200.6 %reduce-scatter.8.cloned.1.call-start = ((), (), s32[]{:S(2)}) async-start(), calls=%async_computation.7 | async-start | bytes 5242880 | tf_op jit(solution)/shard_map/reduce_scatter | solution.py:1054
  316.2 82.9 %collective-permute-start = (bf16[4,1280,128]{2,1,0:T(8,128)(2,1)}, bf16[4,1280,128]{2,1,0:T(8,128)(2,1)}, u32[]{:S(2)}, u32[]{:S(2)}) collective-permute-start(bf16[4,1280,128]{2,1,0:T(8,128)(2,1)} %dynamic-slice_bitcast_fusion.1), channel_id=1, source_target_pairs={{0,4},{4,0},{1,5},{5,1},{2,6},{6,2},{3,7},{7,3},{8,12},{12,8},{9,1... | collective-permute-start | bytes 3932168 | tf_op jit(solution)/shard_map/ppermute | solution.py:1050
  318.3 79.5 %collective-permute-start.1 = (bf16[4,768,128]{2,1,0:T(8,128)(2,1)}, bf16[4,768,128]{2,1,0:T(8,128)(2,1)}, u32[]{:S(2)}, u32[]{:S(2)}) collective-permute-start(bf16[4,768,128]{2,1,0:T(8,128)(2,1)} %dynamic-slice_bitcast_fusion.3), channel_id=1, source_target_pairs={{0,4},{4,0},{1,5},{5,1},{2,6},{6,2},{3,7},{7,3},{8,12},{12,8},{9,1... | collective-permute-start | bytes 2359304 | tf_op jit(solution)/shard_map/ppermute | solution.py:1050
  336.6 37.5 %copy-start.37 = (f32[128]{0:T(128)S(1)}, f32[128]{0:T(128)}, u32[]{:S(2)}) copy-start(f32[128]{0:T(128)} %copy-done.36) | copy-start | bytes 1540
  373.0 47.6 %collective-permute-start.2 = (bf16[4,1280,128]{2,1,0:T(8,128)(2,1)}, bf16[4,1280,128]{2,1,0:T(8,128)(2,1)}, u32[]{:S(2)}, u32[]{:S(2)}) collective-permute-start(bf16[4,1280,128]{2,1,0:T(8,128)(2,1)} %dynamic-slice_bitcast_fusion), channel_id=1, source_target_pairs={{0,4},{4,0},{1,5},{5,1},{2,6},{6,2},{3,7},{7,3},{8,12},{12,8},{9,1... | collective-permute-start | bytes 3932168 | tf_op jit(solution)/shard_map/ppermute | solution.py:1050
  396.6 23.7 %collective-permute-start.3 = (bf16[4,768,128]{2,1,0:T(8,128)(2,1)S(1)}, bf16[4,768,128]{2,1,0:T(8,128)(2,1)S(1)}, u32[]{:S(2)}, u32[]{:S(2)}) collective-permute-start(bf16[4,768,128]{2,1,0:T(8,128)(2,1)S(1)} %dynamic-slice_bitcast_fusion.2), channel_id=1, source_target_pairs={{0,4},{4,0},{1,5},{5,1},{2,6},{6,2},{3,7},{7,3},{8,12},{12,8},{9,1... | collective-permute-start | bytes 2359304 | tf_op jit(solution)/shard_map/ppermute | solution.py:1050
  399.1 21.3 %copy-start.30 = (bf16[2,4,768,128]{3,2,1,0:T(8,128)(2,1)S(1)}, bf16[2,4,768,128]{3,2,1,0:T(8,128)(2,1)}, u32[]{:S(2)}) copy-start(bf16[2,4,768,128]{3,2,1,0:T(8,128)(2,1)} %get-tuple-element.115) | copy-start | bytes 4718596
  399.1 21.5 %copy-start.23 = (bf16[2,4,1280,128]{3,2,1,0:T(8,128)(2,1)S(1)}, bf16[2,4,1280,128]{3,2,1,0:T(8,128)(2,1)}, u32[]{:S(2)}) copy-start(bf16[2,4,1280,128]{3,2,1,0:T(8,128)(2,1)} %get-tuple-element.114) | copy-start | bytes 7864324
  448.7 61.0 %copy-start.20 = (bf16[1,2,3,192,512]{4,3,2,1,0:T(8,128)(2,1)S(1)}, bf16[1,2,3,192,512]{4,3,2,1,0:T(8,128)(2,1)}, u32[]{:S(2)}) copy-start(bf16[1,2,3,192,512]{4,3,2,1,0:T(8,128)(2,1)} %reduce-scatter.6.cloned.1.call-done) | copy-start | bytes 3538948
  462.7 47.1 %copy-start.19 = (bf16[1,2,3,192,512]{4,3,2,1,0:T(8,128)(2,1)S(1)}, bf16[1,2,3,192,512]{4,3,2,1,0:T(8,128)(2,1)}, u32[]{:S(2)}) copy-start(bf16[1,2,3,192,512]{4,3,2,1,0:T(8,128)(2,1)} %reduce-scatter.4.cloned.1.call-done) | copy-start | bytes 3538948
  516.1 35.4 %collective-permute-start.4 = (bf16[2,1344,128]{2,1,0:T(8,128)(2,1)S(1)}, bf16[2,1344,128]{2,1,0:T(8,128)(2,1)S(1)}, u32[]{:S(2)}, u32[]{:S(2)}) collective-permute-start(bf16[2,1344,128]{2,1,0:T(8,128)(2,1)S(1)} %pad_maximum_fusion.3), channel_id=1, source_target_pairs={{0,0},{1,8},{2,16},{3,24},{8,1},{9,9},{10,17},{11,25},{16,2},{17,1... | collective-permute-start | bytes 2064392 | tf_op jit(solution)/shard_map/ppermute | solution.py:1106
  (32 other events, 49.8 us)
Sparse Core Ops, SparseCore 0:
  216.7 85.9 reduce-scatter.3
  313.6 86.0 reduce-scatter.5
  424.8 78.5 reduce-scatter.7

commit v3 on v2

--- a/solution.py
+++ b/solution.py
@@ -15,7 +15,8 @@
 floor_score = -1e30
 bf16 = jnp.bfloat16
 f32 = jnp.float32
-VMEM_LIMIT = 60 << 20
+VMEM_MOST = 60 << 20
+VMEM_SLACK = 8 << 20
 
 
 def mul(a, b):
@@ -45,16 +46,28 @@
         self.value = value
 
 
+def held_bytes(shape, dtype):
+    *lead, rows, lanes = shape
+    total = (rows + 15) // 16 * 16 * ((lanes + 127) // 128 * 128) * jnp.dtype(dtype).itemsize
+    for size in lead:
+        total *= size
+    return total
+
+
 def call(kernel, outs, scratch, *operands):
+    need = sum(held_bytes(s, d) for s, d in outs)
+    need += sum(held_bytes(*s) for s in scratch if isinstance(s, tuple))
+    need += sum(held_bytes(o.shape, o.dtype) for o in operands if not isinstance(o, Far))
+    limit = min(VMEM_MOST, need + VMEM_SLACK)
     vmem = pl.BlockSpec(memory_space=pltpu.VMEM)
-    far = pl.BlockSpec(memory_space=pl.ANY)
+    far = pl.BlockSpec(memory_space=pltpu.HBM)
     return pl.pallas_call(
         kernel,
         out_shape=tuple(jax.ShapeDtypeStruct(s, d) for s, d in outs),
         in_specs=[far if isinstance(o, Far) else vmem for o in operands],
         out_specs=tuple([vmem] * len(outs)),
         scratch_shapes=[pltpu.VMEM(*s) if isinstance(s, tuple) else s for s in scratch],
-        compiler_params=pltpu.CompilerParams(vmem_limit_bytes=VMEM_LIMIT),
+        compiler_params=pltpu.CompilerParams(vmem_limit_bytes=limit),
     )(*[o.value if isinstance(o, Far) else o for o in operands])
 
 
@@ -157,7 +170,7 @@
 
 
 def attend_back_kernel(
-    grad, hidden, source, cosine, sine, queries, keys, values, probs, attended, out_weight, spread,
+    grad, hidden, source, cosine, sine, queries, keys, values, probs, attended, out_weight, spread, near,
     partial, dense, attended_grad, dq, dk, dv, made, lift, weight, sems,
 ):
     count, width = grad.shape
@@ -218,7 +231,7 @@
 
 
 def attend_back(
-    grad, hidden, source, cosine, sine, queries, keys, values, probs, attended, out_weight, spread
+    grad, hidden, source, cosine, sine, queries, keys, values, probs, attended, out_weight, spread, near
 ):
     count, width = hidden.shape
     window = out_weight.shape[0]
@@ -238,7 +251,7 @@
             DMA((16,)),
         ],
         grad, hidden, Far(source), cosine, sine, queries, keys, values, probs, attended, out_weight,
-        spread,
+        spread, Far(source if near is None else near),
     )
 
 
@@ -465,7 +478,7 @@
 
 
 def routed_back_kernel(
-    layer, grad, select, far_up, far_down, arrived, inner, scale,
+    layer, grad, select, far_up, far_down, arrived, inner, scale, after,
     totals, sent, spot,
     picked, deep, up, down, sems,
 ):
@@ -516,7 +529,7 @@
                 totals[a, j, s] = found[a * chunk : (a + 1) * chunk].astype(bf16)
 
 
-def routed_back(layer, grad, select, up, down, arrived, inner, scale):
+def routed_back(layer, grad, select, up, down, arrived, inner, scale, after):
     group, spots, rows = select.shape
     per_owner, slots, width = arrived.shape
     units = down.shape[2]
@@ -535,7 +548,7 @@
             (down.shape[1:], bf16),
             DMA((2,)),
         ],
-        grad, select, Far(up), Far(down), arrived, inner, scale,
+        grad, select, Far(up), Far(down), arrived, inner, scale, Far(up if after is None else after),
     )
 
 
@@ -638,6 +651,24 @@
         grad, mixed, back, router, Far(wide), Far(narrow), gates, sent, spot,
         Far(narrow if after is None else after),
     )
+
+
+def pick_kernel(step, whole, after, out, sem):
+    owners = whole.shape[0]
+    copy = pltpu.make_async_copy(
+        whole.at[lax.rem(lax.axis_index("expert") + step, owners)], out, sem
+    )
+    copy.start()
+    copy.wait()
+
+
+def pick(whole, step, after):
+    return call(
+        functools.partial(pick_kernel, step),
+        [(whole.shape[1:], whole.dtype)],
+        [DMA],
+        Far(whole), Far(after),
+    )[0]
 
 
 MESH = pl.DeviceIdType.MESH
@@ -1040,14 +1071,17 @@
         project = late
     grad = grad_block.astype(f32)
 
-    def near_sum(piece):
-        def part(k):
-            return lax.dynamic_index_in_dim(piece, lax.rem(owner + k, owners), 0, keepdims=False)
-
-        total = part(0).astype(f32)
+    def near_send(piece, after):
+        arrivals = []
         for k in range(1, owners):
             hop = [(b, (b + k) % owners) for b in range(owners)]
-            total = total + lax.ppermute(part(k), "expert", hop).astype(f32)
+            arrivals.append(lax.ppermute(pick(piece, k, after), "expert", hop))
+        return arrivals
+
+    def near_sum(piece, arrivals, after):
+        total = pick(piece, 0, after).astype(f32)
+        for item in arrivals:
+            total = total + item.astype(f32)
         return total.astype(bf16)
 
     def far_sum(piece):
@@ -1063,8 +1097,10 @@
         gains = gains_full[layer]
         if layer < LAYERS - 1:
             grad_plane = gather(grad.astype(bf16), PLANE, 2)
+            arrivals = near_send(dense_a, grad_plane)
         totals, sent, heat = routed_back(
-            layer, grad_plane, select, expert_up, expert_down, arrived, inner, scale
+            layer, grad_plane, select, expert_up, expert_down, arrived, inner, scale,
+            pieces[0] if pieces else None,
         )
         partial, dense_b, router_grad = shared_back(
             layer, grad_plane, mixed, back, router_full[layer], wide, shared_down, gates, sent, heat,
@@ -1073,26 +1109,29 @@
         after = far_sum(totals)
         reduced[layer] = after
         mixed_grad = reduce(partial, PLANE, 4)
+        if pieces:
+            pieces.append(near_sum(dense_a, arrivals, partial))
         gain_b_grad = jnp.sum(mixed_grad * normed_b, axis=0)
         middle_grad = grad + norm_back(mixed_grad * gains[1], normed_b, inverse_b)
         branch_grad = gather(middle_grad.astype(bf16), SLOT, 1)
         partial, dense_a = attend_back(
             branch_grad, hidden, project, cosine, sine, queries, keys, values, probs,
-            attended, out_padded[layer], spread,
+            attended, out_padded[layer], spread, pieces[1] if pieces else None,
         )
         hidden_grad = reduce(partial, SLOT, 3)
         gain_a_grad = jnp.sum(hidden_grad * normed_a, axis=0)
         grad = middle_grad + norm_back(hidden_grad * gains[0], normed_a, inverse_a)
-        pieces += [near_sum(dense_b), near_sum(dense_a)]
+        pieces.append(near_sum(dense_b, near_send(dense_b, mixed_grad), mixed_grad))
         first_rows = dense_b.shape[2]
         small_grads[layer] = jnp.concatenate(
             [router_grad[:experts], gain_a_grad[None], gain_b_grad[None]], axis=0
         )
-    dense = far_sum(jnp.concatenate(pieces, axis=1)).reshape(LAYERS, -1, 128)[::-1]
-    reduced = [(reduced[i], dense[i, :first_rows], dense[i, first_rows:]) for i in range(LAYERS)]
     grad, mixed = lax.optimization_barrier((grad, saved[-1][11]))
     wide, arrived, inner, scale, gates = saved[-1][12:]
     partial = finish(LAYERS - 1, mixed, back, inner, scale, expert_down, wide, shared_down, after)
+    pieces.append(near_sum(dense_a, near_send(dense_a, dense_a), partial))
+    dense = far_sum(jnp.concatenate(pieces, axis=1)).reshape(LAYERS, -1, 128)[::-1]
+    reduced = [(reduced[i], dense[i, :first_rows], dense[i, first_rows:]) for i in range(LAYERS)]
     block_out = (middle + reduce(partial, PLANE, 4)).astype(bf16)[None]
     small_all = lax.psum(jnp.stack(small_grads, axis=0), ("dp", "expert", "wshard"))
     small_own = lax.dynamic_slice_in_dim(small_all, shard * chunk, chunk, axis=2)

time: 570 us -> 559 us (0.981)
  Pallas kernels: 360 us -> 294 us
  local copies, waits for them, and re-layouts: 42.1 us -> 97.4 us
    unnamed x94 -> x296, local copies, waits for them, and re-layouts: 18.1 us -> 77.8 us
    pallas_call x11 -> x19, Pallas kernels: 151 us -> 111 us  [call(): pl.pallas_call(kernel, out_shape=tuple((jax.ShapeDtypeStruct(s, d) for s,...]
    pallas_call x8, Pallas kernels: 114 us -> 87.7 us  [reduce(): pl.pallas_call(functools.partial(reduce_kernel, axes), out_shape=jax.Shap...]
    reduce_scatter x3, waiting for transfers between devices: 0.01 us -> 20.1 us  [far_sum(): return lax.psum_scatter(piece, 'dp', scatter_dimension=0, tiled=True)[0]]
    ppermute x4, waiting for transfers between devices: 19.4 us -> 0.46 us  [near_send(): arrivals.append(lax.ppermute(pick(piece, k, after), 'expert', hop))]
    squeeze x4 -> x0, local copies, waits for them, and re-layouts: 7.62 us -> none  [part(): lax.dynamic_index_in_dim(piece, lax.rem(owner + k, owners), 0, keepdims=F...]
  transfers between devices with their start and end apart: 10 -> 10, of which waited for: 2 -> 4; matrix products, arithmetic and copies ran while one was open for 8% -> 6% of each run, Pallas kernels for 48% -> 39%
where the time goes in v3:
time: 559 us; the launch traced here: 549 us
  Pallas kernels  294 us (53%)
  local copies, waits for them, and re-layouts  97.4 us (17%)
  waiting for transfers between devices  50.6 us (9%)
  blocking collectives  46.4 us (8%)
  other arithmetic  25.9 us (5%)
  starting transfers between devices  18.4 us (3%)
  between operations  16.9 us (3%)
    pallas_call x19, Pallas kernels, call(): pl.pallas_call(kernel, out_shape=tuple((jax.ShapeDtypeStruct(s, d) for s,...  111 us
    pallas_call x8, Pallas kernels, reduce(): pl.pallas_call(functools.partial(reduce_kernel, axes), out_shape=jax.Shap...  87.7 us
    unnamed x296, local copies, waits for them, and re-layouts  77.8 us
    pallas_call x6, Pallas kernels, gather(): pl.pallas_call(functools.partial(gather_kernel, axes), out_shape=jax.Shap...  64 us
    psum x1, blocking collectives, per_device(): lax.psum(jnp.stack(small_grads, axis=0), ('dp', 'expert', 'wshard'))  46.4 us
    pallas_call x1, Pallas kernels, begin(): pl.pallas_call(functools.partial(begin_kernel, groups), out_shape=tuple(o...  31 us
    ppermute x1, waiting for transfers between devices, per_device(): turned = lax.ppermute(turned, ('dp', 'wshard'), transposed).astype(f32)  29.9 us
    reduce_scatter x3, waiting for transfers between devices, far_sum(): return lax.psum_scatter(piece, 'dp', scatter_dimension=0, tiled=True)[0]  20.1 us
  transfers between devices with their start and end apart: 10, of which 4 were waited for; matrix products, arithmetic and copies ran while one was open for 6% of the time, Pallas kernels for 39%

profile of v3, /device:TPU:4, one launch (start us, length us, event | category | flops | bytes accessed | tf_op | source)
XLA Modules:
  0.0 549.2 jit_solution(1051399891317309110)
XLA Ops:
  14.3 31.0 %shard_map.204 = (bf16[512,768]{1,0:T(8,128)(2,1)S(1)}, s32[64,128]{1,0:T(8,128)S(1)}, bf16[64,256]{1,0:T(8,128)(2,1)S(1)}, bf16[1024,768]{1,0:T(8,128)(2,1)S(1)}, bf16[3,768,256]{2,1,0:T(8,128)(2,1)S(1)}) custom-call(bf16[128,768]{1,0:T(8,128)(2,1)S(1)} %bitcast.138, s32[8,128]{1,0:T(8,128)S(1)} %concatenate.32.refs_1_, bf16[16,256]{1,0:T(8,128)(2,1)S(1)} %pad.7.refs_2_, ...), custom_call_target="tpu_custom_call" | custom-call | tf_op jit(solution)/shard_map/pallas_call | solution.py:852
  68.8 8.7 %shard_map.206 = f32[128,768]{1,0:T(8,128)S(1)} custom-call(bf16[512,768]{1,0:T(8,128)(2,1)S(1)} %get-tuple-element.74.p_ref), custom_call_target="tpu_custom_call" | custom-call | tf_op jit(solution)/shard_map/pallas_call | solution.py:906
  78.5 13.5 %shard_map.207.mixed = bf16[1024,768]{1,0:T(8,128)(2,1)S(1)} custom-call(bf16[128,768]{1,0:T(8,128)(2,1)S(1)} %multiply_convert_fusion.2.x_ref), custom_call_target="tpu_custom_call" | custom-call | tf_op jit(solution)/shard_map/pallas_call | solution.py:787
  116.0 16.0 %shard_map.208 = (bf16[1024,768]{1,0:T(8,128)(2,1)S(1)}, bf16[2,640,768]{2,1,0:T(8,128)(2,1)S(1)}, bf16[2,640,1024]{2,1,0:T(8,128)(2,1)S(1)}, f32[2,640,1]{2,1,0:T(8,128)S(1)}, f32[1024,128]{1,0:T(8,128)S(1)}) custom-call(bf16[1024,768]{1,0:T(8,128)(2,1)S(1)} %copy-done.22, bf16[8,160,128]{2,1,0:T(8,128)(2,1)S(1)} %fusion.3.select, ...), custom_call_target="tpu_custom_call" | custom-call | tf_op jit(solution)/shard_map/pallas_call | solution.py:64
  134.2 13.9 %shard_map.209 = f32[128,768]{1,0:T(8,128)S(1)} custom-call(bf16[1024,768]{1,0:T(8,128)(2,1)S(1)} %get-tuple-element.78.p_ref), custom_call_target="tpu_custom_call" | custom-call | tf_op jit(solution)/shard_map/pallas_call | solution.py:906
  169.9 8.7 %shard_map.212 = f32[128,768]{1,0:T(8,128)S(1)} custom-call(bf16[512,768]{1,0:T(8,128)(2,1)S(1)} %get-tuple-element.80.p_ref), custom_call_target="tpu_custom_call" | custom-call | tf_op jit(solution)/shard_map/pallas_call | solution.py:906
  178.8 13.2 %shard_map.213.mixed = bf16[1024,768]{1,0:T(8,128)(2,1)S(1)} custom-call(bf16[128,768]{1,0:T(8,128)(2,1)S(1)} %multiply_convert_fusion.x_ref), custom_call_target="tpu_custom_call" | custom-call | tf_op jit(solution)/shard_map/pallas_call | solution.py:787
  192.1 8.5 %shard_map.214 = (bf16[2,640,768]{2,1,0:T(8,128)(2,1)S(1)}, bf16[2,640,1024]{2,1,0:T(8,128)(2,1)S(1)}, f32[2,640,1]{2,1,0:T(8,128)S(1)}, f32[1024,128]{1,0:T(8,128)S(1)}) custom-call(bf16[1024,768]{1,0:T(8,128)(2,1)S(1)} %shard_map.213.mixed, bf16[8,160,128]{2,1,0:T(8,128)(2,1)S(1)} %fusion.3.select, f32[1024,128]{1,0:T(8,128)S(1)} %copy-done.55, ...), custom_call_target="tpu_custom_call" | custom-call | tf_op jit(solution)/shard_map/pallas_call | solution.py:64
  200.7 12.9 %shard_map.215 = (bf16[4,2,3,192,512]{4,3,2,1,0:T(8,128)(2,1)S(1)}, bf16[8,160,768]{2,1,0:T(8,128)(2,1)S(1)}, f32[8,160,128]{2,1,0:T(8,128)S(1)}) custom-call(bf16[1024,768]{1,0:T(8,128)(2,1)S(1)} %copy-done.47, bf16[8,160,128]{2,1,0:T(8,128)(2,1)S(1)} %fusion.3.select, bf16[2,2,2,768,512]{4,3,2,1,0:T(8,128)(2,1)} %far_up.7, ...), custom_call_target="tpu_custom_call" | custom-call | tf_op jit(solution)/shard_map/pallas_call | solution.py:64
  227.2 11.3 %shard_map.216 = (bf16[1024,768]{1,0:T(8,128)(2,1)S(1)}, bf16[2,4,1280,128]{3,2,1,0:T(8,128)(2,1)S(1)}, f32[128,768]{1,0:T(8,128)S(1)}) custom-call(bf16[1024,768]{1,0:T(8,128)(2,1)S(1)} %copy-done.48, bf16[1024,768]{1,0:T(8,128)(2,1)S(1)} %copy-done.12, bf16[8,128,160]{2,1,0:T(8,128)(2,1)S(1)} %copy-done.25, bf16[128,768]{1,0:T(8,128)(2,1)S(1)} %copy-done.90, ...), custom_call_target="tpu_custom_call" | custom-call | tf_op jit(solution)/shard_map/pallas_call | solution.py:64
  238.5 13.9 %shard_map.217.after = f32[128,768]{1,0:T(8,128)S(1)} custom-call(bf16[1024,768]{1,0:T(8,128)(2,1)S(1)} %get-tuple-element.88.p_ref), custom_call_target="tpu_custom_call" | custom-call | tf_op jit(solution)/shard_map/pallas_call | solution.py:906
  263.2 8.7 %shard_map.219 = (bf16[512,768]{1,0:T(8,128)(2,1)S(1)}, bf16[2,4,768,128]{3,2,1,0:T(8,128)(2,1)S(1)}) custom-call(bf16[512,768]{1,0:T(8,128)(2,1)S(1)} %shard_map.218.grad, bf16[512,768]{1,0:T(8,128)(2,1)S(1)} %copy-done.37, bf16[4,4,192,512]{3,2,1,0:T(8,128)(2,1)} %all-to-all-done.1.source.far_wide.near, f32[512,128]{1,0:T(8,128)S(1)} %copy-done.44, ...), custom_call_target="tpu_custom_call" | custom-call | tf_op jit(solution)/shard_map/pallas_call | solution.py:64
  273.1 8.7 %shard_map.220 = f32[128,768]{1,0:T(8,128)S(1)} custom-call(bf16[512,768]{1,0:T(8,128)(2,1)S(1)} %get-tuple-element.94.p_ref), custom_call_target="tpu_custom_call" | custom-call | tf_op jit(solution)/shard_map/pallas_call | solution.py:906
  283.0 13.2 %shard_map.221.grad.after = bf16[1024,768]{1,0:T(8,128)(2,1)S(1)} custom-call(bf16[128,768]{1,0:T(8,128)(2,1)S(1)} %get-tuple-element.132.x_ref), custom_call_target="tpu_custom_call" | custom-call | tf_op jit(solution)/shard_map/pallas_call | solution.py:787
  299.2 11.5 %shard_map.224 = (bf16[4,2,3,192,512]{4,3,2,1,0:T(8,128)(2,1)S(1)}, bf16[8,160,768]{2,1,0:T(8,128)(2,1)S(1)}, f32[8,160,128]{2,1,0:T(8,128)S(1)}) custom-call(bf16[1024,768]{1,0:T(8,128)(2,1)S(1)} %shard_map.221.grad.after, bf16[8,160,128]{2,1,0:T(8,128)(2,1)S(1)} %fusion.3.select, bf16[2,2,2,768,512]{4,3,2,1,0:T(8,128)(2,1)} %far_up.7, ...), custom_call_target="tpu_custom_call" | custom-call | tf_op jit(solution)/shard_map/pallas_call | solution.py:64
  332.1 11.8 %shard_map.225 = (bf16[1024,768]{1,0:T(8,128)(2,1)S(1)}, bf16[2,4,1280,128]{3,2,1,0:T(8,128)(2,1)S(1)}, f32[128,768]{1,0:T(8,128)S(1)}) custom-call(bf16[1024,768]{1,0:T(8,128)(2,1)S(1)} %copy-done.10, bf16[1024,768]{1,0:T(8,128)(2,1)S(1)} %copy-done.23, bf16[8,128,160]{2,1,0:T(8,128)(2,1)S(1)} %copy-done.26, bf16[128,768]{1,0:T(8,128)(2,1)S(1)} %copy-done.88, ...), custom_call_target="tpu_custom_call" | custom-call | tf_op jit(solution)/shard_map/pallas_call | solution.py:64
  344.8 13.8 %shard_map.226.after = f32[128,768]{1,0:T(8,128)S(1)} custom-call(bf16[1024,768]{1,0:T(8,128)(2,1)S(1)} %get-tuple-element.103.p_ref.after), custom_call_target="tpu_custom_call" | custom-call | tf_op jit(solution)/shard_map/pallas_call | solution.py:906
  359.0 8.2 %shard_map.227.grad = bf16[512,768]{1,0:T(8,128)(2,1)S(1)} custom-call(bf16[128,768]{1,0:T(8,128)(2,1)S(1)} %get-tuple-element.130.x_ref), custom_call_target="tpu_custom_call" | custom-call | tf_op jit(solution)/shard_map/pallas_call | solution.py:787
  371.0 9.2 %shard_map.230 = (bf16[512,768]{1,0:T(8,128)(2,1)S(1)}, bf16[2,4,768,128]{3,2,1,0:T(8,128)(2,1)S(1)}) custom-call(bf16[512,768]{1,0:T(8,128)(2,1)S(1)} %shard_map.227.grad, bf16[512,768]{1,0:T(8,128)(2,1)S(1)} %copy-done.33, bf16[3,768,256]{2,1,0:T(8,128)(2,1)S(1)} %copy-done.61, f32[512,128]{1,0:T(8,128)S(1)} %copy-done.45, f32[512,128]{1,0:T(8,128)S(1)} %copy-done.41, ...), custom_call_target="tpu_custom_call" | custom-call | tf_op jit(solution)/shard_map/pallas_call | solution.py:64
  383.8 8.4 %shard_map.231 = f32[128,768]{1,0:T(8,128)S(1)} custom-call(bf16[512,768]{1,0:T(8,128)(2,1)S(1)} %get-tuple-element.110.p_ref), custom_call_target="tpu_custom_call" | custom-call | tf_op jit(solution)/shard_map/pallas_call | solution.py:906
  424.0 46.4 %psum.7 = f32[2,6,768]{2,1,0:T(8,128)S(1)} all-reduce(f32[2,6,768]{2,1,0:T(8,128)S(1)} %pad_maximum_fusion.4), channel_id=1, replica_groups=mesh['dp'=4,'expert'=2,'wshard'=4] {'dp','expert','wshard'}, use_global_device_ids=true, to_apply=%region_17.18 | all-reduce | flops 9216 | bytes 73728 | tf_op jit(solution)/shard_map/psum | solution.py:1136
  471.8 11.7 %shard_map.233 = f32[128,768]{1,0:T(8,128)S(1)} custom-call(bf16[1024,768]{1,0:T(8,128)(2,1)S(1)} %copy-done.17), custom_call_target="tpu_custom_call" | custom-call | tf_op jit(solution)/shard_map/pallas_call | solution.py:906
  488.7 12.3 %reduce-scatter.8.cloned.1.call-done = bf16[1,4096,128]{2,1,0:T(8,128)(2,1)} async-done(((bf16[4,4096,128]{2,1,0:T(8,128)(2,1)}), bf16[1,4096,128]{2,1,0:T(8,128)(2,1)}) %reduce-scatter.8.cloned.1.call-update) | async-done | bytes 1048592 | tf_op jit(solution)/shard_map/reduce_scatter | solution.py:1088
  509.3 29.9 %collective-permute-done.4 = bf16[2,1344,128]{2,1,0:T(8,128)(2,1)S(1)} collective-permute-done((bf16[2,1344,128]{2,1,0:T(8,128)(2,1)S(1)}, bf16[2,1344,128]{2,1,0:T(8,128)(2,1)S(1)}, u32[]{:S(2)}, u32[]{:S(2)}) %collective-permute-start.4) | collective-permute-done | bytes 688160 | tf_op jit(solution)/shard_map/ppermute | solution.py:1145
  (441 shorter events, 187.1 us)
Async XLA Ops:
  47.5 47.5 %all-to-all-start = ((bf16[4,2,192,512]{3,2,1,0:T(8,128)(2,1)}), bf16[4,2,192,512]{3,2,1,0:T(8,128)(2,1)S(1)}, u32[]{:S(2)}, u32[]{:S(2)}) async-start(bf16[4,2,192,512]{3,2,1,0:T(8,128)(2,1)} %pad_maximum_fusion.1), calls=%async_computation | async-start | bytes 3145728 | tf_op jit(solution)/shard_map/all_to_all | solution.py:1004
  56.2 45.4 %copy-start.139 = (bf16[2,6,768]{2,1,0:T(8,128)(2,1)}, bf16[2,6,768]{2,1,0:T(8,128)(2,1)S(1)}, u32[]{:S(2)}) copy-start(bf16[2,6,768]{2,1,0:T(8,128)(2,1)S(1)} %reshape.258) | copy-start | bytes 55300
  78.0 15.1 %copy-start.134 = (bf16[1,2,192,512]{3,2,1,0:T(8,128)(2,1)S(1)}, bf16[1,2,192,512]{3,2,1,0:T(8,128)(2,1)}, u32[]{:S(2)}) copy-start(bf16[1,2,192,512]{3,2,1,0:T(8,128)(2,1)} %get-tuple-element.142) | copy-start | bytes 1179652
  78.0 15.1 %copy-start.135 = (bf16[1,2,192,512]{3,2,1,0:T(8,128)(2,1)S(1)}, bf16[1,2,192,512]{3,2,1,0:T(8,128)(2,1)}, u32[]{:S(2)}) copy-start(bf16[1,2,192,512]{3,2,1,0:T(8,128)(2,1)} %get-tuple-element.143) | copy-start | bytes 1179652
  96.1 61.1 %all-to-all-start.1 = ((bf16[4,4,192,512]{3,2,1,0:T(8,128)(2,1)}), bf16[4,4,192,512]{3,2,1,0:T(8,128)(2,1)}, u32[]{:S(2)}, u32[]{:S(2)}) async-start(bf16[4,4,192,512]{3,2,1,0:T(8,128)(2,1)} %maximum_maximum_fusion), calls=%async_computation.1 | async-start | bytes 6291456 | tf_op jit(solution)/shard_map/all_to_all | solution.py:1004
  101.4 218.6 %reduce-scatter.4.cloned.1.call-start = ((), (), s32[]{:S(2)}) async-start(), calls=%async_computation.5 | async-start | bytes 5898240 | tf_op jit(solution)/shard_map/reduce_scatter | solution.py:1088
  106.9 25.1 %copy-start.87 = (bf16[128,768]{1,0:T(8,128)(2,1)}, bf16[128,768]{1,0:T(8,128)(2,1)S(1)}, u32[]{:S(2)}) copy-start(bf16[128,768]{1,0:T(8,128)(2,1)S(1)} %get-tuple-element.173.router) | copy-start | bytes 589828
  107.3 24.7 %copy-start.54 = (f32[1024,128]{1,0:T(8,128)}, f32[1024,128]{1,0:T(8,128)S(1)}, u32[]{:S(2)}) copy-start(f32[1024,128]{1,0:T(8,128)S(1)} %or_select_fusion.chosen) | copy-start | bytes 1572868
  108.8 23.2 %copy-start.24 = (bf16[8,128,160]{2,1,0:T(8,128)(2,1)}, bf16[8,128,160]{2,1,0:T(8,128)(2,1)S(1)}, u32[]{:S(2)}) copy-start(bf16[8,128,160]{2,1,0:T(8,128)(2,1)S(1)} %compare_convert_fusion.back) | copy-start | bytes 983044
  148.1 44.0 %slice-start = ((s8[6291456]{0:T(1024)(128)(4,1)}), s8[2097152]{0:T(1024)(128)(4,1)S(1)}, s32[]{:S(2)}) async-start(s8[6291456]{0:T(1024)(128)(4,1)} %bitcast.134), calls=%async_computation.8 | async-start | bytes 4194304
  159.4 19.2 %copy-start.128 = (f32[128,768]{1,0:T(8,128)S(1)}, f32[128,768]{1,0:T(8,128)}, u32[]{:S(2)}) copy-start(f32[128,768]{1,0:T(8,128)} %copy-done.127) | copy-start | bytes 1179652
  159.4 32.7 %slice-start.1 = ((s8[6291456]{0:T(1024)(128)(4,1)}), s8[4194304]{0:T(1024)(128)(4,1)S(1)}, s32[]{:S(2)}) async-start(s8[6291456]{0:T(1024)(128)(4,1)} %bitcast.134), calls=%async_computation.9 | async-start | bytes 8388608
  218.1 183.2 %reduce-scatter.6.cloned.1.call-start = ((), (), s32[]{:S(2)}) async-start(), calls=%async_computation.6 | async-start | bytes 5898240 | tf_op jit(solution)/shard_map/reduce_scatter | solution.py:1088
  252.6 43.7 %collective-permute-start = (bf16[4,1280,128]{2,1,0:T(8,128)(2,1)S(1)}, bf16[4,1280,128]{2,1,0:T(8,128)(2,1)S(1)}, u32[]{:S(2)}, u32[]{:S(2)}) collective-permute-start(bf16[4,1280,128]{2,1,0:T(8,128)(2,1)S(1)} %shard_map.223), channel_id=1, source_target_pairs={{0,4},{4,0},{1,5},{5,1},{2,6},{6,2},{3,7},{7,3},{8,12},{12,8},{9,1... | collective-permute-start | bytes 3932168 | tf_op jit(solution)/shard_map/ppermute | solution.py:1078
  263.2 18.6 %copy-start.129 = (f32[128,768]{1,0:T(8,128)S(1)}, f32[128,768]{1,0:T(8,128)}, u32[]{:S(2)}) copy-start(f32[128,768]{1,0:T(8,128)} %copy-done.127) | copy-start | bytes 1179652
  281.8 15.7 %copy-start.94 = (f32[2,640,1]{2,1,0:T(8,128)S(1)}, f32[2,640,1]{2,1,0:T(8,128)}, u32[]{:S(2)}) copy-start(f32[2,640,1]{2,1,0:T(8,128)} %copy-done.93) | copy-start | bytes 15364
  282.0 15.4 %copy-start.76 = (bf16[2,640,1024]{2,1,0:T(8,128)(2,1)S(1)}, bf16[2,640,1024]{2,1,0:T(8,128)(2,1)}, u32[]{:S(2)}) copy-start(bf16[2,640,1024]{2,1,0:T(8,128)(2,1)} %copy-done.75) | copy-start | bytes 7864324
  315.1 185.8 %reduce-scatter.8.cloned.1.call-start = ((), (), s32[]{:S(2)}) async-start(), calls=%async_computation.7 | async-start | bytes 5242880 | tf_op jit(solution)/shard_map/reduce_scatter | solution.py:1088
  318.9 50.6 %collective-permute-start.1 = (bf16[4,768,128]{2,1,0:T(8,128)(2,1)}, bf16[4,768,128]{2,1,0:T(8,128)(2,1)}, u32[]{:S(2)}, u32[]{:S(2)}) collective-permute-start(bf16[4,768,128]{2,1,0:T(8,128)(2,1)} %shard_map.229), channel_id=1, source_target_pairs={{0,4},{4,0},{1,5},{5,1},{2,6},{6,2},{3,7},{7,3},{8,12},{12,8},{9,1... | collective-permute-start | bytes 2359304 | tf_op jit(solution)/shard_map/ppermute | solution.py:1078
  368.5 49.7 %collective-permute-start.2 = (bf16[4,1280,128]{2,1,0:T(8,128)(2,1)}, bf16[4,1280,128]{2,1,0:T(8,128)(2,1)}, u32[]{:S(2)}, u32[]{:S(2)}) collective-permute-start(bf16[4,1280,128]{2,1,0:T(8,128)(2,1)} %shard_map.235), channel_id=1, source_target_pairs={{0,4},{4,0},{1,5},{5,1},{2,6},{6,2},{3,7},{7,3},{8,12},{12,8},{9,1... | collective-permute-start | bytes 3932168 | tf_op jit(solution)/shard_map/ppermute | solution.py:1078
  381.6 35.2 %collective-permute-start.3 = (bf16[4,768,128]{2,1,0:T(8,128)(2,1)}, bf16[4,768,128]{2,1,0:T(8,128)(2,1)}, u32[]{:S(2)}, u32[]{:S(2)}) collective-permute-start(bf16[4,768,128]{2,1,0:T(8,128)(2,1)} %shard_map.237), channel_id=1, source_target_pairs={{0,4},{4,0},{1,5},{5,1},{2,6},{6,2},{3,7},{7,3},{8,12},{12,8},{9,1... | collective-permute-start | bytes 2359304 | tf_op jit(solution)/shard_map/ppermute | solution.py:1078
  422.2 49.6 %copy-start.17 = (bf16[1024,768]{1,0:T(8,128)(2,1)S(1)}, bf16[1024,768]{1,0:T(8,128)(2,1)}, u32[]{:S(2)}) copy-start(bf16[1024,768]{1,0:T(8,128)(2,1)} %copy-done.16) | copy-start | bytes 4718596
  422.2 61.2 %copy-start.63 = (bf16[1,2,3,192,512]{4,3,2,1,0:T(8,128)(2,1)S(1)}, bf16[1,2,3,192,512]{4,3,2,1,0:T(8,128)(2,1)}, u32[]{:S(2)}) copy-start(bf16[1,2,3,192,512]{4,3,2,1,0:T(8,128)(2,1)} %reduce-scatter.6.cloned.1.call-done) | copy-start | bytes 3538948
  503.0 36.2 %collective-permute-start.4 = (bf16[2,1344,128]{2,1,0:T(8,128)(2,1)S(1)}, bf16[2,1344,128]{2,1,0:T(8,128)(2,1)S(1)}, u32[]{:S(2)}, u32[]{:S(2)}) collective-permute-start(bf16[2,1344,128]{2,1,0:T(8,128)(2,1)S(1)} %pad_maximum_fusion.3), channel_id=1, source_target_pairs={{0,0},{1,8},{2,16},{3,24},{8,1},{9,9},{10,17},{11,25},{16,2},{17,1... | collective-permute-start | bytes 2064392 | tf_op jit(solution)/shard_map/ppermute | solution.py:1145
  (133 other events, 589.8 us)
Sparse Core Ops, SparseCore 0:
  218.2 85.9 reduce-scatter.3
  315.2 85.9 reduce-scatter.5
  422.4 78.5 reduce-scatter.7

commit v4 on v3

--- a/solution.py
+++ b/solution.py
@@ -54,11 +54,11 @@
     return total
 
 
-def call(kernel, outs, scratch, *operands):
+def call(kernel, outs, scratch, *operands, alone=False):
     need = sum(held_bytes(s, d) for s, d in outs)
     need += sum(held_bytes(*s) for s in scratch if isinstance(s, tuple))
     need += sum(held_bytes(o.shape, o.dtype) for o in operands if not isinstance(o, Far))
-    limit = min(VMEM_MOST, need + VMEM_SLACK)
+    limit = VMEM_MOST if alone else min(VMEM_MOST, need + VMEM_SLACK)
     vmem = pl.BlockSpec(memory_space=pltpu.VMEM)
     far = pl.BlockSpec(memory_space=pltpu.HBM)
     return pl.pallas_call(
@@ -420,7 +420,7 @@
 
 
 def finish_kernel(
-    layer, mixed, back, inner, scale, far_down, far_wide, far_narrow, after,
+    layer, mixed, back, inner, scale, far_down, far_wide, far_narrow, after, near,
     partial,
     sent, shared_out, down, wide, narrow, sems, wide_sems,
 ):
@@ -447,7 +447,7 @@
     finish_part(mixed, back, wide, narrow, partial, sent, shared_out)
 
 
-def finish(layer, mixed, back, inner, scale, down, wide, narrow, after):
+def finish(layer, mixed, back, inner, scale, down, wide, narrow, after, near):
     group, rows, spots = back.shape
     width = mixed.shape[1]
     units = down.shape[2]
@@ -464,7 +464,8 @@
             DMA((2,)),
             DMA((8,)),
         ],
-        mixed, back, inner, scale, Far(down), Far(wide), Far(narrow), Far(after),
+        mixed, back, inner, scale, Far(down), Far(wide), Far(narrow), Far(after), Far(near),
+        alone=True,
     )[0]
 
 
@@ -649,7 +650,7 @@
             DMA((8,)),
         ],
         grad, mixed, back, router, Far(wide), Far(narrow), gates, sent, spot,
-        Far(narrow if after is None else after),
+        Far(narrow if after is None else after), alone=True,
     )
 
 
@@ -1128,7 +1129,9 @@
         )
     grad, mixed = lax.optimization_barrier((grad, saved[-1][11]))
     wide, arrived, inner, scale, gates = saved[-1][12:]
-    partial = finish(LAYERS - 1, mixed, back, inner, scale, expert_down, wide, shared_down, after)
+    partial = finish(
+        LAYERS - 1, mixed, back, inner, scale, expert_down, wide, shared_down, after, pieces[-1]
+    )
     pieces.append(near_sum(dense_a, near_send(dense_a, dense_a), partial))
     dense = far_sum(jnp.concatenate(pieces, axis=1)).reshape(LAYERS, -1, 128)[::-1]
     reduced = [(reduced[i], dense[i, :first_rows], dense[i, first_rows:]) for i in range(LAYERS)]

time: 559 us -> 553 us (0.989)
  local copies, waits for them, and re-layouts: 97.4 us -> 71.4 us
  Pallas kernels: 294 us -> 307 us
  waiting for transfers between devices: 50.6 us -> 60.2 us
    unnamed x296 -> x238, local copies, waits for them, and re-layouts: 77.8 us -> 51.8 us
    pallas_call x19, Pallas kernels: 111 us -> 124 us  [call(): pl.pallas_call(kernel, out_shape=tuple((jax.ShapeDtypeStruct(s, d) for s,...]
    reduce_scatter x3, waiting for transfers between devices: 20.1 us -> 28.7 us  [far_sum(): return lax.psum_scatter(piece, 'dp', scatter_dimension=0, tiled=True)[0]]
  transfers between devices with their start and end apart: 10 -> 10, of which waited for: 4 -> 4; matrix products, arithmetic and copies ran while one was open for 6% -> 6% of each run, Pallas kernels for 39% -> 42%
where the time goes in v4:
time: 553 us; the launch traced here: 544 us
  Pallas kernels  307 us (56%)
  local copies, waits for them, and re-layouts  71.4 us (13%)
  waiting for transfers between devices  60.2 us (11%)
  blocking collectives  46.2 us (8%)
  other arithmetic  24.4 us (4%)
  starting transfers between devices  18.6 us (3%)
  between operations  16.7 us (3%)
    pallas_call x19, Pallas kernels, call(): pl.pallas_call(kernel, out_shape=tuple((jax.ShapeDtypeStruct(s, d) for s,...  124 us
    pallas_call x8, Pallas kernels, reduce(): pl.pallas_call(functools.partial(reduce_kernel, axes), out_shape=jax.Shap...  87.9 us
    pallas_call x6, Pallas kernels, gather(): pl.pallas_call(functools.partial(gather_kernel, axes), out_shape=jax.Shap...  63.7 us
    unnamed x238, local copies, waits for them, and re-layouts  51.8 us
    psum x1, blocking collectives, per_device(): lax.psum(jnp.stack(small_grads, axis=0), ('dp', 'expert', 'wshard'))  46.2 us
    pallas_call x1, Pallas kernels, begin(): pl.pallas_call(functools.partial(begin_kernel, groups), out_shape=tuple(o...  31 us
    ppermute x1, waiting for transfers between devices, per_device(): turned = lax.ppermute(turned, ('dp', 'wshard'), transposed).astype(f32)  29.9 us
    reduce_scatter x3, waiting for transfers between devices, far_sum(): return lax.psum_scatter(piece, 'dp', scatter_dimension=0, tiled=True)[0]  28.7 us
  transfers between devices with their start and end apart: 10, of which 4 were waited for; matrix products, arithmetic and copies ran while one was open for 6% of the time, Pallas kernels for 42%

profile of v4, /device:TPU:4, one launch (start us, length us, event | category | flops | bytes accessed | tf_op | source)
XLA Modules:
  0.0 544.4 jit_solution(293356634915106474)
XLA Ops:
  14.4 31.0 %shard_map.204 = (bf16[512,768]{1,0:T(8,128)(2,1)S(1)}, s32[64,128]{1,0:T(8,128)S(1)}, bf16[64,256]{1,0:T(8,128)(2,1)S(1)}, bf16[1024,768]{1,0:T(8,128)(2,1)S(1)}, bf16[3,768,256]{2,1,0:T(8,128)(2,1)S(1)}) custom-call(bf16[128,768]{1,0:T(8,128)(2,1)S(1)} %bitcast.136, s32[8,128]{1,0:T(8,128)S(1)} %concatenate.32.refs_1_, bf16[16,256]{1,0:T(8,128)(2,1)S(1)} %pad.7.refs_2_, ...), custom_call_target="tpu_custom_call" | custom-call | tf_op jit(solution)/shard_map/pallas_call | solution.py:853
  68.8 8.7 %shard_map.206 = f32[128,768]{1,0:T(8,128)S(1)} custom-call(bf16[512,768]{1,0:T(8,128)(2,1)S(1)} %get-tuple-element.74.p_ref), custom_call_target="tpu_custom_call" | custom-call | tf_op jit(solution)/shard_map/pallas_call | solution.py:907
  78.4 13.4 %shard_map.207.mixed = bf16[1024,768]{1,0:T(8,128)(2,1)S(1)} custom-call(bf16[128,768]{1,0:T(8,128)(2,1)S(1)} %multiply_convert_fusion.2.x_ref), custom_call_target="tpu_custom_call" | custom-call | tf_op jit(solution)/shard_map/pallas_call | solution.py:788
  116.0 16.0 %shard_map.208 = (bf16[1024,768]{1,0:T(8,128)(2,1)S(1)}, bf16[2,640,768]{2,1,0:T(8,128)(2,1)S(1)}, bf16[2,640,1024]{2,1,0:T(8,128)(2,1)S(1)}, f32[2,640,1]{2,1,0:T(8,128)S(1)}, f32[1024,128]{1,0:T(8,128)S(1)}) custom-call(bf16[1024,768]{1,0:T(8,128)(2,1)S(1)} %copy-done.13, bf16[8,160,128]{2,1,0:T(8,128)(2,1)S(1)} %fusion.3.select, ...), custom_call_target="tpu_custom_call" | custom-call | tf_op jit(solution)/shard_map/pallas_call | solution.py:64
  134.1 13.9 %shard_map.209 = f32[128,768]{1,0:T(8,128)S(1)} custom-call(bf16[1024,768]{1,0:T(8,128)(2,1)S(1)} %get-tuple-element.78.p_ref), custom_call_target="tpu_custom_call" | custom-call | tf_op jit(solution)/shard_map/pallas_call | solution.py:907
  169.5 8.7 %shard_map.212 = f32[128,768]{1,0:T(8,128)S(1)} custom-call(bf16[512,768]{1,0:T(8,128)(2,1)S(1)} %get-tuple-element.80.p_ref), custom_call_target="tpu_custom_call" | custom-call | tf_op jit(solution)/shard_map/pallas_call | solution.py:907
  178.4 13.2 %shard_map.213.mixed = bf16[1024,768]{1,0:T(8,128)(2,1)S(1)} custom-call(bf16[128,768]{1,0:T(8,128)(2,1)S(1)} %multiply_convert_fusion.x_ref), custom_call_target="tpu_custom_call" | custom-call | tf_op jit(solution)/shard_map/pallas_call | solution.py:788
  200.3 12.9 %shard_map.215 = (bf16[4,2,3,192,512]{4,3,2,1,0:T(8,128)(2,1)S(1)}, bf16[8,160,768]{2,1,0:T(8,128)(2,1)S(1)}, f32[8,160,128]{2,1,0:T(8,128)S(1)}) custom-call(bf16[1024,768]{1,0:T(8,128)(2,1)S(1)} %copy-done.31, bf16[8,160,128]{2,1,0:T(8,128)(2,1)S(1)} %fusion.3.select, bf16[2,2,2,768,512]{4,3,2,1,0:T(8,128)(2,1)} %far_up.7, ...), custom_call_target="tpu_custom_call" | custom-call | tf_op jit(solution)/shard_map/pallas_call | solution.py:64
  217.7 16.1 %shard_map.216 = (bf16[1024,768]{1,0:T(8,128)(2,1)}, bf16[2,4,1280,128]{3,2,1,0:T(8,128)(2,1)}, f32[128,768]{1,0:T(8,128)}) custom-call(bf16[1024,768]{1,0:T(8,128)(2,1)} %copy-done.30, bf16[1024,768]{1,0:T(8,128)(2,1)} %copy-done.5, bf16[8,128,160]{2,1,0:T(8,128)(2,1)} %copy-done.14, bf16[128,768]{1,0:T(8,128)(2,1)} %get-tuple-element.172.router, ...), custom_call_target="tpu_custom_call" | custom-call | tf_op jit(solution)/shard_map/pallas_call | solution.py:64
  235.3 13.9 %shard_map.217.after = f32[128,768]{1,0:T(8,128)S(1)} custom-call(bf16[1024,768]{1,0:T(8,128)(2,1)S(1)} %copy-done.64), custom_call_target="tpu_custom_call" | custom-call | tf_op jit(solution)/shard_map/pallas_call | solution.py:907
  262.3 8.7 %shard_map.219 = (bf16[512,768]{1,0:T(8,128)(2,1)S(1)}, bf16[2,4,768,128]{3,2,1,0:T(8,128)(2,1)S(1)}) custom-call(bf16[512,768]{1,0:T(8,128)(2,1)S(1)} %shard_map.218.grad, bf16[512,768]{1,0:T(8,128)(2,1)S(1)} %shard_map.210.hidden, bf16[4,4,192,512]{3,2,1,0:T(8,128)(2,1)} %all-to-all-done.1.source.far_wide.near, f32[512,128]{1,0:T(8,128)S(1)} %copy-done.28, ...), custom_call_target="tpu_custom_call" | custom-call | tf_op jit(solution)/shard_map/pallas_call | solution.py:64
  272.2 8.7 %shard_map.220 = f32[128,768]{1,0:T(8,128)S(1)} custom-call(bf16[512,768]{1,0:T(8,128)(2,1)S(1)} %get-tuple-element.94.p_ref), custom_call_target="tpu_custom_call" | custom-call | tf_op jit(solution)/shard_map/pallas_call | solution.py:907
  282.1 13.1 %shard_map.221.grad.after = bf16[1024,768]{1,0:T(8,128)(2,1)S(1)} custom-call(bf16[128,768]{1,0:T(8,128)(2,1)S(1)} %get-tuple-element.132.x_ref), custom_call_target="tpu_custom_call" | custom-call | tf_op jit(solution)/shard_map/pallas_call | solution.py:788
  298.2 11.5 %shard_map.224 = (bf16[4,2,3,192,512]{4,3,2,1,0:T(8,128)(2,1)S(1)}, bf16[8,160,768]{2,1,0:T(8,128)(2,1)S(1)}, f32[8,160,128]{2,1,0:T(8,128)S(1)}) custom-call(bf16[1024,768]{1,0:T(8,128)(2,1)S(1)} %shard_map.221.grad.after, bf16[8,160,128]{2,1,0:T(8,128)(2,1)S(1)} %fusion.3.select, bf16[2,2,2,768,512]{4,3,2,1,0:T(8,128)(2,1)} %far_up.7, ...), custom_call_target="tpu_custom_call" | custom-call | tf_op jit(solution)/shard_map/pallas_call | solution.py:64
  318.1 16.6 %shard_map.225 = (bf16[1024,768]{1,0:T(8,128)(2,1)}, bf16[2,4,1280,128]{3,2,1,0:T(8,128)(2,1)}, f32[128,768]{1,0:T(8,128)}) custom-call(bf16[1024,768]{1,0:T(8,128)(2,1)} %copy-done.6, bf16[1024,768]{1,0:T(8,128)(2,1)} %copy-done.12, bf16[8,128,160]{2,1,0:T(8,128)(2,1)} %copy-done.14, bf16[128,768]{1,0:T(8,128)(2,1)} %copy-done.62, ...), custom_call_target="tpu_custom_call" | custom-call | tf_op jit(solution)/shard_map/pallas_call | solution.py:64
  337.7 13.9 %shard_map.226.after = f32[128,768]{1,0:T(8,128)S(1)} custom-call(bf16[1024,768]{1,0:T(8,128)(2,1)S(1)} %copy-done.35), custom_call_target="tpu_custom_call" | custom-call | tf_op jit(solution)/shard_map/pallas_call | solution.py:907
  361.8 9.2 %shard_map.230 = (bf16[512,768]{1,0:T(8,128)(2,1)S(1)}, bf16[2,4,768,128]{3,2,1,0:T(8,128)(2,1)S(1)}) custom-call(bf16[512,768]{1,0:T(8,128)(2,1)S(1)} %shard_map.227.grad, bf16[512,768]{1,0:T(8,128)(2,1)S(1)} %copy-done.22, bf16[3,768,256]{2,1,0:T(8,128)(2,1)S(1)} %copy-done.41, f32[512,128]{1,0:T(8,128)S(1)} %copy-done.29, f32[512,128]{1,0:T(8,128)S(1)} %copy-done.25, ...), custom_call_target="tpu_custom_call" | custom-call | tf_op jit(solution)/shard_map/pallas_call | solution.py:64
  370.9 8.7 %shard_map.231 = f32[128,768]{1,0:T(8,128)S(1)} custom-call(bf16[512,768]{1,0:T(8,128)(2,1)S(1)} %get-tuple-element.110.p_ref), custom_call_target="tpu_custom_call" | custom-call | tf_op jit(solution)/shard_map/pallas_call | solution.py:907
  384.8 15.6 %reduce-scatter.6.cloned.1.call-done = bf16[1,2,3,192,512]{4,3,2,1,0:T(8,128)(2,1)} async-done(((bf16[4,2,3,192,512]{4,3,2,1,0:T(8,128)(2,1)}), bf16[1,2,3,192,512]{4,3,2,1,0:T(8,128)(2,1)}) %reduce-scatter.6.cloned.1.call-update) | async-done | bytes 1179664 | tf_op jit(solution)/shard_map/reduce_scatter | solution.py:1089
  400.4 11.6 %shard_map.234.p_ref.after = bf16[1024,768]{1,0:T(8,128)(2,1)} custom-call(bf16[1024,768]{1,0:T(8,128)(2,1)} %copy-done.5, bf16[8,128,160]{2,1,0:T(8,128)(2,1)} %copy-done.14, bf16[2,640,1024]{2,1,0:T(8,128)(2,1)} %copy-done.20, f32[2,640,1]{2,1,0:T(8,128)} %copy-done.51, bf16[2,2,512,768]{3,2,1,0:T(8,128)(2,1)} %far_down.7, ...), custom_call_target="tpu_custom_call" | custom-call | tf_op jit(solution)/shard_map/pallas_call | solution.py:64
  419.3 46.2 %psum.7 = f32[2,6,768]{2,1,0:T(8,128)S(1)} all-reduce(f32[2,6,768]{2,1,0:T(8,128)S(1)} %pad_maximum_fusion.4), channel_id=1, replica_groups=mesh['dp'=4,'expert'=2,'wshard'=4] {'dp','expert','wshard'}, use_global_device_ids=true, to_apply=%region_17.18 | all-reduce | flops 9216 | bytes 73728 | tf_op jit(solution)/shard_map/psum | solution.py:1139
  470.5 11.7 %shard_map.235 = f32[128,768]{1,0:T(8,128)S(1)} custom-call(bf16[1024,768]{1,0:T(8,128)(2,1)S(1)} %copy-done.9), custom_call_target="tpu_custom_call" | custom-call | tf_op jit(solution)/shard_map/pallas_call | solution.py:907
  482.9 13.2 %reduce-scatter.8.cloned.1.call-done = bf16[1,4096,128]{2,1,0:T(8,128)(2,1)} async-done(((bf16[4,4096,128]{2,1,0:T(8,128)(2,1)}), bf16[1,4096,128]{2,1,0:T(8,128)(2,1)}) %reduce-scatter.8.cloned.1.call-update) | async-done | bytes 1048592 | tf_op jit(solution)/shard_map/reduce_scatter | solution.py:1089
  504.4 29.9 %collective-permute-done.4 = bf16[2,1344,128]{2,1,0:T(8,128)(2,1)S(1)} collective-permute-done((bf16[2,1344,128]{2,1,0:T(8,128)(2,1)S(1)}, bf16[2,1344,128]{2,1,0:T(8,128)(2,1)S(1)}, u32[]{:S(2)}, u32[]{:S(2)}) %collective-permute-start.4) | collective-permute-done | bytes 688160 | tf_op jit(solution)/shard_map/ppermute | solution.py:1148
  (383 shorter events, 161.5 us)
Async XLA Ops:
  47.5 47.5 %all-to-all-start = ((bf16[4,2,192,512]{3,2,1,0:T(8,128)(2,1)}), bf16[4,2,192,512]{3,2,1,0:T(8,128)(2,1)S(1)}, u32[]{:S(2)}, u32[]{:S(2)}) async-start(bf16[4,2,192,512]{3,2,1,0:T(8,128)(2,1)} %pad_maximum_fusion.1), calls=%async_computation | async-start | bytes 3145728 | tf_op jit(solution)/shard_map/all_to_all | solution.py:1005
  56.1 45.5 %copy-start.110 = (bf16[2,6,768]{2,1,0:T(8,128)(2,1)}, bf16[2,6,768]{2,1,0:T(8,128)(2,1)S(1)}, u32[]{:S(2)}) copy-start(bf16[2,6,768]{2,1,0:T(8,128)(2,1)S(1)} %reshape.258) | copy-start | bytes 55300
  96.2 61.0 %all-to-all-start.1 = ((bf16[4,4,192,512]{3,2,1,0:T(8,128)(2,1)}), bf16[4,4,192,512]{3,2,1,0:T(8,128)(2,1)}, u32[]{:S(2)}, u32[]{:S(2)}) async-start(bf16[4,4,192,512]{3,2,1,0:T(8,128)(2,1)} %maximum_maximum_fusion), calls=%async_computation.1 | async-start | bytes 6291456 | tf_op jit(solution)/shard_map/all_to_all | solution.py:1005
  101.5 216.6 %reduce-scatter.4.cloned.1.call-start = ((), (), s32[]{:S(2)}) async-start(), calls=%async_computation.5 | async-start | bytes 5898240 | tf_op jit(solution)/shard_map/reduce_scatter | solution.py:1089
  106.9 25.1 %copy-start.62 = (bf16[128,768]{1,0:T(8,128)(2,1)}, bf16[128,768]{1,0:T(8,128)(2,1)S(1)}, u32[]{:S(2)}) copy-start(bf16[128,768]{1,0:T(8,128)(2,1)S(1)} %get-tuple-element.173.router) | copy-start | bytes 589828
  107.2 24.8 %copy-start.36 = (f32[1024,128]{1,0:T(8,128)}, f32[1024,128]{1,0:T(8,128)S(1)}, u32[]{:S(2)}) copy-start(f32[1024,128]{1,0:T(8,128)S(1)} %or_select_fusion.chosen) | copy-start | bytes 1572868
  108.8 23.2 %copy-start.14 = (bf16[8,128,160]{2,1,0:T(8,128)(2,1)}, bf16[8,128,160]{2,1,0:T(8,128)(2,1)S(1)}, u32[]{:S(2)}) copy-start(bf16[8,128,160]{2,1,0:T(8,128)(2,1)S(1)} %compare_convert_fusion.back) | copy-start | bytes 983044
  148.0 43.6 %slice-start = ((s8[6291456]{0:T(1024)(128)(4,1)}), s8[2097152]{0:T(1024)(128)(4,1)S(1)}, s32[]{:S(2)}) async-start(s8[6291456]{0:T(1024)(128)(4,1)} %bitcast.134), calls=%async_computation.8 | async-start | bytes 4194304
  159.1 19.1 %copy-start.97 = (f32[128,768]{1,0:T(8,128)S(1)}, f32[128,768]{1,0:T(8,128)}, u32[]{:S(2)}) copy-start(f32[128,768]{1,0:T(8,128)} %copy-done.96) | copy-start | bytes 1179652
  159.1 32.6 %slice-start.1 = ((s8[6291456]{0:T(1024)(128)(4,1)}), s8[4194304]{0:T(1024)(128)(4,1)S(1)}, s32[]{:S(2)}) async-start(s8[6291456]{0:T(1024)(128)(4,1)} %bitcast.134), calls=%async_computation.9 | async-start | bytes 8388608
  178.3 21.9 %copy-start.89 = (f32[128,768]{1,0:T(8,128)}, f32[128,768]{1,0:T(8,128)S(1)}, u32[]{:S(2)}) copy-start(f32[128,768]{1,0:T(8,128)S(1)} %get-tuple-element.135) | copy-start | bytes 1179652
  217.7 182.8 %reduce-scatter.6.cloned.1.call-start = ((), (), s32[]{:S(2)}) async-start(), calls=%async_computation.6 | async-start | bytes 5898240 | tf_op jit(solution)/shard_map/reduce_scatter | solution.py:1089
  251.0 44.3 %collective-permute-start = (bf16[4,1280,128]{2,1,0:T(8,128)(2,1)S(1)}, bf16[4,1280,128]{2,1,0:T(8,128)(2,1)S(1)}, u32[]{:S(2)}, u32[]{:S(2)}) collective-permute-start(bf16[4,1280,128]{2,1,0:T(8,128)(2,1)S(1)} %shard_map.223), channel_id=1, source_target_pairs={{0,4},{4,0},{1,5},{5,1},{2,6},{6,2},{3,7},{7,3},{8,12},{12,8},{9,1... | collective-permute-start | bytes 3932168 | tf_op jit(solution)/shard_map/ppermute | solution.py:1079
  262.3 18.6 %copy-start.98 = (f32[128,768]{1,0:T(8,128)S(1)}, f32[128,768]{1,0:T(8,128)}, u32[]{:S(2)}) copy-start(f32[128,768]{1,0:T(8,128)} %copy-done.96) | copy-start | bytes 1179652
  272.2 24.3 %copy-start.68 = (f32[2,640,1]{2,1,0:T(8,128)S(1)}, f32[2,640,1]{2,1,0:T(8,128)}, u32[]{:S(2)}) copy-start(f32[2,640,1]{2,1,0:T(8,128)} %copy-done.67) | copy-start | bytes 15364
  281.1 15.4 %copy-start.53 = (bf16[2,640,1024]{2,1,0:T(8,128)(2,1)S(1)}, bf16[2,640,1024]{2,1,0:T(8,128)(2,1)}, u32[]{:S(2)}) copy-start(bf16[2,640,1024]{2,1,0:T(8,128)(2,1)} %copy-done.52) | copy-start | bytes 7864324
  314.2 181.9 %reduce-scatter.8.cloned.1.call-start = ((), (), s32[]{:S(2)}) async-start(), calls=%async_computation.7 | async-start | bytes 5242880 | tf_op jit(solution)/shard_map/reduce_scatter | solution.py:1089
  317.0 44.4 %collective-permute-start.1 = (bf16[4,768,128]{2,1,0:T(8,128)(2,1)}, bf16[4,768,128]{2,1,0:T(8,128)(2,1)S(1)}, u32[]{:S(2)}, u32[]{:S(2)}) collective-permute-start(bf16[4,768,128]{2,1,0:T(8,128)(2,1)} %shard_map.229), channel_id=1, source_target_pairs={{0,4},{4,0},{1,5},{5,1},{2,6},{6,2},{3,7},{7,3},{8,12},{12,8},{9,1... | collective-permute-start | bytes 2359304 | tf_op jit(solution)/shard_map/ppermute | solution.py:1079
  336.1 15.5 %copy-start.19 = (bf16[2,4,1280,128]{3,2,1,0:T(8,128)(2,1)S(1)}, bf16[2,4,1280,128]{3,2,1,0:T(8,128)(2,1)}, u32[]{:S(2)}) copy-start(bf16[2,4,1280,128]{3,2,1,0:T(8,128)(2,1)} %get-tuple-element.113.whole) | copy-start | bytes 7864324
  351.9 31.5 %collective-permute-start.2 = (bf16[4,1280,128]{2,1,0:T(8,128)(2,1)S(1)}, bf16[4,1280,128]{2,1,0:T(8,128)(2,1)S(1)}, u32[]{:S(2)}, u32[]{:S(2)}) collective-permute-start(bf16[4,1280,128]{2,1,0:T(8,128)(2,1)S(1)} %shard_map.233), channel_id=1, source_target_pairs={{0,4},{4,0},{1,5},{5,1},{2,6},{6,2},{3,7},{7,3},{8,12},{12,8},{9,1... | collective-permute-start | bytes 3932168 | tf_op jit(solution)/shard_map/ppermute | solution.py:1079
  379.7 33.8 %collective-permute-start.3 = (bf16[4,768,128]{2,1,0:T(8,128)(2,1)S(1)}, bf16[4,768,128]{2,1,0:T(8,128)(2,1)}, u32[]{:S(2)}, u32[]{:S(2)}) collective-permute-start(bf16[4,768,128]{2,1,0:T(8,128)(2,1)S(1)} %shard_map.237), channel_id=1, source_target_pairs={{0,4},{4,0},{1,5},{5,1},{2,6},{6,2},{3,7},{7,3},{8,12},{12,8},{9,1... | collective-permute-start | bytes 2359304 | tf_op jit(solution)/shard_map/ppermute | solution.py:1079
  417.6 49.3 %copy-start.100 = (bf16[1,2,3,192,512]{4,3,2,1,0:T(8,128)(2,1)S(1)}, bf16[1,2,3,192,512]{4,3,2,1,0:T(8,128)(2,1)}, u32[]{:S(2)}) copy-start(bf16[1,2,3,192,512]{4,3,2,1,0:T(8,128)(2,1)} %reduce-scatter.6.cloned.1.call-done) | copy-start | bytes 3538948
  417.6 49.4 %copy-start.101 = (bf16[1,2,3,192,512]{4,3,2,1,0:T(8,128)(2,1)S(1)}, bf16[1,2,3,192,512]{4,3,2,1,0:T(8,128)(2,1)}, u32[]{:S(2)}) copy-start(bf16[1,2,3,192,512]{4,3,2,1,0:T(8,128)(2,1)} %reduce-scatter.4.cloned.1.call-done) | copy-start | bytes 3538948
  498.1 36.2 %collective-permute-start.4 = (bf16[2,1344,128]{2,1,0:T(8,128)(2,1)S(1)}, bf16[2,1344,128]{2,1,0:T(8,128)(2,1)S(1)}, u32[]{:S(2)}, u32[]{:S(2)}) collective-permute-start(bf16[2,1344,128]{2,1,0:T(8,128)(2,1)S(1)} %pad_maximum_fusion.3), channel_id=1, source_target_pairs={{0,0},{1,8},{2,16},{3,24},{8,1},{9,9},{10,17},{11,25},{16,2},{17,1... | collective-permute-start | bytes 2064392 | tf_op jit(solution)/shard_map/ppermute | solution.py:1148
  (104 other events, 546.6 us)
Sparse Core Ops, SparseCore 0:
  217.8 85.9 reduce-scatter.3
  314.3 86.0 reduce-scatter.5
  417.7 78.3 reduce-scatter.7

commit v5 on v4

--- a/solution.py
+++ b/solution.py
@@ -165,7 +165,7 @@
         attend_kernel,
         [((count, width), bf16), piece, piece, piece, ((heads, count, count), bf16), piece],
         [((3, width, window), bf16), DMA((16,))],
-        hidden, Far(source), cosine, sine, length, out_weight,
+        hidden, Far(source), cosine, sine, length, out_weight, alone=True,
     )
 
 
@@ -377,6 +377,7 @@
             DMA((8,)),
         ],
         mixed, select, back, chosen, router, Far(up), Far(down), Far(wide), Far(narrow),
+        alone=True,
     )
 
 
@@ -420,7 +421,7 @@
 
 
 def finish_kernel(
-    layer, mixed, back, inner, scale, far_down, far_wide, far_narrow, after, near,
+    layer, mixed, back, inner, scale, far_down, far_wide, far_narrow, near,
     partial,
     sent, shared_out, down, wide, narrow, sems, wide_sems,
 ):
@@ -447,7 +448,7 @@
     finish_part(mixed, back, wide, narrow, partial, sent, shared_out)
 
 
-def finish(layer, mixed, back, inner, scale, down, wide, narrow, after, near):
+def finish(layer, mixed, back, inner, scale, down, wide, narrow, near):
     group, rows, spots = back.shape
     width = mixed.shape[1]
     units = down.shape[2]
@@ -464,7 +465,7 @@
             DMA((2,)),
             DMA((8,)),
         ],
-        mixed, back, inner, scale, Far(down), Far(wide), Far(narrow), Far(after), Far(near),
+        mixed, back, inner, scale, Far(down), Far(wide), Far(narrow), Far(near),
         alone=True,
     )[0]
 
@@ -1080,7 +1081,10 @@
         return arrivals
 
     def near_sum(piece, arrivals, after):
-        total = pick(piece, 0, after).astype(f32)
+        if after is None:
+            total = lax.dynamic_index_in_dim(piece, owner, 0, keepdims=False).astype(f32)
+        else:
+            total = pick(piece, 0, after).astype(f32)
         for item in arrivals:
             total = total + item.astype(f32)
         return total.astype(bf16)
@@ -1122,7 +1126,7 @@
         hidden_grad = reduce(partial, SLOT, 3)
         gain_a_grad = jnp.sum(hidden_grad * normed_a, axis=0)
         grad = middle_grad + norm_back(hidden_grad * gains[0], normed_a, inverse_a)
-        pieces.append(near_sum(dense_b, near_send(dense_b, mixed_grad), mixed_grad))
+        pieces.append(near_sum(dense_b, near_send(dense_b, mixed_grad), None))
         first_rows = dense_b.shape[2]
         small_grads[layer] = jnp.concatenate(
             [router_grad[:experts], gain_a_grad[None], gain_b_grad[None]], axis=0
@@ -1130,13 +1134,15 @@
     grad, mixed = lax.optimization_barrier((grad, saved[-1][11]))
     wide, arrived, inner, scale, gates = saved[-1][12:]
     partial = finish(
-        LAYERS - 1, mixed, back, inner, scale, expert_down, wide, shared_down, after, pieces[-1]
+        LAYERS - 1, mixed, back, inner, scale, expert_down, wide, shared_down, pieces[-1]
     )
     pieces.append(near_sum(dense_a, near_send(dense_a, dense_a), partial))
     dense = far_sum(jnp.concatenate(pieces, axis=1)).reshape(LAYERS, -1, 128)[::-1]
     reduced = [(reduced[i], dense[i, :first_rows], dense[i, first_rows:]) for i in range(LAYERS)]
     block_out = (middle + reduce(partial, PLANE, 4)).astype(bf16)[None]
-    small_all = lax.psum(jnp.stack(small_grads, axis=0), ("dp", "expert", "wshard"))
+    small_all = pick(jnp.stack(small_grads, axis=0).reshape(1, lines, width), 0, after)
+    small_all = lax.psum(small_all, ("dp", "expert", "wshard"))
+    small_all = small_all.reshape(LAYERS, experts + 2, width)
     small_own = lax.dynamic_slice_in_dim(small_all, shard * chunk, chunk, axis=2)
     turned = jnp.stack(
         [

time: 553 us -> 547 us (0.989)
  waiting for transfers between devices: 60.2 us -> 44.3 us
  Pallas kernels: 307 us -> 320 us
  local copies, waits for them, and re-layouts: 71.4 us -> 60.9 us
  other arithmetic: 24.4 us -> 32.8 us
    reduce_scatter x3, waiting for transfers between devices: 28.7 us -> 11.2 us  [far_sum(): return lax.psum_scatter(piece, 'dp', scatter_dimension=0, tiled=True)[0]]
    unnamed x238 -> x216, local copies, waits for them, and re-layouts: 51.8 us -> 39.6 us
    pallas_call x19 -> x18, Pallas kernels: 124 us -> 133 us  [call(): pl.pallas_call(kernel, out_shape=tuple((jax.ShapeDtypeStruct(s, d) for s,...]
  transfers between devices with their start and end apart: 10 -> 10, of which waited for: 4 -> 4; matrix products, arithmetic and copies ran while one was open for 6% -> 8% of each run, Pallas kernels for 42% -> 44%
where the time goes in v5:
time: 547 us; the launch traced here: 538 us
  Pallas kernels  320 us (59%)
  local copies, waits for them, and re-layouts  60.9 us (11%)
  blocking collectives  45.2 us (8%)
  waiting for transfers between devices  44.3 us (8%)
  other arithmetic  32.8 us (6%)
  starting transfers between devices  18.4 us (3%)
  between operations  16.5 us (3%)
    pallas_call x18, Pallas kernels, call(): pl.pallas_call(kernel, out_shape=tuple((jax.ShapeDtypeStruct(s, d) for s,...  133 us
    pallas_call x8, Pallas kernels, reduce(): pl.pallas_call(functools.partial(reduce_kernel, axes), out_shape=jax.Shap...  91.7 us
    pallas_call x6, Pallas kernels, gather(): pl.pallas_call(functools.partial(gather_kernel, axes), out_shape=jax.Shap...  64 us
    psum x1, blocking collectives, per_device(): small_all = lax.psum(small_all, ('dp', 'expert', 'wshard'))  45.2 us
    unnamed x216, local copies, waits for them, and re-layouts  39.6 us
    pallas_call x1, Pallas kernels, begin(): pl.pallas_call(functools.partial(begin_kernel, groups), out_shape=tuple(o...  31 us
    ppermute x1, waiting for transfers between devices, per_device(): turned = lax.ppermute(turned, ('dp', 'wshard'), transposed).astype(f32)  29.9 us
    reduce_scatter x3, waiting for transfers between devices, far_sum(): return lax.psum_scatter(piece, 'dp', scatter_dimension=0, tiled=True)[0]  11.2 us
  transfers between devices with their start and end apart: 10, of which 4 were waited for; matrix products, arithmetic and copies ran while one was open for 8% of the time, Pallas kernels for 44%

profile of v5, /device:TPU:4, one launch (start us, length us, event | category | flops | bytes accessed | tf_op | source)
XLA Modules:
  0.0 538.1 jit_solution(14592061749713086742)
XLA Ops:
  14.3 31.0 %shard_map.204 = (bf16[512,768]{1,0:T(8,128)(2,1)S(1)}, s32[64,128]{1,0:T(8,128)S(1)}, bf16[64,256]{1,0:T(8,128)(2,1)S(1)}, bf16[1024,768]{1,0:T(8,128)(2,1)S(1)}, bf16[3,768,256]{2,1,0:T(8,128)(2,1)S(1)}) custom-call(bf16[128,768]{1,0:T(8,128)(2,1)S(1)} %bitcast.141, s32[8,128]{1,0:T(8,128)S(1)} %concatenate.32.refs_1_, bf16[16,256]{1,0:T(8,128)(2,1)S(1)} %pad.7.refs_2_, ...), custom_call_target="tpu_custom_call" | custom-call | tf_op jit(solution)/shard_map/pallas_call | solution.py:854
  69.2 8.7 %shard_map.206 = f32[128,768]{1,0:T(8,128)S(1)} custom-call(bf16[512,768]{1,0:T(8,128)(2,1)S(1)} %copy-done.57), custom_call_target="tpu_custom_call" | custom-call | tf_op jit(solution)/shard_map/pallas_call | solution.py:908
  79.5 13.4 %shard_map.207.mixed = bf16[1024,768]{1,0:T(8,128)(2,1)S(1)} custom-call(bf16[128,768]{1,0:T(8,128)(2,1)S(1)} %multiply_convert_fusion.2.x_ref), custom_call_target="tpu_custom_call" | custom-call | tf_op jit(solution)/shard_map/pallas_call | solution.py:789
  108.5 18.1 %shard_map.208 = (bf16[1024,768]{1,0:T(8,128)(2,1)}, bf16[2,640,768]{2,1,0:T(8,128)(2,1)}, bf16[2,640,1024]{2,1,0:T(8,128)(2,1)}, f32[2,640,1]{2,1,0:T(8,128)}, f32[1024,128]{1,0:T(8,128)}) custom-call(bf16[1024,768]{1,0:T(8,128)(2,1)} %copy-done.10, bf16[8,160,128]{2,1,0:T(8,128)(2,1)} %fusion.5.select, bf16[8,128,160]{2,1,0:T(8,128)(2,1)} %compare_convert_fusion.back, ...), custom_call_target="tpu_custom_call" | custom-call | tf_op jit(solution)/shard_map/pallas_call | solution.py:64
  128.0 16.2 %shard_map.209 = f32[128,768]{1,0:T(8,128)S(1)} custom-call(bf16[1024,768]{1,0:T(8,128)(2,1)S(1)} %copy-done.53), custom_call_target="tpu_custom_call" | custom-call | tf_op jit(solution)/shard_map/pallas_call | solution.py:908
  156.2 8.7 %shard_map.211 = (bf16[512,768]{1,0:T(8,128)(2,1)}, bf16[512,256]{1,0:T(8,128)(2,1)}, bf16[512,256]{1,0:T(8,128)(2,1)}, bf16[512,256]{1,0:T(8,128)(2,1)}, bf16[4...) custom-call(bf16[512,768]{1,0:T(8,128)(2,1)} %copy-done.17, bf16[4,4,192,512]{3,2,1,0:T(8,128)(2,1)} %copy-done.1, ...), custom_call_target="tpu_custom_call" | custom-call | tf_op jit(solution)/shard_map/pallas_call | solution.py:64
  166.1 8.7 %shard_map.212 = f32[128,768]{1,0:T(8,128)S(1)} custom-call(bf16[512,768]{1,0:T(8,128)(2,1)S(1)} %copy-done.56), custom_call_target="tpu_custom_call" | custom-call | tf_op jit(solution)/shard_map/pallas_call | solution.py:908
  175.7 13.2 %shard_map.213.mixed = bf16[1024,768]{1,0:T(8,128)(2,1)S(1)} custom-call(bf16[128,768]{1,0:T(8,128)(2,1)S(1)} %multiply_convert_fusion.x_ref), custom_call_target="tpu_custom_call" | custom-call | tf_op jit(solution)/shard_map/pallas_call | solution.py:789
  201.7 12.8 %shard_map.215 = (bf16[4,2,3,192,512]{4,3,2,1,0:T(8,128)(2,1)S(1)}, bf16[8,160,768]{2,1,0:T(8,128)(2,1)S(1)}, f32[8,160,128]{2,1,0:T(8,128)S(1)}) custom-call(bf16[1024,768]{1,0:T(8,128)(2,1)S(1)} %copy-done.24, bf16[8,160,128]{2,1,0:T(8,128)(2,1)S(1)} %copy-done.14, bf16[2,2,2,768,512]{4,3,2,1,0:T(8,128)(2,1)} %far_up.7, ...), custom_call_target="tpu_custom_call" | custom-call | tf_op jit(solution)/shard_map/pallas_call | solution.py:64
  218.9 16.1 %shard_map.216 = (bf16[1024,768]{1,0:T(8,128)(2,1)}, bf16[2,4,1280,128]{3,2,1,0:T(8,128)(2,1)}, f32[128,768]{1,0:T(8,128)}) custom-call(bf16[1024,768]{1,0:T(8,128)(2,1)} %copy-done.23, bf16[1024,768]{1,0:T(8,128)(2,1)} %copy-done.7, bf16[8,128,160]{2,1,0:T(8,128)(2,1)} %compare_convert_fusion.back, bf16[128,768]{1,0:T(8,128)(2,1)} %copy-done.51, ...), custom_call_target="tpu_custom_call" | custom-call | tf_op jit(solution)/shard_map/pallas_call | solution.py:64
  236.5 13.9 %shard_map.217.after = f32[128,768]{1,0:T(8,128)S(1)} custom-call(bf16[1024,768]{1,0:T(8,128)(2,1)S(1)} %copy-done.52), custom_call_target="tpu_custom_call" | custom-call | tf_op jit(solution)/shard_map/pallas_call | solution.py:908
  267.8 8.9 %shard_map.219 = (bf16[512,768]{1,0:T(8,128)(2,1)S(1)}, bf16[2,4,768,128]{3,2,1,0:T(8,128)(2,1)S(1)}) custom-call(bf16[512,768]{1,0:T(8,128)(2,1)S(1)} %shard_map.218.grad, bf16[512,768]{1,0:T(8,128)(2,1)S(1)} %copy-done.18, bf16[4,4,192,512]{3,2,1,0:T(8,128)(2,1)S(1)} %copy-done.2, f32[512,128]{1,0:T(8,128)S(1)} %copy-done.21, f32[512,128]{1,0:T(8,128)S(1)} %copy-done.19, ...), custom_call_target="tpu_custom_call" | custom-call | tf_op jit(solution)/shard_map/pallas_call | solution.py:64
  277.9 8.7 %shard_map.220 = f32[128,768]{1,0:T(8,128)S(1)} custom-call(bf16[512,768]{1,0:T(8,128)(2,1)S(1)} %get-tuple-element.94.p_ref), custom_call_target="tpu_custom_call" | custom-call | tf_op jit(solution)/shard_map/pallas_call | solution.py:908
  288.4 13.3 %shard_map.221.grad.after = bf16[1024,768]{1,0:T(8,128)(2,1)S(1)} custom-call(bf16[128,768]{1,0:T(8,128)(2,1)S(1)} %get-tuple-element.132.x_ref), custom_call_target="tpu_custom_call" | custom-call | tf_op jit(solution)/shard_map/pallas_call | solution.py:789
  304.5 11.6 %shard_map.223 = (bf16[4,2,3,192,512]{4,3,2,1,0:T(8,128)(2,1)S(1)}, bf16[8,160,768]{2,1,0:T(8,128)(2,1)S(1)}, f32[8,160,128]{2,1,0:T(8,128)S(1)}) custom-call(bf16[1024,768]{1,0:T(8,128)(2,1)S(1)} %shard_map.221.grad.after, bf16[8,160,128]{2,1,0:T(8,128)(2,1)S(1)} %copy-done.15, bf16[2,2,2,768,512]{4,3,2,1,0:T(8,128)(2,1)} %far_up.7, ...), custom_call_target="tpu_custom_call" | custom-call | tf_op jit(solution)/shard_map/pallas_call | solution.py:64
  324.2 16.6 %shard_map.224 = (bf16[1024,768]{1,0:T(8,128)(2,1)}, bf16[2,4,1280,128]{3,2,1,0:T(8,128)(2,1)}, f32[128,768]{1,0:T(8,128)}) custom-call(bf16[1024,768]{1,0:T(8,128)(2,1)} %copy-done.5, bf16[1024,768]{1,0:T(8,128)(2,1)} %copy-done.10, bf16[8,128,160]{2,1,0:T(8,128)(2,1)} %compare_convert_fusion.back, bf16[128,768]{1,0:T(8,128)(2,1)} %get-tuple-element.173.router, ...), custom_call_target="tpu_custom_call" | custom-call | tf_op jit(solution)/shard_map/pallas_call | solution.py:64
  343.6 13.9 %shard_map.225.after = f32[128,768]{1,0:T(8,128)S(1)} custom-call(bf16[1024,768]{1,0:T(8,128)(2,1)S(1)} %copy-done.28), custom_call_target="tpu_custom_call" | custom-call | tf_op jit(solution)/shard_map/pallas_call | solution.py:908
  367.6 9.2 %shard_map.229 = (bf16[512,768]{1,0:T(8,128)(2,1)S(1)}, bf16[2,4,768,128]{3,2,1,0:T(8,128)(2,1)S(1)}) custom-call(bf16[512,768]{1,0:T(8,128)(2,1)S(1)} %shard_map.226.grad, bf16[512,768]{1,0:T(8,128)(2,1)S(1)} %copy-done.16, bf16[3,768,256]{2,1,0:T(8,128)(2,1)S(1)} %copy-done.38, f32[512,128]{1,0:T(8,128)S(1)} %copy-done.22, f32[512,128]{1,0:T(8,128)S(1)} %copy-done.20, ...), custom_call_target="tpu_custom_call" | custom-call | tf_op jit(solution)/shard_map/pallas_call | solution.py:64
  376.7 8.7 %shard_map.230 = f32[128,768]{1,0:T(8,128)S(1)} custom-call(bf16[512,768]{1,0:T(8,128)(2,1)S(1)} %get-tuple-element.110.p_ref), custom_call_target="tpu_custom_call" | custom-call | tf_op jit(solution)/shard_map/pallas_call | solution.py:908
  390.5 11.7 %shard_map.232.p_ref.after = bf16[1024,768]{1,0:T(8,128)(2,1)} custom-call(bf16[1024,768]{1,0:T(8,128)(2,1)} %copy-done.7, bf16[8,128,160]{2,1,0:T(8,128)(2,1)} %compare_convert_fusion.back, bf16[2,640,1024]{2,1,0:T(8,128)(2,1)} %copy-done.13, f32[2,640,1]{2,1,0:T(8,128)} %copy-done.44, bf16[2,2,512,768]{3,2,1,0:T(8,128)(2,1)} %far_down.7, ...), custom_call_target="tpu_custom_call" | custom-call | tf_op jit(solution)/shard_map/pallas_call | solution.py:64
  412.9 45.2 %psum.7 = f32[2,6,768]{2,1,0:T(8,128)S(1)} all-reduce(f32[2,6,768]{2,1,0:T(8,128)S(1)} %reshape.274), channel_id=1, replica_groups=mesh['dp'=4,'expert'=2,'wshard'=4] {'dp','expert','wshard'}, use_global_device_ids=true, to_apply=%region_17.18 | all-reduce | flops 9216 | bytes 73728 | tf_op jit(solution)/shard_map/psum | solution.py:1144
  463.1 13.0 %shard_map.233 = f32[128,768]{1,0:T(8,128)S(1)} custom-call(bf16[1024,768]{1,0:T(8,128)(2,1)S(1)} %copy-done.9), custom_call_target="tpu_custom_call" | custom-call | tf_op jit(solution)/shard_map/pallas_call | solution.py:908
  476.8 11.1 %reduce-scatter.6.cloned.1.call-done = bf16[1,4096,128]{2,1,0:T(8,128)(2,1)} async-done(((bf16[4,4096,128]{2,1,0:T(8,128)(2,1)}), bf16[1,4096,128]{2,1,0:T(8,128)(2,1)}) %reduce-scatter.6.cloned.1.call-update) | async-done | bytes 1048592 | tf_op jit(solution)/shard_map/reduce_scatter | solution.py:1093
  498.2 29.9 %collective-permute-done.4 = bf16[2,1344,128]{2,1,0:T(8,128)(2,1)S(1)} collective-permute-done((bf16[2,1344,128]{2,1,0:T(8,128)(2,1)S(1)}, bf16[2,1344,128]{2,1,0:T(8,128)(2,1)S(1)}, u32[]{:S(2)}, u32[]{:S(2)}) %collective-permute-start.4) | collective-permute-done | bytes 688160 | tf_op jit(solution)/shard_map/ppermute | solution.py:1154
  (361 shorter events, 159.2 us)
Async XLA Ops:
  47.5 48.4 %all-to-all-start = ((bf16[4,2,192,512]{3,2,1,0:T(8,128)(2,1)}), bf16[4,2,192,512]{3,2,1,0:T(8,128)(2,1)}, u32[]{:S(2)}, u32[]{:S(2)}) async-start(bf16[4,2,192,512]{3,2,1,0:T(8,128)(2,1)} %pad_maximum_fusion.1), calls=%async_computation | async-start | bytes 3145728 | tf_op jit(solution)/shard_map/all_to_all | solution.py:1006
  59.5 19.1 %copy-start.79 = (bf16[3,192,768]{2,1,0:T(8,128)(2,1)S(1)}, bf16[3,192,768]{2,1,0:T(8,128)(2,1)}, u32[]{:S(2)}) copy-start(bf16[3,192,768]{2,1,0:T(8,128)(2,1)} %slice_bitcast_fusion.2) | copy-start | bytes 2654212
  78.9 15.2 %copy-start.84 = (bf16[1,2,192,512]{3,2,1,0:T(8,128)(2,1)S(1)}, bf16[1,2,192,512]{3,2,1,0:T(8,128)(2,1)}, u32[]{:S(2)}) copy-start(bf16[1,2,192,512]{3,2,1,0:T(8,128)(2,1)} %get-tuple-element.143) | copy-start | bytes 1179652
  96.0 58.5 %all-to-all-start.1 = ((bf16[4,4,192,512]{3,2,1,0:T(8,128)(2,1)}), bf16[4,4,192,512]{3,2,1,0:T(8,128)(2,1)S(1)}, u32[]{:S(2)}, u32[]{:S(2)}) async-start(bf16[4,4,192,512]{3,2,1,0:T(8,128)(2,1)} %maximum_maximum_fusion), calls=%async_computation.1 | async-start | bytes 6291456 | tf_op jit(solution)/shard_map/all_to_all | solution.py:1006
  100.4 223.9 %reduce-scatter.4.cloned.1.call-start = ((), (), s32[]{:S(2)}) async-start(), calls=%async_computation.5 | async-start | bytes 5898240 | tf_op jit(solution)/shard_map/reduce_scatter | solution.py:1093
  106.4 82.5 %copy-start.51 = (bf16[128,768]{1,0:T(8,128)(2,1)}, bf16[128,768]{1,0:T(8,128)(2,1)S(1)}, u32[]{:S(2)}) copy-start(bf16[128,768]{1,0:T(8,128)(2,1)S(1)} %get-tuple-element.172.router) | copy-start | bytes 589828
  128.0 16.2 %copy-start.74 = (f32[128,768]{1,0:T(8,128)S(1)}, f32[128,768]{1,0:T(8,128)}, u32[]{:S(2)}) copy-start(f32[128,768]{1,0:T(8,128)} %copy-done.73) | copy-start | bytes 1179652
  156.2 18.6 %copy-start.77 = (f32[128,768]{1,0:T(8,128)S(1)}, f32[128,768]{1,0:T(8,128)}, u32[]{:S(2)}) copy-start(f32[128,768]{1,0:T(8,128)} %copy-done.76) | copy-start | bytes 1179652
  174.9 25.9 %copy-start.91 = (f32[128]{0:T(128)}, f32[128]{0:T(128)S(1)}, u32[]{:S(2)}) copy-start(f32[128]{0:T(128)S(1)} %add_rsqrt_fusion.2) | copy-start | bytes 1540
  218.9 192.7 %reduce-scatter.8.cloned.1.call-start = ((), (), s32[]{:S(2)}) async-start(), calls=%async_computation.7 | async-start | bytes 5898240 | tf_op jit(solution)/shard_map/reduce_scatter | solution.py:1093
  253.3 48.4 %collective-permute-start = (bf16[4,1280,128]{2,1,0:T(8,128)(2,1)}, bf16[4,1280,128]{2,1,0:T(8,128)(2,1)}, u32[]{:S(2)}, u32[]{:S(2)}) collective-permute-start(bf16[4,1280,128]{2,1,0:T(8,128)(2,1)} %shard_map.222), channel_id=1, source_target_pairs={{0,4},{4,0},{1,5},{5,1},{2,6},{6,2},{3,7},{7,3},{8,12},{12,8},{9,1... | collective-permute-start | bytes 3932168 | tf_op jit(solution)/shard_map/ppermute | solution.py:1080
  267.8 18.8 %copy-start.78 = (f32[128,768]{1,0:T(8,128)S(1)}, f32[128,768]{1,0:T(8,128)}, u32[]{:S(2)}) copy-start(f32[128,768]{1,0:T(8,128)} %copy-done.76) | copy-start | bytes 1179652
  267.8 18.8 %copy-start.98 = (f32[128]{0:T(128)S(1)}, f32[128]{0:T(128)}, u32[]{:S(2)}) copy-start(f32[128]{0:T(128)} %copy-done.97) | copy-start | bytes 1540
  267.8 36.2 %copy-start.49 = (bf16[2,640,768]{2,1,0:T(8,128)(2,1)S(1)}, bf16[2,640,768]{2,1,0:T(8,128)(2,1)}, u32[]{:S(2)}) copy-start(bf16[2,640,768]{2,1,0:T(8,128)(2,1)} %get-tuple-element.96.arrived) | copy-start | bytes 5898244
  277.9 26.1 %copy-start.45 = (bf16[2,640,1024]{2,1,0:T(8,128)(2,1)S(1)}, bf16[2,640,1024]{2,1,0:T(8,128)(2,1)}, u32[]{:S(2)}) copy-start(bf16[2,640,1024]{2,1,0:T(8,128)(2,1)} %get-tuple-element.97.inner) | copy-start | bytes 7864324
  288.4 15.6 %copy-start.58 = (f32[2,640,1]{2,1,0:T(8,128)S(1)}, f32[2,640,1]{2,1,0:T(8,128)}, u32[]{:S(2)}) copy-start(f32[2,640,1]{2,1,0:T(8,128)} %get-tuple-element.98.scale) | copy-start | bytes 15364
  320.4 167.6 %reduce-scatter.6.cloned.1.call-start = ((), (), s32[]{:S(2)}) async-start(), calls=%async_computation.6 | async-start | bytes 5242880 | tf_op jit(solution)/shard_map/reduce_scatter | solution.py:1093
  323.2 44.1 %collective-permute-start.1 = (bf16[4,768,128]{2,1,0:T(8,128)(2,1)}, bf16[4,768,128]{2,1,0:T(8,128)(2,1)S(1)}, u32[]{:S(2)}, u32[]{:S(2)}) collective-permute-start(bf16[4,768,128]{2,1,0:T(8,128)(2,1)} %shard_map.228), channel_id=1, source_target_pairs={{0,4},{4,0},{1,5},{5,1},{2,6},{6,2},{3,7},{7,3},{8,12},{12,8},{9,1... | collective-permute-start | bytes 2359304 | tf_op jit(solution)/shard_map/ppermute | solution.py:1080
  342.2 15.3 %copy-start.29 = (bf16[2,4,1280,128]{3,2,1,0:T(8,128)(2,1)S(1)}, bf16[2,4,1280,128]{3,2,1,0:T(8,128)(2,1)}, u32[]{:S(2)}) copy-start(bf16[2,4,1280,128]{3,2,1,0:T(8,128)(2,1)} %get-tuple-element.112.whole) | copy-start | bytes 7864324
  357.7 31.4 %collective-permute-start.2 = (bf16[4,1280,128]{2,1,0:T(8,128)(2,1)S(1)}, bf16[4,1280,128]{2,1,0:T(8,128)(2,1)S(1)}, u32[]{:S(2)}, u32[]{:S(2)}) collective-permute-start(bf16[4,1280,128]{2,1,0:T(8,128)(2,1)S(1)} %shard_map.231), channel_id=1, source_target_pairs={{0,4},{4,0},{1,5},{5,1},{2,6},{6,2},{3,7},{7,3},{8,12},{12,8},{9,1... | collective-permute-start | bytes 3932168 | tf_op jit(solution)/shard_map/ppermute | solution.py:1080
  385.6 20.0 %collective-permute-start.3 = (bf16[4,768,128]{2,1,0:T(8,128)(2,1)S(1)}, bf16[4,768,128]{2,1,0:T(8,128)(2,1)}, u32[]{:S(2)}, u32[]{:S(2)}) collective-permute-start(bf16[4,768,128]{2,1,0:T(8,128)(2,1)S(1)} %shard_map.235), channel_id=1, source_target_pairs={{0,4},{4,0},{1,5},{5,1},{2,6},{6,2},{3,7},{7,3},{8,12},{12,8},{9,1... | collective-permute-start | bytes 2359304 | tf_op jit(solution)/shard_map/ppermute | solution.py:1080
  412.8 46.6 %copy-start.36 = (bf16[1,2,3,192,512]{4,3,2,1,0:T(8,128)(2,1)S(1)}, bf16[1,2,3,192,512]{4,3,2,1,0:T(8,128)(2,1)}, u32[]{:S(2)}) copy-start(bf16[1,2,3,192,512]{4,3,2,1,0:T(8,128)(2,1)} %reduce-scatter.8.cloned.1.call-done) | copy-start | bytes 3538948
  412.8 46.7 %copy-start.80 = (bf16[1,2,3,192,512]{4,3,2,1,0:T(8,128)(2,1)S(1)}, bf16[1,2,3,192,512]{4,3,2,1,0:T(8,128)(2,1)}, u32[]{:S(2)}) copy-start(bf16[1,2,3,192,512]{4,3,2,1,0:T(8,128)(2,1)} %reduce-scatter.4.cloned.1.call-done) | copy-start | bytes 3538948
  491.9 36.2 %collective-permute-start.4 = (bf16[2,1344,128]{2,1,0:T(8,128)(2,1)S(1)}, bf16[2,1344,128]{2,1,0:T(8,128)(2,1)S(1)}, u32[]{:S(2)}, u32[]{:S(2)}) collective-permute-start(bf16[2,1344,128]{2,1,0:T(8,128)(2,1)S(1)} %pad_maximum_fusion.3), channel_id=1, source_target_pairs={{0,0},{1,8},{2,16},{3,24},{8,1},{9,9},{10,17},{11,25},{16,2},{17,1... | collective-permute-start | bytes 2064392 | tf_op jit(solution)/shard_map/ppermute | solution.py:1154
  (93 other events, 488.4 us)
Sparse Core Ops, SparseCore 0:
  219.0 85.9 reduce-scatter.3
  320.5 85.9 reduce-scatter.7
  409.4 78.5 reduce-scatter.5

commit v6 on v5

--- a/solution.py
+++ b/solution.py
@@ -42,8 +42,9 @@
 
 
 class Far:
-    def __init__(self, value):
+    def __init__(self, value, space=pltpu.HBM):
         self.value = value
+        self.space = space
 
 
 def held_bytes(shape, dtype):
@@ -60,11 +61,12 @@
     need += sum(held_bytes(o.shape, o.dtype) for o in operands if not isinstance(o, Far))
     limit = VMEM_MOST if alone else min(VMEM_MOST, need + VMEM_SLACK)
     vmem = pl.BlockSpec(memory_space=pltpu.VMEM)
-    far = pl.BlockSpec(memory_space=pltpu.HBM)
     return pl.pallas_call(
         kernel,
         out_shape=tuple(jax.ShapeDtypeStruct(s, d) for s, d in outs),
-        in_specs=[far if isinstance(o, Far) else vmem for o in operands],
+        in_specs=[
+            pl.BlockSpec(memory_space=o.space) if isinstance(o, Far) else vmem for o in operands
+        ],
         out_specs=tuple([vmem] * len(outs)),
         scratch_shapes=[pltpu.VMEM(*s) if isinstance(s, tuple) else s for s in scratch],
         compiler_params=pltpu.CompilerParams(vmem_limit_bytes=limit),
@@ -669,7 +671,7 @@
         functools.partial(pick_kernel, step),
         [(whole.shape[1:], whole.dtype)],
         [DMA],
-        Far(whole), Far(after),
+        Far(whole, pl.ANY), Far(after, pl.ANY),
     )[0]
 
 
@@ -800,10 +802,12 @@
 
 def begin_kernel(groups, *refs):
     n = len(groups)
-    blocks, weight = refs[:n], refs[n]
-    outs, columns = refs[n + 1 : 2 * n + 1], refs[2 * n + 1]
-    sems = [refs[2 * n + 2 + 4 * i : 2 * n + 6 + 4 * i] for i in range(n)]
-    send, recv, local = refs[6 * n + 2 :]
+    blocks, weight, shared = refs[:n], refs[n], refs[n + 1]
+    refs = refs[n + 2 :]
+    outs, columns, early, late = refs[:n], refs[n], refs[n + 1], refs[n + 2]
+    refs = refs[n + 3 :]
+    sems = [refs[4 * i : 4 * i + 4] for i in range(n)]
+    send, recv, local, packed = refs[4 * n :]
     tall, wide, owner, shard = layout(PLANE)
     chunk = weight.shape[2]
     window = columns.shape[2]
@@ -832,36 +836,54 @@
         copies.append(copy)
     own = pltpu.make_async_copy(piece(shard), lines, local)
     own.start()
+    pairs = []
+    units = early.shape[3]
+    for a in range(wide):
+        mine = pl.ds(a * units, units)
+        pairs.append((shared.at[0, :, :, mine], early.at[a]))
+        pairs.append((shared.at[1, :, :, mine], late.at[a, pl.ds(0, 2)]))
+        lanes = pl.ds(a * chunk // 128 * 128, window)
+        for i, part in enumerate((0, 1, 2, 2)):
+            there = pl.ds(i % 2 * window, window)
+            pairs.append((weight.at[1, part, :, lanes], late.at[a, 2 + i // 2, :, there]))
+    moves = fetch(pairs, packed)
     sent = [gather_start(g, blocks[i], outs[i], sems[i]) for i, g in enumerate(groups)]
     for i, g in enumerate(groups):
         sent[i] = sent[i] + gather_pass(g, blocks[i], outs[i], sems[i])
     for i, g in enumerate(groups):
         gather_end(g, blocks[i], outs[i], sems[i], sent[i])
     own.wait()
+    settle_all(moves)
     for copy in copies:
         copy.wait_recv()
         copy.wait_send()
 
 
-def begin(blocks, groups, weight, window, cid):
+def begin(blocks, groups, weight, shared, window, cid):
     vmem = pl.BlockSpec(memory_space=pltpu.VMEM)
     width = weight.shape[3]
     others = lax.axis_size("wshard") - 1
     outs = [
         jax.ShapeDtypeStruct((group_size(g) * x.shape[0],) + x.shape[1:], x.dtype)
         for x, g in zip(blocks, groups)
-    ] + [jax.ShapeDtypeStruct((3, width, window), weight.dtype)]
+    ]
+    shards = others + 1
+    chunk, units = weight.shape[2], shared.shape[3] // shards
+    assert 2 * window == units
+    outs.append(jax.ShapeDtypeStruct((3, width, window), weight.dtype))
+    outs.append(jax.ShapeDtypeStruct((shards, 2, chunk, units), weight.dtype))
+    outs.append(jax.ShapeDtypeStruct((shards, 4, chunk, units), weight.dtype))
     return pl.pallas_call(
         functools.partial(begin_kernel, groups),
         out_shape=tuple(outs),
-        in_specs=[vmem] * len(blocks) + [pl.BlockSpec(memory_space=pl.ANY)],
+        in_specs=[vmem] * len(blocks) + [pl.BlockSpec(memory_space=pltpu.HBM)] * 2,
         out_specs=tuple([vmem] * len(outs)),
         scratch_shapes=[s for g in groups for s in gather_sems(g)]
-        + [DMA((others,)), DMA((others,)), DMA],
+        + [DMA((others,)), DMA((others,)), DMA, DMA((6 * shards,))],
         compiler_params=pltpu.CompilerParams(
             collective_id=cid, has_side_effects=True, vmem_limit_bytes=32 << 20
         ),
-    )(*blocks, weight)
+    )(*blocks, weight, shared)
 
 
 def reduce_kernel(axes, p_ref, o_ref, inbox, total, second, send, recv, fsend, frecv):
@@ -960,7 +982,6 @@
     side = width // columns
     window = (chunk + 127) // 128 * 128
     offset = lax.rem(shard * chunk, 128)
-    starts = [a * chunk // 128 * 128 for a in range(shards)]
     transposed = [(a * shards + b, b * shards + a) for a in range(planes) for b in range(shards)]
 
     positions = shard * rows + jnp.arange(rows, dtype=jnp.int32)
@@ -974,8 +995,9 @@
     small = small.reshape(lines, chunk)
     small = jnp.pad(small, ((0, -lines % 16), (0, window - chunk)))
     grad_block = (cotangent[0].astype(f32) * valid[:, None].astype(f32)).astype(bf16)
-    slot_tokens, facts, small, grad_plane, project = begin(
-        (tokens[0], facts, small, grad_block), (SLOT, PLANE, SLOT, PLANE), qkv_weight, window, 5
+    slot_tokens, facts, small, grad_plane, project, early, late = begin(
+        (tokens[0], facts, small, grad_block), (SLOT, PLANE, SLOT, PLANE), qkv_weight, shared_up,
+        window, 5,
     )
     facts = facts.reshape(group, 8, rows)
     small = small.reshape(shards, -1, window)[:, :lines, :chunk]
@@ -998,26 +1020,11 @@
     both = (facts[:, 0, :, None] == named) | (facts[:, 1, :, None] == named)
     chosen = jnp.where(both, 0.0, floor_score).astype(f32).reshape(group * rows, 128)
 
-    def columns_of(weight, size, places):
-        return jnp.stack([weight[..., s : s + size] for s in places], axis=0)
-
     def exchanged(packed, after):
         packed, after = lax.optimization_barrier((packed, after))
         return lax.all_to_all(packed, "wshard", split_axis=0, concat_axis=0, tiled=True), after
 
-    assert 2 * window == units
-    own_units = [a * units for a in range(shards)]
-    early = columns_of(shared_up[0], units, own_units)
     early, slot_tokens = exchanged(early, slot_tokens)
-    late = columns_of(qkv_weight[1], window, starts)
-    late = jnp.concatenate(
-        [
-            columns_of(shared_up[1], units, own_units),
-            jnp.concatenate([late[:, 0:1], late[:, 1:2]], axis=3),
-            jnp.concatenate([late[:, 2:3], late[:, 2:3]], axis=3),
-        ],
-        axis=1,
-    )
     router_full = jnp.zeros((LAYERS, 128, width), bf16)
     router_full = router_full.at[:, :experts].set(small[:, :experts])
     gains_full = small[:, experts:].astype(f32)

time: 547 us -> 544 us (level)
    unnamed x216 -> x206, local copies, waits for them, and re-layouts: 39.6 us -> 46 us
  transfers between devices with their start and end apart: 10 -> 10, of which waited for: 4 -> 4; matrix products, arithmetic and copies ran while one was open for 8% -> 7% of each run, Pallas kernels for 44% -> 44%
where the time goes in v6:
time: 544 us; the launch traced here: 536 us
  Pallas kernels  321 us (59%)
  local copies, waits for them, and re-layouts  60.6 us (11%)
  blocking collectives  45.2 us (8%)
  waiting for transfers between devices  44.2 us (8%)
  other arithmetic  30.6 us (6%)
  starting transfers between devices  17.8 us (3%)
  between operations  16.4 us (3%)
    pallas_call x18, Pallas kernels, call(): pl.pallas_call(kernel, out_shape=tuple((jax.ShapeDtypeStruct(s, d) for s,...  133 us
    pallas_call x8, Pallas kernels, reduce(): pl.pallas_call(functools.partial(reduce_kernel, axes), out_shape=jax.Shap...  91.7 us
    pallas_call x6, Pallas kernels, gather(): pl.pallas_call(functools.partial(gather_kernel, axes), out_shape=jax.Shap...  64 us
    unnamed x206, local copies, waits for them, and re-layouts  46 us
    psum x1, blocking collectives, per_device(): small_all = lax.psum(small_all, ('dp', 'expert', 'wshard'))  45.2 us
    pallas_call x1, Pallas kernels, begin(): pl.pallas_call(functools.partial(begin_kernel, groups), out_shape=tuple(o...  32.5 us
    ppermute x1, waiting for transfers between devices, per_device(): turned = lax.ppermute(turned, ('dp', 'wshard'), transposed).astype(f32)  29.9 us
    reduce_scatter x3, waiting for transfers between devices, far_sum(): return lax.psum_scatter(piece, 'dp', scatter_dimension=0, tiled=True)[0]  11.1 us
  transfers between devices with their start and end apart: 10, of which 4 were waited for; matrix products, arithmetic and copies ran while one was open for 7% of the time, Pallas kernels for 44%

profile of v6, /device:TPU:4, one launch (start us, length us, event | category | flops | bytes accessed | tf_op | source)
XLA Modules:
  0.0 536.2 jit_solution(10942247930329068317)
XLA Ops:
  15.4 32.5 %shard_map.204 = (bf16[512,768]{1,0:T(8,128)(2,1)S(1)}, s32[64,128]{1,0:T(8,128)S(1)}, bf16[64,256]{1,0:T(8,128)(2,1)S(1)}, bf16[1024,768]{1,0:T(8,128)(2,1)S(1)...) custom-call(bf16[128,768]{1,0:T(8,128)(2,1)S(1)} %bitcast.111, ...), custom_call_target="tpu_custom_call" | custom-call | tf_op jit(solution)/shard_map/pallas_call | solution.py:876
  70.7 8.7 %shard_map.206 = f32[128,768]{1,0:T(8,128)S(1)} custom-call(bf16[512,768]{1,0:T(8,128)(2,1)S(1)} %copy-done.60), custom_call_target="tpu_custom_call" | custom-call | tf_op jit(solution)/shard_map/pallas_call | solution.py:930
  80.3 13.4 %shard_map.207.mixed = bf16[1024,768]{1,0:T(8,128)(2,1)S(1)} custom-call(bf16[128,768]{1,0:T(8,128)(2,1)S(1)} %multiply_convert_fusion.2.x_ref), custom_call_target="tpu_custom_call" | custom-call | tf_op jit(solution)/shard_map/pallas_call | solution.py:791
  108.5 18.2 %shard_map.208 = (bf16[1024,768]{1,0:T(8,128)(2,1)}, bf16[2,640,768]{2,1,0:T(8,128)(2,1)}, bf16[2,640,1024]{2,1,0:T(8,128)(2,1)}, f32[2,640,1]{2,1,0:T(8,128)}, f32[1024,128]{1,0:T(8,128)}) custom-call(bf16[1024,768]{1,0:T(8,128)(2,1)} %copy-done.10, bf16[8,160,128]{2,1,0:T(8,128)(2,1)} %fusion.5.select, bf16[8,128,160]{2,1,0:T(8,128)(2,1)} %compare_convert_fusion.back, ...), custom_call_target="tpu_custom_call" | custom-call | tf_op jit(solution)/shard_map/pallas_call | solution.py:64
  128.1 16.2 %shard_map.209 = f32[128,768]{1,0:T(8,128)S(1)} custom-call(bf16[1024,768]{1,0:T(8,128)(2,1)S(1)} %copy-done.56), custom_call_target="tpu_custom_call" | custom-call | tf_op jit(solution)/shard_map/pallas_call | solution.py:930
  156.3 8.7 %shard_map.211 = (bf16[512,768]{1,0:T(8,128)(2,1)}, bf16[512,256]{1,0:T(8,128)(2,1)}, bf16[512,256]{1,0:T(8,128)(2,1)}, bf16[512,256]{1,0:T(8,128)(2,1)}, bf16[4...) custom-call(bf16[512,768]{1,0:T(8,128)(2,1)} %copy-done.17, bf16[4,4,192,512]{3,2,1,0:T(8,128)(2,1)} %copy-done.1, ...), custom_call_target="tpu_custom_call" | custom-call | tf_op jit(solution)/shard_map/pallas_call | solution.py:64
  166.1 8.7 %shard_map.212 = f32[128,768]{1,0:T(8,128)S(1)} custom-call(bf16[512,768]{1,0:T(8,128)(2,1)S(1)} %copy-done.59), custom_call_target="tpu_custom_call" | custom-call | tf_op jit(solution)/shard_map/pallas_call | solution.py:930
  175.8 13.2 %shard_map.213.mixed = bf16[1024,768]{1,0:T(8,128)(2,1)S(1)} custom-call(bf16[128,768]{1,0:T(8,128)(2,1)S(1)} %multiply_convert_fusion.x_ref), custom_call_target="tpu_custom_call" | custom-call | tf_op jit(solution)/shard_map/pallas_call | solution.py:791
  201.8 12.8 %shard_map.215 = (bf16[4,2,3,192,512]{4,3,2,1,0:T(8,128)(2,1)S(1)}, bf16[8,160,768]{2,1,0:T(8,128)(2,1)S(1)}, f32[8,160,128]{2,1,0:T(8,128)S(1)}) custom-call(bf16[1024,768]{1,0:T(8,128)(2,1)S(1)} %copy-done.24, bf16[8,160,128]{2,1,0:T(8,128)(2,1)S(1)} %copy-done.14, bf16[2,2,2,768,512]{4,3,2,1,0:T(8,128)(2,1)} %far_up.7, ...), custom_call_target="tpu_custom_call" | custom-call | tf_op jit(solution)/shard_map/pallas_call | solution.py:64
  219.0 16.1 %shard_map.216 = (bf16[1024,768]{1,0:T(8,128)(2,1)}, bf16[2,4,1280,128]{3,2,1,0:T(8,128)(2,1)}, f32[128,768]{1,0:T(8,128)}) custom-call(bf16[1024,768]{1,0:T(8,128)(2,1)} %copy-done.23, bf16[1024,768]{1,0:T(8,128)(2,1)} %copy-done.7, bf16[8,128,160]{2,1,0:T(8,128)(2,1)} %compare_convert_fusion.back, bf16[128,768]{1,0:T(8,128)(2,1)} %copy-done.54, ...), custom_call_target="tpu_custom_call" | custom-call | tf_op jit(solution)/shard_map/pallas_call | solution.py:64
  236.5 13.9 %shard_map.217.after = f32[128,768]{1,0:T(8,128)S(1)} custom-call(bf16[1024,768]{1,0:T(8,128)(2,1)S(1)} %copy-done.55), custom_call_target="tpu_custom_call" | custom-call | tf_op jit(solution)/shard_map/pallas_call | solution.py:930
  267.8 8.9 %shard_map.219 = (bf16[512,768]{1,0:T(8,128)(2,1)S(1)}, bf16[2,4,768,128]{3,2,1,0:T(8,128)(2,1)S(1)}) custom-call(bf16[512,768]{1,0:T(8,128)(2,1)S(1)} %shard_map.218.grad, bf16[512,768]{1,0:T(8,128)(2,1)S(1)} %copy-done.18, bf16[4,4,192,512]{3,2,1,0:T(8,128)(2,1)S(1)} %copy-done.2, f32[512,128]{1,0:T(8,128)S(1)} %copy-done.21, f32[512,128]{1,0:T(8,128)S(1)} %copy-done.19, ...), custom_call_target="tpu_custom_call" | custom-call | tf_op jit(solution)/shard_map/pallas_call | solution.py:64
  277.9 8.7 %shard_map.220 = f32[128,768]{1,0:T(8,128)S(1)} custom-call(bf16[512,768]{1,0:T(8,128)(2,1)S(1)} %get-tuple-element.98.p_ref), custom_call_target="tpu_custom_call" | custom-call | tf_op jit(solution)/shard_map/pallas_call | solution.py:930
  288.4 13.3 %shard_map.221.grad.after = bf16[1024,768]{1,0:T(8,128)(2,1)S(1)} custom-call(bf16[128,768]{1,0:T(8,128)(2,1)S(1)} %get-tuple-element.136.x_ref), custom_call_target="tpu_custom_call" | custom-call | tf_op jit(solution)/shard_map/pallas_call | solution.py:791
  304.6 11.6 %shard_map.223 = (bf16[4,2,3,192,512]{4,3,2,1,0:T(8,128)(2,1)S(1)}, bf16[8,160,768]{2,1,0:T(8,128)(2,1)S(1)}, f32[8,160,128]{2,1,0:T(8,128)S(1)}) custom-call(bf16[1024,768]{1,0:T(8,128)(2,1)S(1)} %shard_map.221.grad.after, bf16[8,160,128]{2,1,0:T(8,128)(2,1)S(1)} %copy-done.15, bf16[2,2,2,768,512]{4,3,2,1,0:T(8,128)(2,1)} %far_up.7, ...), custom_call_target="tpu_custom_call" | custom-call | tf_op jit(solution)/shard_map/pallas_call | solution.py:64
  324.2 16.6 %shard_map.224 = (bf16[1024,768]{1,0:T(8,128)(2,1)}, bf16[2,4,1280,128]{3,2,1,0:T(8,128)(2,1)}, f32[128,768]{1,0:T(8,128)}) custom-call(bf16[1024,768]{1,0:T(8,128)(2,1)} %copy-done.5, bf16[1024,768]{1,0:T(8,128)(2,1)} %copy-done.10, bf16[8,128,160]{2,1,0:T(8,128)(2,1)} %compare_convert_fusion.back, bf16[128,768]{1,0:T(8,128)(2,1)} %get-tuple-element.160.router, ...), custom_call_target="tpu_custom_call" | custom-call | tf_op jit(solution)/shard_map/pallas_call | solution.py:64
  343.6 13.9 %shard_map.225.after = f32[128,768]{1,0:T(8,128)S(1)} custom-call(bf16[1024,768]{1,0:T(8,128)(2,1)S(1)} %copy-done.28), custom_call_target="tpu_custom_call" | custom-call | tf_op jit(solution)/shard_map/pallas_call | solution.py:930
  367.6 9.2 %shard_map.229 = (bf16[512,768]{1,0:T(8,128)(2,1)S(1)}, bf16[2,4,768,128]{3,2,1,0:T(8,128)(2,1)S(1)}) custom-call(bf16[512,768]{1,0:T(8,128)(2,1)S(1)} %shard_map.226.grad, bf16[512,768]{1,0:T(8,128)(2,1)S(1)} %copy-done.16, bf16[3,768,256]{2,1,0:T(8,128)(2,1)S(1)} %copy-done.38, f32[512,128]{1,0:T(8,128)S(1)} %copy-done.22, f32[512,128]{1,0:T(8,128)S(1)} %copy-done.20, ...), custom_call_target="tpu_custom_call" | custom-call | tf_op jit(solution)/shard_map/pallas_call | solution.py:64
  376.7 8.7 %shard_map.230 = f32[128,768]{1,0:T(8,128)S(1)} custom-call(bf16[512,768]{1,0:T(8,128)(2,1)S(1)} %get-tuple-element.114.p_ref), custom_call_target="tpu_custom_call" | custom-call | tf_op jit(solution)/shard_map/pallas_call | solution.py:930
  390.5 11.7 %shard_map.232.p_ref.after = bf16[1024,768]{1,0:T(8,128)(2,1)} custom-call(bf16[1024,768]{1,0:T(8,128)(2,1)} %copy-done.7, bf16[8,128,160]{2,1,0:T(8,128)(2,1)} %compare_convert_fusion.back, bf16[2,640,1024]{2,1,0:T(8,128)(2,1)} %copy-done.13, f32[2,640,1]{2,1,0:T(8,128)} %copy-done.46, bf16[2,2,512,768]{3,2,1,0:T(8,128)(2,1)} %far_down.7, ...), custom_call_target="tpu_custom_call" | custom-call | tf_op jit(solution)/shard_map/pallas_call | solution.py:64
  412.9 45.2 %psum.7 = f32[2,6,768]{2,1,0:T(8,128)S(1)} all-reduce(f32[2,6,768]{2,1,0:T(8,128)S(1)} %reshape.274), channel_id=1, replica_groups=mesh['dp'=4,'expert'=2,'wshard'=4] {'dp','expert','wshard'}, use_global_device_ids=true, to_apply=%region_17.18 | all-reduce | flops 9216 | bytes 73728 | tf_op jit(solution)/shard_map/psum | solution.py:1151
  463.1 13.0 %shard_map.233 = f32[128,768]{1,0:T(8,128)S(1)} custom-call(bf16[1024,768]{1,0:T(8,128)(2,1)S(1)} %copy-done.9), custom_call_target="tpu_custom_call" | custom-call | tf_op jit(solution)/shard_map/pallas_call | solution.py:930
  476.8 11.1 %reduce-scatter.6.cloned.1.call-done = bf16[1,4096,128]{2,1,0:T(8,128)(2,1)} async-done(((bf16[4,4096,128]{2,1,0:T(8,128)(2,1)}), bf16[1,4096,128]{2,1,0:T(8,128)(2,1)}) %reduce-scatter.6.cloned.1.call-update) | async-done | bytes 1048592 | tf_op jit(solution)/shard_map/reduce_scatter | solution.py:1100
  496.3 29.9 %collective-permute-done.4 = bf16[2,1344,128]{2,1,0:T(8,128)(2,1)S(1)} collective-permute-done((bf16[2,1344,128]{2,1,0:T(8,128)(2,1)S(1)}, bf16[2,1344,128]{2,1,0:T(8,128)(2,1)S(1)}, u32[]{:S(2)}, u32[]{:S(2)}) %collective-permute-start.4) | collective-permute-done | bytes 688160 | tf_op jit(solution)/shard_map/ppermute | solution.py:1161
  (342 shorter events, 155.9 us)
Async XLA Ops:
  51.7 43.2 %all-to-all-start = ((bf16[4,2,192,512]{3,2,1,0:T(8,128)(2,1)}), bf16[4,2,192,512]{3,2,1,0:T(8,128)(2,1)S(1)}, u32[]{:S(2)}, u32[]{:S(2)}) async-start(bf16[4,2,192,512]{3,2,1,0:T(8,128)(2,1)} %get-tuple-element.81), calls=%async_computation | async-start | bytes 3145728 | tf_op jit(solution)/shard_map/all_to_all | solution.py:1025
  57.4 43.2 %copy-start.89 = (bf16[2,6,768]{2,1,0:T(8,128)(2,1)}, bf16[2,6,768]{2,1,0:T(8,128)(2,1)S(1)}, u32[]{:S(2)}) copy-start(bf16[2,6,768]{2,1,0:T(8,128)(2,1)S(1)} %reshape.268) | copy-start | bytes 55300
  61.0 18.4 %copy-start.42 = (bf16[1,128,768]{2,1,0:T(8,128)(2,1)S(1)}, bf16[1,128,768]{2,1,0:T(8,128)(2,1)}, u32[]{:S(2)}) copy-start(bf16[1,128,768]{2,1,0:T(8,128)(2,1)} %param.15) | copy-start | bytes 589828
  79.6 15.3 %copy-start.77 = (f32[128,768]{1,0:T(8,128)}, f32[128,768]{1,0:T(8,128)S(1)}, u32[]{:S(2)}) copy-start(f32[128,768]{1,0:T(8,128)S(1)} %get-tuple-element.143) | copy-start | bytes 1179652
  96.1 58.6 %all-to-all-start.1 = ((bf16[4,4,192,512]{3,2,1,0:T(8,128)(2,1)}), bf16[4,4,192,512]{3,2,1,0:T(8,128)(2,1)S(1)}, u32[]{:S(2)}, u32[]{:S(2)}) async-start(bf16[4,4,192,512]{3,2,1,0:T(8,128)(2,1)} %copy-done.45), calls=%async_computation.1 | async-start | bytes 6291456 | tf_op jit(solution)/shard_map/all_to_all | solution.py:1025
  100.5 223.8 %reduce-scatter.4.cloned.1.call-start = ((), (), s32[]{:S(2)}) async-start(), calls=%async_computation.5 | async-start | bytes 5898240 | tf_op jit(solution)/shard_map/reduce_scatter | solution.py:1100
  106.5 82.5 %copy-start.54 = (bf16[128,768]{1,0:T(8,128)(2,1)}, bf16[128,768]{1,0:T(8,128)(2,1)S(1)}, u32[]{:S(2)}) copy-start(bf16[128,768]{1,0:T(8,128)(2,1)S(1)} %get-tuple-element.159.router) | copy-start | bytes 589828
  128.1 16.3 %copy-start.78 = (f32[128,768]{1,0:T(8,128)S(1)}, f32[128,768]{1,0:T(8,128)}, u32[]{:S(2)}) copy-start(f32[128,768]{1,0:T(8,128)} %copy-done.77) | copy-start | bytes 1179652
  156.3 18.5 %copy-start.81 = (f32[128,768]{1,0:T(8,128)S(1)}, f32[128,768]{1,0:T(8,128)}, u32[]{:S(2)}) copy-start(f32[128,768]{1,0:T(8,128)} %copy-done.80) | copy-start | bytes 1179652
  175.0 25.9 %copy-start.92 = (f32[128]{0:T(128)}, f32[128]{0:T(128)S(1)}, u32[]{:S(2)}) copy-start(f32[128]{0:T(128)S(1)} %add_rsqrt_fusion.2) | copy-start | bytes 1540
  218.9 192.6 %reduce-scatter.8.cloned.1.call-start = ((), (), s32[]{:S(2)}) async-start(), calls=%async_computation.7 | async-start | bytes 5898240 | tf_op jit(solution)/shard_map/reduce_scatter | solution.py:1100
  253.3 48.4 %collective-permute-start = (bf16[4,1280,128]{2,1,0:T(8,128)(2,1)}, bf16[4,1280,128]{2,1,0:T(8,128)(2,1)}, u32[]{:S(2)}, u32[]{:S(2)}) collective-permute-start(bf16[4,1280,128]{2,1,0:T(8,128)(2,1)} %shard_map.222), channel_id=1, source_target_pairs={{0,4},{4,0},{1,5},{5,1},{2,6},{6,2},{3,7},{7,3},{8,12},{12,8},{9,1... | collective-permute-start | bytes 3932168 | tf_op jit(solution)/shard_map/ppermute | solution.py:1087
  267.8 18.8 %copy-start.82 = (f32[128,768]{1,0:T(8,128)S(1)}, f32[128,768]{1,0:T(8,128)}, u32[]{:S(2)}) copy-start(f32[128,768]{1,0:T(8,128)} %copy-done.80) | copy-start | bytes 1179652
  267.8 18.8 %copy-start.100 = (f32[128]{0:T(128)S(1)}, f32[128]{0:T(128)}, u32[]{:S(2)}) copy-start(f32[128]{0:T(128)} %copy-done.99) | copy-start | bytes 1540
  267.8 36.2 %copy-start.51 = (bf16[2,640,768]{2,1,0:T(8,128)(2,1)S(1)}, bf16[2,640,768]{2,1,0:T(8,128)(2,1)}, u32[]{:S(2)}) copy-start(bf16[2,640,768]{2,1,0:T(8,128)(2,1)} %get-tuple-element.100.arrived) | copy-start | bytes 5898244
  277.9 26.1 %copy-start.47 = (bf16[2,640,1024]{2,1,0:T(8,128)(2,1)S(1)}, bf16[2,640,1024]{2,1,0:T(8,128)(2,1)}, u32[]{:S(2)}) copy-start(bf16[2,640,1024]{2,1,0:T(8,128)(2,1)} %get-tuple-element.101.inner) | copy-start | bytes 7864324
  288.4 15.6 %copy-start.61 = (f32[2,640,1]{2,1,0:T(8,128)S(1)}, f32[2,640,1]{2,1,0:T(8,128)}, u32[]{:S(2)}) copy-start(f32[2,640,1]{2,1,0:T(8,128)} %get-tuple-element.102.scale) | copy-start | bytes 15364
  320.4 167.5 %reduce-scatter.6.cloned.1.call-start = ((), (), s32[]{:S(2)}) async-start(), calls=%async_computation.6 | async-start | bytes 5242880 | tf_op jit(solution)/shard_map/reduce_scatter | solution.py:1100
  323.2 44.0 %collective-permute-start.1 = (bf16[4,768,128]{2,1,0:T(8,128)(2,1)}, bf16[4,768,128]{2,1,0:T(8,128)(2,1)S(1)}, u32[]{:S(2)}, u32[]{:S(2)}) collective-permute-start(bf16[4,768,128]{2,1,0:T(8,128)(2,1)} %shard_map.228), channel_id=1, source_target_pairs={{0,4},{4,0},{1,5},{5,1},{2,6},{6,2},{3,7},{7,3},{8,12},{12,8},{9,1... | collective-permute-start | bytes 2359304 | tf_op jit(solution)/shard_map/ppermute | solution.py:1087
  357.7 31.4 %collective-permute-start.2 = (bf16[4,1280,128]{2,1,0:T(8,128)(2,1)S(1)}, bf16[4,1280,128]{2,1,0:T(8,128)(2,1)S(1)}, u32[]{:S(2)}, u32[]{:S(2)}) collective-permute-start(bf16[4,1280,128]{2,1,0:T(8,128)(2,1)S(1)} %shard_map.231), channel_id=1, source_target_pairs={{0,4},{4,0},{1,5},{5,1},{2,6},{6,2},{3,7},{7,3},{8,12},{12,8},{9,1... | collective-permute-start | bytes 3932168 | tf_op jit(solution)/shard_map/ppermute | solution.py:1087
  385.5 20.0 %collective-permute-start.3 = (bf16[4,768,128]{2,1,0:T(8,128)(2,1)S(1)}, bf16[4,768,128]{2,1,0:T(8,128)(2,1)}, u32[]{:S(2)}, u32[]{:S(2)}) collective-permute-start(bf16[4,768,128]{2,1,0:T(8,128)(2,1)S(1)} %shard_map.235), channel_id=1, source_target_pairs={{0,4},{4,0},{1,5},{5,1},{2,6},{6,2},{3,7},{7,3},{8,12},{12,8},{9,1... | collective-permute-start | bytes 2359304 | tf_op jit(solution)/shard_map/ppermute | solution.py:1087
  412.8 46.6 %copy-start.36 = (bf16[1,2,3,192,512]{4,3,2,1,0:T(8,128)(2,1)S(1)}, bf16[1,2,3,192,512]{4,3,2,1,0:T(8,128)(2,1)}, u32[]{:S(2)}) copy-start(bf16[1,2,3,192,512]{4,3,2,1,0:T(8,128)(2,1)} %reduce-scatter.8.cloned.1.call-done) | copy-start | bytes 3538948
  412.8 46.7 %copy-start.83 = (bf16[1,2,3,192,512]{4,3,2,1,0:T(8,128)(2,1)S(1)}, bf16[1,2,3,192,512]{4,3,2,1,0:T(8,128)(2,1)}, u32[]{:S(2)}) copy-start(bf16[1,2,3,192,512]{4,3,2,1,0:T(8,128)(2,1)} %reduce-scatter.4.cloned.1.call-done) | copy-start | bytes 3538948
  490.0 36.2 %collective-permute-start.4 = (bf16[2,1344,128]{2,1,0:T(8,128)(2,1)S(1)}, bf16[2,1344,128]{2,1,0:T(8,128)(2,1)S(1)}, u32[]{:S(2)}, u32[]{:S(2)}) collective-permute-start(bf16[2,1344,128]{2,1,0:T(8,128)(2,1)S(1)} %pad_maximum_fusion.1), channel_id=1, source_target_pairs={{0,0},{1,8},{2,16},{3,24},{8,1},{9,9},{10,17},{11,25},{16,2},{17,1... | collective-permute-start | bytes 2064392 | tf_op jit(solution)/shard_map/ppermute | solution.py:1161
  (88 other events, 475.5 us)
Sparse Core Ops, SparseCore 0:
  219.0 85.9 reduce-scatter.3
  320.5 85.9 reduce-scatter.7
  409.4 78.4 reduce-scatter.5

commit v7 on v6

--- a/solution.py
+++ b/solution.py
@@ -620,14 +620,19 @@
             base += chunk
     own_grad = grad[rows_at(owner, count), :]
     for b in range(columns):
-        dense[b % owners, b // owners, base : base + units, 0:side] = mul_tn(
-            shared_deep[2], own_grad[:, b * side : (b + 1) * side]
-        ).astype(bf16)
+        found = mul_tn(own_grad[:, b * side : (b + 1) * side], shared_deep[2]).astype(bf16)
+        for h in range(units // 128):
+            here = slice(base + h * side, base + (h + 1) * side)
+            dense[b % owners, b // owners, here, :] = found[:, h * 128 : (h + 1) * 128]
+
+
+def down_rows(width, units, planes, owners):
+    return units // 128 * (width // (planes * owners))
 
 
 def dense_rows(width, units, planes, owners):
     part = units // owners
-    return 2 * (part // min(part, 128)) * (width // planes) + units
+    return 2 * (part // min(part, 128)) * (width // planes) + down_rows(width, units, planes, owners)
 
 
 def shared_back(layer, grad, mixed, back, router, wide, narrow, gates, sent, spot, after):
@@ -1123,7 +1128,6 @@
         mixed_grad = reduce(partial, PLANE, 4)
         if pieces:
             pieces.append(near_sum(dense_a, arrivals, partial))
-        gain_b_grad = jnp.sum(mixed_grad * normed_b, axis=0)
         middle_grad = grad + norm_back(mixed_grad * gains[1], normed_b, inverse_b)
         branch_grad = gather(middle_grad.astype(bf16), SLOT, 1)
         partial, dense_a = attend_back(
@@ -1131,13 +1135,10 @@
             attended, out_padded[layer], spread, pieces[1] if pieces else None,
         )
         hidden_grad = reduce(partial, SLOT, 3)
-        gain_a_grad = jnp.sum(hidden_grad * normed_a, axis=0)
         grad = middle_grad + norm_back(hidden_grad * gains[0], normed_a, inverse_a)
         pieces.append(near_sum(dense_b, near_send(dense_b, mixed_grad), None))
         first_rows = dense_b.shape[2]
-        small_grads[layer] = jnp.concatenate(
-            [router_grad[:experts], gain_a_grad[None], gain_b_grad[None]], axis=0
-        )
+        small_grads[layer] = (router_grad, hidden_grad, normed_a, mixed_grad, normed_b)
     grad, mixed = lax.optimization_barrier((grad, saved[-1][11]))
     wide, arrived, inner, scale, gates = saved[-1][12:]
     partial = finish(
@@ -1147,13 +1148,24 @@
     dense = far_sum(jnp.concatenate(pieces, axis=1)).reshape(LAYERS, -1, 128)[::-1]
     reduced = [(reduced[i], dense[i, :first_rows], dense[i, first_rows:]) for i in range(LAYERS)]
     block_out = (middle + reduce(partial, PLANE, 4)).astype(bf16)[None]
+    for layer in range(LAYERS):
+        router_grad, hidden_grad, normed_a, mixed_grad, normed_b = small_grads[layer]
+        if layer > 0:
+            hidden_grad = pick(hidden_grad[None], 0, partial)
+            mixed_grad = pick(mixed_grad[None], 0, partial)
+        gain_a_grad = jnp.sum(hidden_grad * normed_a, axis=0)
+        gain_b_grad = jnp.sum(mixed_grad * normed_b, axis=0)
+        small_grads[layer] = jnp.concatenate(
+            [router_grad[:experts], gain_a_grad[None], gain_b_grad[None]], axis=0
+        )
     small_all = pick(jnp.stack(small_grads, axis=0).reshape(1, lines, width), 0, after)
     small_all = lax.psum(small_all, ("dp", "expert", "wshard"))
     small_all = small_all.reshape(LAYERS, experts + 2, width)
     small_own = lax.dynamic_slice_in_dim(small_all, shard * chunk, chunk, axis=2)
+    low = down_rows(width, units, planes, owners)
     turned = jnp.stack(
         [
-            jnp.concatenate([dense_a[: 3 * chunk], dense_b[: dense_b.shape[0] - units]], axis=0)
+            jnp.concatenate([dense_a[: 3 * chunk], dense_b[: dense_b.shape[0] - low]], axis=0)
             for _, dense_b, dense_a in reduced
         ],
         axis=0,
@@ -1166,7 +1178,9 @@
     up_grad = turned[:, 3 * chunk :, :size].reshape(LAYERS, 2, part // size, chunk, size)
     up_grad = up_grad.transpose(0, 1, 3, 2, 4).reshape(LAYERS, 2, chunk, part)
     out_grad = jnp.stack([item[2][3 * chunk :, :side] for item in reduced], axis=0)
-    down_grad = jnp.stack([item[1][item[1].shape[0] - units :, :side] for item in reduced], axis=0)
+    down_grad = jnp.stack([item[1][item[1].shape[0] - low :] for item in reduced], axis=0)
+    down_grad = down_grad.reshape(LAYERS, units // 128, side, 128).transpose(0, 1, 3, 2)
+    down_grad = down_grad.reshape(LAYERS, units, side)
     return (
         block_out,
         grad.astype(bf16)[None],

time: 544 us -> 534 us (0.982)
  other arithmetic: 30.6 us -> 23.8 us
    pallas_call x18 -> x20, Pallas kernels: 133 us -> 132 us  [call(): pl.pallas_call(kernel, out_shape=tuple((jax.ShapeDtypeStruct(s, d) for s,...]
    unnamed x206 -> x196, local copies, waits for them, and re-layouts: 46 us -> 46.3 us
  transfers between devices with their start and end apart: 10 -> 10, of which waited for: 4 -> 3; matrix products, arithmetic and copies ran while one was open for 7% -> 6% of each run, Pallas kernels for 44% -> 45%
where the time goes in v7:
time: 534 us; the launch traced here: 526 us
  Pallas kernels  320 us (60%)
  local copies, waits for them, and re-layouts  64.1 us (12%)
  blocking collectives  45 us (8%)
  waiting for transfers between devices  38.9 us (7%)
  other arithmetic  23.8 us (4%)
  starting transfers between devices  17.6 us (3%)
  between operations  16.4 us (3%)
    pallas_call x20, Pallas kernels, call(): pl.pallas_call(kernel, out_shape=tuple((jax.ShapeDtypeStruct(s, d) for s,...  132 us
    pallas_call x8, Pallas kernels, reduce(): pl.pallas_call(functools.partial(reduce_kernel, axes), out_shape=jax.Shap...  91.6 us
    pallas_call x6, Pallas kernels, gather(): pl.pallas_call(functools.partial(gather_kernel, axes), out_shape=jax.Shap...  63.9 us
    unnamed x196, local copies, waits for them, and re-layouts  46.3 us
    psum x1, blocking collectives, per_device(): small_all = lax.psum(small_all, ('dp', 'expert', 'wshard'))  45 us
    pallas_call x1, Pallas kernels, begin(): pl.pallas_call(functools.partial(begin_kernel, groups), out_shape=tuple(o...  32.5 us
    ppermute x1, waiting for transfers between devices, per_device(): turned = lax.ppermute(turned, ('dp', 'wshard'), transposed).astype(f32)  29.6 us
  transfers between devices with their start and end apart: 10, of which 3 were waited for; matrix products, arithmetic and copies ran while one was open for 6% of the time, Pallas kernels for 45%

profile of v7, /device:TPU:4, one launch (start us, length us, event | category | flops | bytes accessed | tf_op | source)
XLA Modules:
  0.0 526.0 jit_solution(7487020714704208109)
XLA Ops:
  15.4 32.5 %shard_map.204 = (bf16[512,768]{1,0:T(8,128)(2,1)S(1)}, s32[64,128]{1,0:T(8,128)S(1)}, bf16[64,256]{1,0:T(8,128)(2,1)S(1)}, bf16[1024,768]{1,0:T(8,128)(2,1)S(1)...) custom-call(bf16[128,768]{1,0:T(8,128)(2,1)S(1)} %bitcast.115, ...), custom_call_target="tpu_custom_call" | custom-call | tf_op jit(solution)/shard_map/pallas_call | solution.py:881
  61.0 8.6 %shard_map.205 = (bf16[512,768]{1,0:T(8,128)(2,1)}, bf16[512,256]{1,0:T(8,128)(2,1)}, bf16[512,256]{1,0:T(8,128)(2,1)}, bf16[512,256]{1,0:T(8,128)(2,1)}, bf16[4...) custom-call(bf16[512,768]{1,0:T(8,128)(2,1)} %fusion.4.hidden, bf16[3,768,256]{2,1,0:T(8,128)(2,1)} %copy-done.39, ...), custom_call_target="tpu_custom_call" | custom-call | tf_op jit(solution)/shard_map/pallas_call | solution.py:64
  70.7 8.7 %shard_map.206 = f32[128,768]{1,0:T(8,128)S(1)} custom-call(bf16[512,768]{1,0:T(8,128)(2,1)S(1)} %copy-done.62), custom_call_target="tpu_custom_call" | custom-call | tf_op jit(solution)/shard_map/pallas_call | solution.py:935
  80.4 13.4 %shard_map.207.mixed = bf16[1024,768]{1,0:T(8,128)(2,1)S(1)} custom-call(bf16[128,768]{1,0:T(8,128)(2,1)S(1)} %multiply_convert_fusion.2.x_ref), custom_call_target="tpu_custom_call" | custom-call | tf_op jit(solution)/shard_map/pallas_call | solution.py:796
  108.7 18.2 %shard_map.208 = (bf16[1024,768]{1,0:T(8,128)(2,1)}, bf16[2,640,768]{2,1,0:T(8,128)(2,1)}, bf16[2,640,1024]{2,1,0:T(8,128)(2,1)}, f32[2,640,1]{2,1,0:T(8,128)}, f32[1024,128]{1,0:T(8,128)}) custom-call(bf16[1024,768]{1,0:T(8,128)(2,1)} %copy-done.10, bf16[8,160,128]{2,1,0:T(8,128)(2,1)} %fusion.5.select, bf16[8,128,160]{2,1,0:T(8,128)(2,1)} %compare_convert_fusion.back, ...), custom_call_target="tpu_custom_call" | custom-call | tf_op jit(solution)/shard_map/pallas_call | solution.py:64
  128.3 16.2 %shard_map.209 = f32[128,768]{1,0:T(8,128)S(1)} custom-call(bf16[1024,768]{1,0:T(8,128)(2,1)S(1)} %copy-done.58), custom_call_target="tpu_custom_call" | custom-call | tf_op jit(solution)/shard_map/pallas_call | solution.py:935
  156.3 8.7 %shard_map.211 = (bf16[512,768]{1,0:T(8,128)(2,1)}, bf16[512,256]{1,0:T(8,128)(2,1)}, bf16[512,256]{1,0:T(8,128)(2,1)}, bf16[512,256]{1,0:T(8,128)(2,1)}, bf16[4...) custom-call(bf16[512,768]{1,0:T(8,128)(2,1)} %copy-done.17, bf16[4,4,192,512]{3,2,1,0:T(8,128)(2,1)} %copy-done.1, ...), custom_call_target="tpu_custom_call" | custom-call | tf_op jit(solution)/shard_map/pallas_call | solution.py:64
  166.1 8.7 %shard_map.212 = f32[128,768]{1,0:T(8,128)S(1)} custom-call(bf16[512,768]{1,0:T(8,128)(2,1)S(1)} %copy-done.61), custom_call_target="tpu_custom_call" | custom-call | tf_op jit(solution)/shard_map/pallas_call | solution.py:935
  175.1 13.2 %shard_map.213.mixed = bf16[1024,768]{1,0:T(8,128)(2,1)S(1)} custom-call(bf16[128,768]{1,0:T(8,128)(2,1)S(1)} %multiply_convert_fusion.x_ref), custom_call_target="tpu_custom_call" | custom-call | tf_op jit(solution)/shard_map/pallas_call | solution.py:796
  201.0 12.8 %shard_map.215 = (bf16[4,2,3,192,512]{4,3,2,1,0:T(8,128)(2,1)S(1)}, bf16[8,160,768]{2,1,0:T(8,128)(2,1)S(1)}, f32[8,160,128]{2,1,0:T(8,128)S(1)}) custom-call(bf16[1024,768]{1,0:T(8,128)(2,1)S(1)} %copy-done.24, bf16[8,160,128]{2,1,0:T(8,128)(2,1)S(1)} %copy-done.14, bf16[2,2,2,768,512]{4,3,2,1,0:T(8,128)(2,1)} %far_up.7, ...), custom_call_target="tpu_custom_call" | custom-call | tf_op jit(solution)/shard_map/pallas_call | solution.py:64
  218.3 15.7 %shard_map.216 = (bf16[1024,768]{1,0:T(8,128)(2,1)}, bf16[2,4,1152,128]{3,2,1,0:T(8,128)(2,1)}, f32[128,768]{1,0:T(8,128)}) custom-call(bf16[1024,768]{1,0:T(8,128)(2,1)} %copy-done.23, bf16[1024,768]{1,0:T(8,128)(2,1)} %copy-done.9, bf16[8,128,160]{2,1,0:T(8,128)(2,1)} %compare_convert_fusion.back, bf16[128,768]{1,0:T(8,128)(2,1)} %copy-done.56, ...), custom_call_target="tpu_custom_call" | custom-call | tf_op jit(solution)/shard_map/pallas_call | solution.py:64
  235.5 13.9 %shard_map.217.after = f32[128,768]{1,0:T(8,128)S(1)} custom-call(bf16[1024,768]{1,0:T(8,128)(2,1)S(1)} %copy-done.57), custom_call_target="tpu_custom_call" | custom-call | tf_op jit(solution)/shard_map/pallas_call | solution.py:935
  260.7 8.9 %shard_map.219 = (bf16[512,768]{1,0:T(8,128)(2,1)S(1)}, bf16[2,4,768,128]{3,2,1,0:T(8,128)(2,1)S(1)}) custom-call(bf16[512,768]{1,0:T(8,128)(2,1)S(1)} %shard_map.218.grad, bf16[512,768]{1,0:T(8,128)(2,1)S(1)} %copy-done.18, bf16[4,4,192,512]{3,2,1,0:T(8,128)(2,1)S(1)} %copy-done.2, f32[512,128]{1,0:T(8,128)S(1)} %copy-done.21, f32[512,128]{1,0:T(8,128)S(1)} %copy-done.19, ...), custom_call_target="tpu_custom_call" | custom-call | tf_op jit(solution)/shard_map/pallas_call | solution.py:64
  270.9 8.7 %shard_map.220 = f32[128,768]{1,0:T(8,128)S(1)} custom-call(bf16[512,768]{1,0:T(8,128)(2,1)S(1)} %get-tuple-element.98.p_ref), custom_call_target="tpu_custom_call" | custom-call | tf_op jit(solution)/shard_map/pallas_call | solution.py:935
  280.8 13.3 %shard_map.221.grad.after = bf16[1024,768]{1,0:T(8,128)(2,1)S(1)} custom-call(bf16[128,768]{1,0:T(8,128)(2,1)S(1)} %get-tuple-element.132.x_ref), custom_call_target="tpu_custom_call" | custom-call | tf_op jit(solution)/shard_map/pallas_call | solution.py:796
  297.0 11.4 %shard_map.223 = (bf16[4,2,3,192,512]{4,3,2,1,0:T(8,128)(2,1)S(1)}, bf16[8,160,768]{2,1,0:T(8,128)(2,1)S(1)}, f32[8,160,128]{2,1,0:T(8,128)S(1)}) custom-call(bf16[1024,768]{1,0:T(8,128)(2,1)S(1)} %shard_map.221.grad.after, bf16[8,160,128]{2,1,0:T(8,128)(2,1)S(1)} %copy-done.15, bf16[2,2,2,768,512]{4,3,2,1,0:T(8,128)(2,1)} %far_up.7, ...), custom_call_target="tpu_custom_call" | custom-call | tf_op jit(solution)/shard_map/pallas_call | solution.py:64
  316.7 16.1 %shard_map.224 = (bf16[1024,768]{1,0:T(8,128)(2,1)}, bf16[2,4,1152,128]{3,2,1,0:T(8,128)(2,1)}, f32[128,768]{1,0:T(8,128)}) custom-call(bf16[1024,768]{1,0:T(8,128)(2,1)} %copy-done.7, bf16[1024,768]{1,0:T(8,128)(2,1)} %copy-done.10, bf16[8,128,160]{2,1,0:T(8,128)(2,1)} %compare_convert_fusion.back, bf16[128,768]{1,0:T(8,128)(2,1)} %get-tuple-element.158.router, ...), custom_call_target="tpu_custom_call" | custom-call | tf_op jit(solution)/shard_map/pallas_call | solution.py:64
  334.2 13.9 %shard_map.225.after = f32[128,768]{1,0:T(8,128)S(1)} custom-call(bf16[1024,768]{1,0:T(8,128)(2,1)S(1)} %copy-done.27), custom_call_target="tpu_custom_call" | custom-call | tf_op jit(solution)/shard_map/pallas_call | solution.py:935
  360.8 8.9 %shard_map.229 = (bf16[512,768]{1,0:T(8,128)(2,1)S(1)}, bf16[2,4,768,128]{3,2,1,0:T(8,128)(2,1)S(1)}) custom-call(bf16[512,768]{1,0:T(8,128)(2,1)S(1)} %shard_map.226.grad, bf16[512,768]{1,0:T(8,128)(2,1)S(1)} %copy-done.16, bf16[3,768,256]{2,1,0:T(8,128)(2,1)S(1)} %copy-done.40, f32[512,128]{1,0:T(8,128)S(1)} %copy-done.22, f32[512,128]{1,0:T(8,128)S(1)} %copy-done.20, ...), custom_call_target="tpu_custom_call" | custom-call | tf_op jit(solution)/shard_map/pallas_call | solution.py:64
  369.7 8.7 %shard_map.230 = f32[128,768]{1,0:T(8,128)S(1)} custom-call(bf16[512,768]{1,0:T(8,128)(2,1)S(1)} %get-tuple-element.114.p_ref), custom_call_target="tpu_custom_call" | custom-call | tf_op jit(solution)/shard_map/pallas_call | solution.py:935
  382.3 11.6 %shard_map.232.p_ref.after = bf16[1024,768]{1,0:T(8,128)(2,1)} custom-call(bf16[1024,768]{1,0:T(8,128)(2,1)} %copy-done.9, bf16[8,128,160]{2,1,0:T(8,128)(2,1)} %compare_convert_fusion.back, bf16[2,640,1024]{2,1,0:T(8,128)(2,1)} %copy-done.13, f32[2,640,1]{2,1,0:T(8,128)} %copy-done.48, bf16[2,2,512,768]{3,2,1,0:T(8,128)(2,1)} %far_down.7, ...), custom_call_target="tpu_custom_call" | custom-call | tf_op jit(solution)/shard_map/pallas_call | solution.py:64
  403.6 13.0 %shard_map.233 = f32[128,768]{1,0:T(8,128)S(1)} custom-call(bf16[1024,768]{1,0:T(8,128)(2,1)S(1)} %copy-done.6), custom_call_target="tpu_custom_call" | custom-call | tf_op jit(solution)/shard_map/pallas_call | solution.py:935
  420.0 45.0 %psum.7 = f32[2,6,768]{2,1,0:T(8,128)S(1)} all-reduce(f32[2,6,768]{2,1,0:T(8,128)S(1)} %reshape.284), channel_id=1, replica_groups=mesh['dp'=4,'expert'=2,'wshard'=4] {'dp','expert','wshard'}, use_global_device_ids=true, to_apply=%region_17.18 | all-reduce | flops 9216 | bytes 73728 | tf_op jit(solution)/shard_map/psum | solution.py:1162
  486.4 29.6 %collective-permute-done.4 = bf16[2,1344,128]{2,1,0:T(8,128)(2,1)S(1)} collective-permute-done((bf16[2,1344,128]{2,1,0:T(8,128)(2,1)S(1)}, bf16[2,1344,128]{2,1,0:T(8,128)(2,1)S(1)}, u32[]{:S(2)}, u32[]{:S(2)}) %collective-permute-start.4) | collective-permute-done | bytes 688160 | tf_op jit(solution)/shard_map/ppermute | solution.py:1173
  (336 shorter events, 150.0 us)
Async XLA Ops:
  51.7 43.4 %all-to-all-start = ((bf16[4,2,192,512]{3,2,1,0:T(8,128)(2,1)}), bf16[4,2,192,512]{3,2,1,0:T(8,128)(2,1)S(1)}, u32[]{:S(2)}, u32[]{:S(2)}) async-start(bf16[4,2,192,512]{3,2,1,0:T(8,128)(2,1)} %get-tuple-element.81), calls=%async_computation | async-start | bytes 3145728 | tf_op jit(solution)/shard_map/all_to_all | solution.py:1030
  57.4 43.3 %copy-start.91 = (bf16[2,6,768]{2,1,0:T(8,128)(2,1)}, bf16[2,6,768]{2,1,0:T(8,128)(2,1)S(1)}, u32[]{:S(2)}) copy-start(bf16[2,6,768]{2,1,0:T(8,128)(2,1)S(1)} %reshape.278) | copy-start | bytes 55300
  61.0 18.4 %copy-start.44 = (bf16[1,128,768]{2,1,0:T(8,128)(2,1)S(1)}, bf16[1,128,768]{2,1,0:T(8,128)(2,1)}, u32[]{:S(2)}) copy-start(bf16[1,128,768]{2,1,0:T(8,128)(2,1)} %param.15) | copy-start | bytes 589828
  96.2 58.4 %all-to-all-start.1 = ((bf16[4,4,192,512]{3,2,1,0:T(8,128)(2,1)}), bf16[4,4,192,512]{3,2,1,0:T(8,128)(2,1)S(1)}, u32[]{:S(2)}, u32[]{:S(2)}) async-start(bf16[4,4,192,512]{3,2,1,0:T(8,128)(2,1)} %copy-done.47), calls=%async_computation.1 | async-start | bytes 6291456 | tf_op jit(solution)/shard_map/all_to_all | solution.py:1030
  100.6 216.0 %reduce-scatter.4.cloned.1.call-start = ((), (), s32[]{:S(2)}) async-start(), calls=%async_computation.5 | async-start | bytes 5898240 | tf_op jit(solution)/shard_map/reduce_scatter | solution.py:1105
  106.7 81.6 %copy-start.56 = (bf16[128,768]{1,0:T(8,128)(2,1)}, bf16[128,768]{1,0:T(8,128)(2,1)S(1)}, u32[]{:S(2)}) copy-start(bf16[128,768]{1,0:T(8,128)(2,1)S(1)} %get-tuple-element.157.router) | copy-start | bytes 589828
  128.3 16.2 %copy-start.84 = (f32[128,768]{1,0:T(8,128)S(1)}, f32[128,768]{1,0:T(8,128)}, u32[]{:S(2)}) copy-start(f32[128,768]{1,0:T(8,128)} %copy-done.83) | copy-start | bytes 1179652
  144.7 135.1 %copy-start.94 = (f32[128]{0:T(128)}, f32[128]{0:T(128)S(1)}, u32[]{:S(2)}) copy-start(f32[128]{0:T(128)S(1)} %add_rsqrt_fusion.3) | copy-start | bytes 1540
  156.3 18.5 %copy-start.78 = (f32[128,768]{1,0:T(8,128)S(1)}, f32[128,768]{1,0:T(8,128)}, u32[]{:S(2)}) copy-start(f32[128,768]{1,0:T(8,128)} %copy-done.77) | copy-start | bytes 1179652
  175.0 104.8 %copy-start.75 = (f32[128,768]{1,0:T(8,128)}, f32[128,768]{1,0:T(8,128)S(1)}, u32[]{:S(2)}) copy-start(f32[128,768]{1,0:T(8,128)S(1)} %get-tuple-element.135) | copy-start | bytes 1179652
  218.2 200.5 %reduce-scatter.8.cloned.1.call-start = ((), (), s32[]{:S(2)}) async-start(), calls=%async_computation.7 | async-start | bytes 5898240 | tf_op jit(solution)/shard_map/reduce_scatter | solution.py:1105
  218.3 42.3 %copy-start.59 = (bf16[256,256]{1,0:T(8,128)(2,1)}, bf16[256,256]{1,0:T(8,128)(2,1)S(1)}, u32[]{:S(2)}) copy-start(bf16[256,256]{1,0:T(8,128)(2,1)S(1)} %fusion.16.spread) | copy-start | bytes 393220
  218.3 42.3 %copy-start.51 = (bf16[4,512,512]{2,1,0:T(8,128)(2,1)S(1)}, bf16[4,512,512]{2,1,0:T(8,128)(2,1)}, u32[]{:S(2)}) copy-start(bf16[4,512,512]{2,1,0:T(8,128)(2,1)} %get-tuple-element.96.probs) | copy-start | bytes 6291460
  251.3 42.8 %collective-permute-start = (bf16[4,1152,128]{2,1,0:T(8,128)(2,1)S(1)}, bf16[4,1152,128]{2,1,0:T(8,128)(2,1)S(1)}, u32[]{:S(2)}, u32[]{:S(2)}) collective-permute-start(bf16[4,1152,128]{2,1,0:T(8,128)(2,1)S(1)} %shard_map.222), channel_id=1, source_target_pairs={{0,4},{4,0},{1,5},{5,1},{2,6},{6,2},{3,7},{7,3},{8,12},{12,8},{9,1... | collective-permute-start | bytes 3538952 | tf_op jit(solution)/shard_map/ppermute | solution.py:1092
  260.7 18.8 %copy-start.79 = (f32[128,768]{1,0:T(8,128)S(1)}, f32[128,768]{1,0:T(8,128)}, u32[]{:S(2)}) copy-start(f32[128,768]{1,0:T(8,128)} %copy-done.77) | copy-start | bytes 1179652
  260.7 34.5 %copy-start.53 = (bf16[2,640,768]{2,1,0:T(8,128)(2,1)S(1)}, bf16[2,640,768]{2,1,0:T(8,128)(2,1)}, u32[]{:S(2)}) copy-start(bf16[2,640,768]{2,1,0:T(8,128)(2,1)} %get-tuple-element.100.arrived) | copy-start | bytes 5898244
  270.9 24.4 %copy-start.49 = (bf16[2,640,1024]{2,1,0:T(8,128)(2,1)S(1)}, bf16[2,640,1024]{2,1,0:T(8,128)(2,1)}, u32[]{:S(2)}) copy-start(bf16[2,640,1024]{2,1,0:T(8,128)(2,1)} %get-tuple-element.101.inner) | copy-start | bytes 7864324
  312.7 163.6 %reduce-scatter.6.cloned.1.call-start = ((), (), s32[]{:S(2)}) async-start(), calls=%async_computation.6 | async-start | bytes 4915200 | tf_op jit(solution)/shard_map/reduce_scatter | solution.py:1105
  315.8 44.7 %collective-permute-start.1 = (bf16[4,768,128]{2,1,0:T(8,128)(2,1)}, bf16[4,768,128]{2,1,0:T(8,128)(2,1)S(1)}, u32[]{:S(2)}, u32[]{:S(2)}) collective-permute-start(bf16[4,768,128]{2,1,0:T(8,128)(2,1)} %shard_map.228), channel_id=1, source_target_pairs={{0,4},{4,0},{1,5},{5,1},{2,6},{6,2},{3,7},{7,3},{8,12},{12,8},{9,1... | collective-permute-start | bytes 2359304 | tf_op jit(solution)/shard_map/ppermute | solution.py:1092
  349.9 31.0 %collective-permute-start.2 = (bf16[4,1152,128]{2,1,0:T(8,128)(2,1)S(1)}, bf16[4,1152,128]{2,1,0:T(8,128)(2,1)S(1)}, u32[]{:S(2)}, u32[]{:S(2)}) collective-permute-start(bf16[4,1152,128]{2,1,0:T(8,128)(2,1)S(1)} %shard_map.231), channel_id=1, source_target_pairs={{0,4},{4,0},{1,5},{5,1},{2,6},{6,2},{3,7},{7,3},{8,12},{12,8},{9,1... | collective-permute-start | bytes 3538952 | tf_op jit(solution)/shard_map/ppermute | solution.py:1092
  378.8 19.6 %collective-permute-start.3 = (bf16[4,768,128]{2,1,0:T(8,128)(2,1)S(1)}, bf16[4,768,128]{2,1,0:T(8,128)(2,1)}, u32[]{:S(2)}, u32[]{:S(2)}) collective-permute-start(bf16[4,768,128]{2,1,0:T(8,128)(2,1)S(1)} %shard_map.235), channel_id=1, source_target_pairs={{0,4},{4,0},{1,5},{5,1},{2,6},{6,2},{3,7},{7,3},{8,12},{12,8},{9,1... | collective-permute-start | bytes 2359304 | tf_op jit(solution)/shard_map/ppermute | solution.py:1092
  419.9 46.4 %copy-start.38 = (bf16[1,2,3,192,512]{4,3,2,1,0:T(8,128)(2,1)S(1)}, bf16[1,2,3,192,512]{4,3,2,1,0:T(8,128)(2,1)}, u32[]{:S(2)}) copy-start(bf16[1,2,3,192,512]{4,3,2,1,0:T(8,128)(2,1)} %reduce-scatter.8.cloned.1.call-done) | copy-start | bytes 3538948
  419.9 46.5 %copy-start.86 = (bf16[1,2,3,192,512]{4,3,2,1,0:T(8,128)(2,1)S(1)}, bf16[1,2,3,192,512]{4,3,2,1,0:T(8,128)(2,1)}, u32[]{:S(2)}) copy-start(bf16[1,2,3,192,512]{4,3,2,1,0:T(8,128)(2,1)} %reduce-scatter.4.cloned.1.call-done) | copy-start | bytes 3538948
  479.8 36.2 %collective-permute-start.4 = (bf16[2,1344,128]{2,1,0:T(8,128)(2,1)S(1)}, bf16[2,1344,128]{2,1,0:T(8,128)(2,1)S(1)}, u32[]{:S(2)}, u32[]{:S(2)}) collective-permute-start(bf16[2,1344,128]{2,1,0:T(8,128)(2,1)S(1)} %pad_maximum_fusion.1), channel_id=1, source_target_pairs={{0,0},{1,8},{2,16},{3,24},{8,1},{9,9},{10,17},{11,25},{16,2},{17,1... | collective-permute-start | bytes 2064392 | tf_op jit(solution)/shard_map/ppermute | solution.py:1173
  (84 other events, 461.9 us)
Sparse Core Ops, SparseCore 0:
  218.3 85.9 reduce-scatter.3
  312.9 85.9 reduce-scatter.7
  402.0 74.2 reduce-scatter.5

commit v8 on v7

--- a/solution.py
+++ b/solution.py
@@ -1117,7 +1117,7 @@
             arrivals = near_send(dense_a, grad_plane)
         totals, sent, heat = routed_back(
             layer, grad_plane, select, expert_up, expert_down, arrived, inner, scale,
-            pieces[0] if pieces else None,
+            crossed[-1] if pieces else None,
         )
         partial, dense_b, router_grad = shared_back(
             layer, grad_plane, mixed, back, router_full[layer], wide, shared_down, gates, sent, heat,
@@ -1136,7 +1136,8 @@
         )
         hidden_grad = reduce(partial, SLOT, 3)
         grad = middle_grad + norm_back(hidden_grad * gains[0], normed_a, inverse_a)
-        pieces.append(near_sum(dense_b, near_send(dense_b, mixed_grad), None))
+        crossed = near_send(dense_b, mixed_grad)
+        pieces.append(near_sum(dense_b, crossed, None))
         first_rows = dense_b.shape[2]
         small_grads[layer] = (router_grad, hidden_grad, normed_a, mixed_grad, normed_b)
     grad, mixed = lax.optimization_barrier((grad, saved[-1][11]))

time: 534 us -> 534 us (level)
    unnamed x196 -> x198, local copies, waits for them, and re-layouts: 46.3 us -> 44.2 us
where the time goes in v8:
time: 534 us; the launch traced here: 526 us
  Pallas kernels  321 us (60%)
  local copies, waits for them, and re-layouts  61.9 us (12%)
  blocking collectives  45.3 us (8%)
  waiting for transfers between devices  38.7 us (7%)
  other arithmetic  24.8 us (5%)
  starting transfers between devices  17.5 us (3%)
  between operations  16.5 us (3%)
    pallas_call x20, Pallas kernels, call(): pl.pallas_call(kernel, out_shape=tuple((jax.ShapeDtypeStruct(s, d) for s,...  133 us
    pallas_call x8, Pallas kernels, reduce(): pl.pallas_call(functools.partial(reduce_kernel, axes), out_shape=jax.Shap...  91.7 us
    pallas_call x6, Pallas kernels, gather(): pl.pallas_call(functools.partial(gather_kernel, axes), out_shape=jax.Shap...  64 us
    psum x1, blocking collectives, per_device(): small_all = lax.psum(small_all, ('dp', 'expert', 'wshard'))  45.3 us
    unnamed x198, local copies, waits for them, and re-layouts  44.2 us
    pallas_call x1, Pallas kernels, begin(): pl.pallas_call(functools.partial(begin_kernel, groups), out_shape=tuple(o...  32.4 us
    ppermute x1, waiting for transfers between devices, per_device(): turned = lax.ppermute(turned, ('dp', 'wshard'), transposed).astype(f32)  29.7 us
  transfers between devices with their start and end apart: 10, of which 3 were waited for; matrix products, arithmetic and copies ran while one was open for 6% of the time, Pallas kernels for 45%

profile of v8, /device:TPU:4, one launch (start us, length us, event | category | flops | bytes accessed | tf_op | source)
XLA Modules:
  0.0 526.1 jit_solution(1763046202893883631)
XLA Ops:
  15.4 32.4 %shard_map.204 = (bf16[512,768]{1,0:T(8,128)(2,1)S(1)}, s32[64,128]{1,0:T(8,128)S(1)}, bf16[64,256]{1,0:T(8,128)(2,1)S(1)}, bf16[1024,768]{1,0:T(8,128)(2,1)S(1)...) custom-call(bf16[128,768]{1,0:T(8,128)(2,1)S(1)} %bitcast.115, ...), custom_call_target="tpu_custom_call" | custom-call | tf_op jit(solution)/shard_map/pallas_call | solution.py:881
  61.0 8.6 %shard_map.205 = (bf16[512,768]{1,0:T(8,128)(2,1)}, bf16[512,256]{1,0:T(8,128)(2,1)}, bf16[512,256]{1,0:T(8,128)(2,1)}, bf16[512,256]{1,0:T(8,128)(2,1)}, bf16[4...) custom-call(bf16[512,768]{1,0:T(8,128)(2,1)} %fusion.4.hidden, bf16[3,768,256]{2,1,0:T(8,128)(2,1)} %copy-done.39, ...), custom_call_target="tpu_custom_call" | custom-call | tf_op jit(solution)/shard_map/pallas_call | solution.py:64
  70.7 8.7 %shard_map.206 = f32[128,768]{1,0:T(8,128)S(1)} custom-call(bf16[512,768]{1,0:T(8,128)(2,1)S(1)} %copy-done.62), custom_call_target="tpu_custom_call" | custom-call | tf_op jit(solution)/shard_map/pallas_call | solution.py:935
  80.4 13.4 %shard_map.207.mixed = bf16[1024,768]{1,0:T(8,128)(2,1)S(1)} custom-call(bf16[128,768]{1,0:T(8,128)(2,1)S(1)} %multiply_convert_fusion.2.x_ref), custom_call_target="tpu_custom_call" | custom-call | tf_op jit(solution)/shard_map/pallas_call | solution.py:796
  108.7 18.2 %shard_map.208 = (bf16[1024,768]{1,0:T(8,128)(2,1)}, bf16[2,640,768]{2,1,0:T(8,128)(2,1)}, bf16[2,640,1024]{2,1,0:T(8,128)(2,1)}, f32[2,640,1]{2,1,0:T(8,128)}, f32[1024,128]{1,0:T(8,128)}) custom-call(bf16[1024,768]{1,0:T(8,128)(2,1)} %copy-done.10, bf16[8,160,128]{2,1,0:T(8,128)(2,1)} %fusion.5.select, bf16[8,128,160]{2,1,0:T(8,128)(2,1)} %compare_convert_fusion.back, ...), custom_call_target="tpu_custom_call" | custom-call | tf_op jit(solution)/shard_map/pallas_call | solution.py:64
  128.3 16.2 %shard_map.209 = f32[128,768]{1,0:T(8,128)S(1)} custom-call(bf16[1024,768]{1,0:T(8,128)(2,1)S(1)} %copy-done.58), custom_call_target="tpu_custom_call" | custom-call | tf_op jit(solution)/shard_map/pallas_call | solution.py:935
  156.3 8.7 %shard_map.211 = (bf16[512,768]{1,0:T(8,128)(2,1)}, bf16[512,256]{1,0:T(8,128)(2,1)}, bf16[512,256]{1,0:T(8,128)(2,1)}, bf16[512,256]{1,0:T(8,128)(2,1)}, bf16[4...) custom-call(bf16[512,768]{1,0:T(8,128)(2,1)} %copy-done.15, bf16[4,4,192,512]{3,2,1,0:T(8,128)(2,1)} %copy-done.1, ...), custom_call_target="tpu_custom_call" | custom-call | tf_op jit(solution)/shard_map/pallas_call | solution.py:64
  166.2 8.7 %shard_map.212 = f32[128,768]{1,0:T(8,128)S(1)} custom-call(bf16[512,768]{1,0:T(8,128)(2,1)S(1)} %copy-done.61), custom_call_target="tpu_custom_call" | custom-call | tf_op jit(solution)/shard_map/pallas_call | solution.py:935
  175.1 13.2 %shard_map.213.mixed = bf16[1024,768]{1,0:T(8,128)(2,1)S(1)} custom-call(bf16[128,768]{1,0:T(8,128)(2,1)S(1)} %multiply_convert_fusion.x_ref), custom_call_target="tpu_custom_call" | custom-call | tf_op jit(solution)/shard_map/pallas_call | solution.py:796
  201.0 12.8 %shard_map.215 = (bf16[4,2,3,192,512]{4,3,2,1,0:T(8,128)(2,1)S(1)}, bf16[8,160,768]{2,1,0:T(8,128)(2,1)S(1)}, f32[8,160,128]{2,1,0:T(8,128)S(1)}) custom-call(bf16[1024,768]{1,0:T(8,128)(2,1)S(1)} %copy-done.22, bf16[8,160,128]{2,1,0:T(8,128)(2,1)S(1)} %copy-done.12, bf16[2,2,2,768,512]{4,3,2,1,0:T(8,128)(2,1)} %far_up.7, ...), custom_call_target="tpu_custom_call" | custom-call | tf_op jit(solution)/shard_map/pallas_call | solution.py:64
  218.3 15.7 %shard_map.216 = (bf16[1024,768]{1,0:T(8,128)(2,1)}, bf16[2,4,1152,128]{3,2,1,0:T(8,128)(2,1)}, f32[128,768]{1,0:T(8,128)}) custom-call(bf16[1024,768]{1,0:T(8,128)(2,1)} %copy-done.21, bf16[1024,768]{1,0:T(8,128)(2,1)} %copy-done.9, bf16[8,128,160]{2,1,0:T(8,128)(2,1)} %compare_convert_fusion.back, bf16[128,768]{1,0:T(8,128)(2,1)} %copy-done.56, ...), custom_call_target="tpu_custom_call" | custom-call | tf_op jit(solution)/shard_map/pallas_call | solution.py:64
  235.5 13.9 %shard_map.217.after = f32[128,768]{1,0:T(8,128)S(1)} custom-call(bf16[1024,768]{1,0:T(8,128)(2,1)S(1)} %copy-done.57), custom_call_target="tpu_custom_call" | custom-call | tf_op jit(solution)/shard_map/pallas_call | solution.py:935
  260.8 8.9 %shard_map.219 = (bf16[512,768]{1,0:T(8,128)(2,1)S(1)}, bf16[2,4,768,128]{3,2,1,0:T(8,128)(2,1)S(1)}) custom-call(bf16[512,768]{1,0:T(8,128)(2,1)S(1)} %shard_map.218.grad, bf16[512,768]{1,0:T(8,128)(2,1)S(1)} %copy-done.16, bf16[4,4,192,512]{3,2,1,0:T(8,128)(2,1)S(1)} %copy-done.2, f32[512,128]{1,0:T(8,128)S(1)} %copy-done.19, f32[512,128]{1,0:T(8,128)S(1)} %copy-done.17, ...), custom_call_target="tpu_custom_call" | custom-call | tf_op jit(solution)/shard_map/pallas_call | solution.py:64
  270.9 8.7 %shard_map.220 = f32[128,768]{1,0:T(8,128)S(1)} custom-call(bf16[512,768]{1,0:T(8,128)(2,1)S(1)} %get-tuple-element.98.p_ref), custom_call_target="tpu_custom_call" | custom-call | tf_op jit(solution)/shard_map/pallas_call | solution.py:935
  280.9 13.2 %shard_map.221.grad.after = bf16[1024,768]{1,0:T(8,128)(2,1)S(1)} custom-call(bf16[128,768]{1,0:T(8,128)(2,1)S(1)} %get-tuple-element.132.x_ref), custom_call_target="tpu_custom_call" | custom-call | tf_op jit(solution)/shard_map/pallas_call | solution.py:796
  294.2 12.3 %shard_map.223 = (bf16[4,2,3,192,512]{4,3,2,1,0:T(8,128)(2,1)S(1)}, bf16[8,160,768]{2,1,0:T(8,128)(2,1)S(1)}, f32[8,160,128]{2,1,0:T(8,128)S(1)}) custom-call(bf16[1024,768]{1,0:T(8,128)(2,1)S(1)} %shard_map.221.grad.after, bf16[8,160,128]{2,1,0:T(8,128)(2,1)S(1)} %copy-done.13, bf16[2,2,2,768,512]{4,3,2,1,0:T(8,128)(2,1)} %far_up.7, ...), custom_call_target="tpu_custom_call" | custom-call | tf_op jit(solution)/shard_map/pallas_call | solution.py:64
  316.4 16.5 %shard_map.224 = (bf16[1024,768]{1,0:T(8,128)(2,1)}, bf16[2,4,1152,128]{3,2,1,0:T(8,128)(2,1)}, f32[128,768]{1,0:T(8,128)}) custom-call(bf16[1024,768]{1,0:T(8,128)(2,1)} %copy-done.7, bf16[1024,768]{1,0:T(8,128)(2,1)} %copy-done.10, bf16[8,128,160]{2,1,0:T(8,128)(2,1)} %compare_convert_fusion.back, bf16[128,768]{1,0:T(8,128)(2,1)} %get-tuple-element.158.router, ...), custom_call_target="tpu_custom_call" | custom-call | tf_op jit(solution)/shard_map/pallas_call | solution.py:64
  334.3 13.8 %shard_map.225.after = f32[128,768]{1,0:T(8,128)S(1)} custom-call(bf16[1024,768]{1,0:T(8,128)(2,1)S(1)} %copy-done.25), custom_call_target="tpu_custom_call" | custom-call | tf_op jit(solution)/shard_map/pallas_call | solution.py:935
  360.7 9.2 %shard_map.229 = (bf16[512,768]{1,0:T(8,128)(2,1)S(1)}, bf16[2,4,768,128]{3,2,1,0:T(8,128)(2,1)S(1)}) custom-call(bf16[512,768]{1,0:T(8,128)(2,1)S(1)} %shard_map.226.grad, bf16[512,768]{1,0:T(8,128)(2,1)S(1)} %copy-done.14, bf16[3,768,256]{2,1,0:T(8,128)(2,1)S(1)} %copy-done.40, f32[512,128]{1,0:T(8,128)S(1)} %copy-done.20, f32[512,128]{1,0:T(8,128)S(1)} %copy-done.18, ...), custom_call_target="tpu_custom_call" | custom-call | tf_op jit(solution)/shard_map/pallas_call | solution.py:64
  369.9 8.7 %shard_map.230 = f32[128,768]{1,0:T(8,128)S(1)} custom-call(bf16[512,768]{1,0:T(8,128)(2,1)S(1)} %get-tuple-element.114.p_ref), custom_call_target="tpu_custom_call" | custom-call | tf_op jit(solution)/shard_map/pallas_call | solution.py:935
  382.3 11.6 %shard_map.232.p_ref.after = bf16[1024,768]{1,0:T(8,128)(2,1)} custom-call(bf16[1024,768]{1,0:T(8,128)(2,1)} %copy-done.9, bf16[8,128,160]{2,1,0:T(8,128)(2,1)} %compare_convert_fusion.back, bf16[2,640,1024]{2,1,0:T(8,128)(2,1)} %copy-done.11, f32[2,640,1]{2,1,0:T(8,128)} %copy-done.48, bf16[2,2,512,768]{3,2,1,0:T(8,128)(2,1)} %far_down.7, ...), custom_call_target="tpu_custom_call" | custom-call | tf_op jit(solution)/shard_map/pallas_call | solution.py:64
  403.4 13.1 %shard_map.233 = f32[128,768]{1,0:T(8,128)S(1)} custom-call(bf16[1024,768]{1,0:T(8,128)(2,1)S(1)} %copy-done.6), custom_call_target="tpu_custom_call" | custom-call | tf_op jit(solution)/shard_map/pallas_call | solution.py:935
  420.0 45.3 %psum.7 = f32[2,6,768]{2,1,0:T(8,128)S(1)} all-reduce(f32[2,6,768]{2,1,0:T(8,128)S(1)} %reshape.284), channel_id=1, replica_groups=mesh['dp'=4,'expert'=2,'wshard'=4] {'dp','expert','wshard'}, use_global_device_ids=true, to_apply=%region_17.18 | all-reduce | flops 9216 | bytes 73728 | tf_op jit(solution)/shard_map/psum | solution.py:1163
  486.4 29.7 %collective-permute-done.4 = bf16[2,1344,128]{2,1,0:T(8,128)(2,1)S(1)} collective-permute-done((bf16[2,1344,128]{2,1,0:T(8,128)(2,1)S(1)}, bf16[2,1344,128]{2,1,0:T(8,128)(2,1)S(1)}, u32[]{:S(2)}, u32[]{:S(2)}) %collective-permute-start.4) | collective-permute-done | bytes 688160 | tf_op jit(solution)/shard_map/ppermute | solution.py:1174
  (338 shorter events, 148.0 us)
Async XLA Ops:
  51.7 43.4 %all-to-all-start = ((bf16[4,2,192,512]{3,2,1,0:T(8,128)(2,1)}), bf16[4,2,192,512]{3,2,1,0:T(8,128)(2,1)S(1)}, u32[]{:S(2)}, u32[]{:S(2)}) async-start(bf16[4,2,192,512]{3,2,1,0:T(8,128)(2,1)} %get-tuple-element.81), calls=%async_computation | async-start | bytes 3145728 | tf_op jit(solution)/shard_map/all_to_all | solution.py:1030
  57.4 43.3 %copy-start.92 = (bf16[2,6,768]{2,1,0:T(8,128)(2,1)}, bf16[2,6,768]{2,1,0:T(8,128)(2,1)S(1)}, u32[]{:S(2)}) copy-start(bf16[2,6,768]{2,1,0:T(8,128)(2,1)S(1)} %reshape.278) | copy-start | bytes 55300
  61.0 18.4 %copy-start.44 = (bf16[1,128,768]{2,1,0:T(8,128)(2,1)S(1)}, bf16[1,128,768]{2,1,0:T(8,128)(2,1)}, u32[]{:S(2)}) copy-start(bf16[1,128,768]{2,1,0:T(8,128)(2,1)} %param.15) | copy-start | bytes 589828
  96.2 58.4 %all-to-all-start.1 = ((bf16[4,4,192,512]{3,2,1,0:T(8,128)(2,1)}), bf16[4,4,192,512]{3,2,1,0:T(8,128)(2,1)S(1)}, u32[]{:S(2)}, u32[]{:S(2)}) async-start(bf16[4,4,192,512]{3,2,1,0:T(8,128)(2,1)} %copy-done.47), calls=%async_computation.1 | async-start | bytes 6291456 | tf_op jit(solution)/shard_map/all_to_all | solution.py:1030
  100.6 215.8 %reduce-scatter.4.cloned.1.call-start = ((), (), s32[]{:S(2)}) async-start(), calls=%async_computation.5 | async-start | bytes 5898240 | tf_op jit(solution)/shard_map/reduce_scatter | solution.py:1105
  106.6 81.7 %copy-start.56 = (bf16[128,768]{1,0:T(8,128)(2,1)}, bf16[128,768]{1,0:T(8,128)(2,1)S(1)}, u32[]{:S(2)}) copy-start(bf16[128,768]{1,0:T(8,128)(2,1)S(1)} %get-tuple-element.157.router) | copy-start | bytes 589828
  144.6 135.2 %copy-start.95 = (f32[128]{0:T(128)}, f32[128]{0:T(128)S(1)}, u32[]{:S(2)}) copy-start(f32[128]{0:T(128)S(1)} %add_rsqrt_fusion.3) | copy-start | bytes 1540
  156.3 18.6 %copy-start.78 = (f32[128,768]{1,0:T(8,128)S(1)}, f32[128,768]{1,0:T(8,128)}, u32[]{:S(2)}) copy-start(f32[128,768]{1,0:T(8,128)} %copy-done.77) | copy-start | bytes 1179652
  175.0 104.8 %copy-start.75 = (f32[128,768]{1,0:T(8,128)}, f32[128,768]{1,0:T(8,128)S(1)}, u32[]{:S(2)}) copy-start(f32[128,768]{1,0:T(8,128)S(1)} %get-tuple-element.135) | copy-start | bytes 1179652
  218.2 200.5 %reduce-scatter.8.cloned.1.call-start = ((), (), s32[]{:S(2)}) async-start(), calls=%async_computation.7 | async-start | bytes 5898240 | tf_op jit(solution)/shard_map/reduce_scatter | solution.py:1105
  218.3 42.4 %copy-start.59 = (bf16[256,256]{1,0:T(8,128)(2,1)}, bf16[256,256]{1,0:T(8,128)(2,1)S(1)}, u32[]{:S(2)}) copy-start(bf16[256,256]{1,0:T(8,128)(2,1)S(1)} %fusion.16.spread) | copy-start | bytes 393220
  218.3 42.3 %copy-start.51 = (bf16[4,512,512]{2,1,0:T(8,128)(2,1)S(1)}, bf16[4,512,512]{2,1,0:T(8,128)(2,1)}, u32[]{:S(2)}) copy-start(bf16[4,512,512]{2,1,0:T(8,128)(2,1)} %get-tuple-element.96.probs) | copy-start | bytes 6291460
  251.3 42.8 %collective-permute-start = (bf16[4,1152,128]{2,1,0:T(8,128)(2,1)S(1)}, bf16[4,1152,128]{2,1,0:T(8,128)(2,1)S(1)}, u32[]{:S(2)}, u32[]{:S(2)}) collective-permute-start(bf16[4,1152,128]{2,1,0:T(8,128)(2,1)S(1)} %shard_map.222), channel_id=1, source_target_pairs={{0,4},{4,0},{1,5},{5,1},{2,6},{6,2},{3,7},{7,3},{8,12},{12,8},{9,1... | collective-permute-start | bytes 3538952 | tf_op jit(solution)/shard_map/ppermute | solution.py:1092
  260.7 18.9 %copy-start.79 = (f32[128,768]{1,0:T(8,128)S(1)}, f32[128,768]{1,0:T(8,128)}, u32[]{:S(2)}) copy-start(f32[128,768]{1,0:T(8,128)} %copy-done.77) | copy-start | bytes 1179652
  260.7 33.4 %copy-start.53 = (bf16[2,640,768]{2,1,0:T(8,128)(2,1)S(1)}, bf16[2,640,768]{2,1,0:T(8,128)(2,1)}, u32[]{:S(2)}) copy-start(bf16[2,640,768]{2,1,0:T(8,128)(2,1)} %get-tuple-element.100.arrived) | copy-start | bytes 5898244
  260.8 33.4 %copy-start.63 = (f32[2,640,1]{2,1,0:T(8,128)S(1)}, f32[2,640,1]{2,1,0:T(8,128)}, u32[]{:S(2)}) copy-start(f32[2,640,1]{2,1,0:T(8,128)} %get-tuple-element.102.scale) | copy-start | bytes 15364
  270.9 23.3 %copy-start.49 = (bf16[2,640,1024]{2,1,0:T(8,128)(2,1)S(1)}, bf16[2,640,1024]{2,1,0:T(8,128)(2,1)}, u32[]{:S(2)}) copy-start(bf16[2,640,1024]{2,1,0:T(8,128)(2,1)} %get-tuple-element.101.inner) | copy-start | bytes 7864324
  310.9 165.5 %reduce-scatter.6.cloned.1.call-start = ((), (), s32[]{:S(2)}) async-start(), calls=%async_computation.6 | async-start | bytes 4915200 | tf_op jit(solution)/shard_map/reduce_scatter | solution.py:1105
  313.7 46.7 %collective-permute-start.1 = (bf16[4,768,128]{2,1,0:T(8,128)(2,1)}, bf16[4,768,128]{2,1,0:T(8,128)(2,1)S(1)}, u32[]{:S(2)}, u32[]{:S(2)}) collective-permute-start(bf16[4,768,128]{2,1,0:T(8,128)(2,1)} %shard_map.228), channel_id=1, source_target_pairs={{0,4},{4,0},{1,5},{5,1},{2,6},{6,2},{3,7},{7,3},{8,12},{12,8},{9,1... | collective-permute-start | bytes 2359304 | tf_op jit(solution)/shard_map/ppermute | solution.py:1092
  350.0 30.9 %collective-permute-start.2 = (bf16[4,1152,128]{2,1,0:T(8,128)(2,1)S(1)}, bf16[4,1152,128]{2,1,0:T(8,128)(2,1)S(1)}, u32[]{:S(2)}, u32[]{:S(2)}) collective-permute-start(bf16[4,1152,128]{2,1,0:T(8,128)(2,1)S(1)} %shard_map.231), channel_id=1, source_target_pairs={{0,4},{4,0},{1,5},{5,1},{2,6},{6,2},{3,7},{7,3},{8,12},{12,8},{9,1... | collective-permute-start | bytes 3538952 | tf_op jit(solution)/shard_map/ppermute | solution.py:1092
  378.7 19.6 %collective-permute-start.3 = (bf16[4,768,128]{2,1,0:T(8,128)(2,1)S(1)}, bf16[4,768,128]{2,1,0:T(8,128)(2,1)}, u32[]{:S(2)}, u32[]{:S(2)}) collective-permute-start(bf16[4,768,128]{2,1,0:T(8,128)(2,1)S(1)} %shard_map.235), channel_id=1, source_target_pairs={{0,4},{4,0},{1,5},{5,1},{2,6},{6,2},{3,7},{7,3},{8,12},{12,8},{9,1... | collective-permute-start | bytes 2359304 | tf_op jit(solution)/shard_map/ppermute | solution.py:1092
  419.9 46.8 %copy-start.38 = (bf16[1,2,3,192,512]{4,3,2,1,0:T(8,128)(2,1)S(1)}, bf16[1,2,3,192,512]{4,3,2,1,0:T(8,128)(2,1)}, u32[]{:S(2)}) copy-start(bf16[1,2,3,192,512]{4,3,2,1,0:T(8,128)(2,1)} %reduce-scatter.8.cloned.1.call-done) | copy-start | bytes 3538948
  419.9 46.9 %copy-start.86 = (bf16[1,2,3,192,512]{4,3,2,1,0:T(8,128)(2,1)S(1)}, bf16[1,2,3,192,512]{4,3,2,1,0:T(8,128)(2,1)}, u32[]{:S(2)}) copy-start(bf16[1,2,3,192,512]{4,3,2,1,0:T(8,128)(2,1)} %reduce-scatter.4.cloned.1.call-done) | copy-start | bytes 3538948
  479.9 36.2 %collective-permute-start.4 = (bf16[2,1344,128]{2,1,0:T(8,128)(2,1)S(1)}, bf16[2,1344,128]{2,1,0:T(8,128)(2,1)S(1)}, u32[]{:S(2)}, u32[]{:S(2)}) collective-permute-start(bf16[2,1344,128]{2,1,0:T(8,128)(2,1)S(1)} %pad_maximum_fusion.1), channel_id=1, source_target_pairs={{0,0},{1,8},{2,16},{3,24},{8,1},{9,9},{10,17},{11,25},{16,2},{17,1... | collective-permute-start | bytes 2064392 | tf_op jit(solution)/shard_map/ppermute | solution.py:1174
  (85 other events, 459.4 us)
Sparse Core Ops, SparseCore 0:
  218.3 85.9 reduce-scatter.3
  311.0 85.9 reduce-scatter.7
  401.9 74.5 reduce-scatter.5
